TPU v7x, 32 devices: a whole 2x2x4 slice. The times are simulated.
32 devices in a mesh: half: 2 (over x), seq: 4 (over z), head: 4 (over y, core).
Axes of the slice: x: 2, y: 2, z: 4, core: 2. Of those that a mesh axis runs over, the one named last changes fastest.
Arguments:
- enc_states: bfloat16 [8192, 4096], P(('half', 'seq')), may hold values from -64 to 64
- norm_gain: float32 [4096], replicated, may hold values from 0.25 to 4
- kv_weight: bfloat16 [4096, 1024], P(None, 'head'), may hold values from -1 to 1
- queries: bfloat16 [1024, 4096], P(('half', 'seq'), 'head'), may hold values from -512 to 512
- cotangent: bfloat16 [1024, 4096], P(('half', 'seq'), 'head'), may hold values from -8 to 8
Outputs:
- context: bfloat16 [1024, 4096], P(('half', 'seq'), 'head')
- d_queries: bfloat16 [1024, 4096], P(('half', 'seq'), 'head')
- d_keys_values: bfloat16 [8192, 1024], P(('half', 'seq'), 'head')
All inputs are finite; a program needn't handle non-finite values.
Results may differ from a plain program's by a relative error of at most 0.013.
The roundings to bfloat16 on the way count: a program that leaves them out, or rounds other values in their place, can miss the bound.
Values may be sent and summed in bfloat16 or wider, within the bound.
No kernel may reach another device: no remote copies, remote signals or barrier semaphores. Data moves between devices by JAX's collectives and lax.ppermute only.
A program may use at most 128 MiB of HBM per device.

v0:
```python
import jax
import jax.numpy as jnp
from jax import lax
from jax.sharding import PartitionSpec as P

HD = 64


eps = 1e-06
block_rows = 1024


def block_of():
    return block_rows


def split_blocks(tensor):
    block_size = block_of()
    return tensor.reshape((tensor.shape[0] // block_size, block_size) + tensor.shape[1:])


def join_blocks(tensor):
    return tensor.reshape((tensor.shape[0] * tensor.shape[1],) + tensor.shape[2:])


def to_rows(matrix, groups, head_size):
    tokens = matrix.shape[0]
    per_group = matrix.shape[1] // (groups * head_size)
    shaped = matrix.reshape(tokens, groups, per_group, head_size).transpose(0, 2, 1, 3)
    return shaped.reshape(tokens * per_group, groups, head_size)


def from_rows(row_tensor, tokens):
    length, groups, head_size = row_tensor.shape
    per_group = length // tokens
    shaped = row_tensor.reshape(tokens, per_group, groups, head_size).transpose(0, 2, 1, 3)
    return shaped.reshape(tokens, groups * per_group * head_size)


def block_scores(query_block, pair_block, head_size):
    length = pair_block.shape[0]
    pieces = pair_block.reshape(length, -1, 2, head_size)
    key_rows = pieces[:, :, 0, :]
    values = pieces[:, :, 1, :]
    scores = jnp.einsum("rgd,bgd->rgb", query_block, key_rows, preferred_element_type=jnp.float32)
    return (scores * head_size ** (-0.5), key_rows, values)


def row_maxima(query_rows, pair_rows, head_size):

    def row_by_rows(query_block):

        def row_advance(largest, pair_block):
            scores = block_scores(query_block, pair_block, head_size)[0]
            return (jnp.maximum(largest, jnp.max(scores, axis=2)), None)

        initial = jnp.full(query_block.shape[:2], -jnp.inf, jnp.float32)
        return lax.scan(row_advance, initial, split_blocks(pair_rows))[0]

    return join_blocks(lax.map(row_by_rows, split_blocks(query_rows)))


def weighted_sums(query_rows, pair_rows, row_max, head_size):

    def weighted_by_rows(blocks):
        query_block, max_block = blocks

        def weighted_advance(running, pair_block):
            totals, accumulated = running
            scores, key_rows, values = block_scores(query_block, pair_block, head_size)
            exponent = jnp.exp(scores - max_block[:, :, None])
            accumulated = accumulated + jnp.einsum(
                "rgb,bgd->rgd",
                exponent.astype(jnp.bfloat16),
                values,
                preferred_element_type=jnp.float32,
            )
            return ((totals + jnp.sum(exponent, axis=2), accumulated), None)

        initial = (
            jnp.zeros(max_block.shape, jnp.float32),
            jnp.zeros(query_block.shape, jnp.float32),
        )
        return lax.scan(weighted_advance, initial, split_blocks(pair_rows))[0]

    totals, accumulated = lax.map(
        weighted_by_rows, (split_blocks(query_rows), split_blocks(row_max))
    )
    return (join_blocks(totals), join_blocks(accumulated))


def gradients(query_rows, grad_rows, pair_rows, row_max, totals, deltas, head_size):
    pair_blocks = split_blocks(pair_rows)

    def gradients_by_rows(pair_sum, blocks):
        query_block, grad_block, max_block, total_block, delta_block = blocks

        def gradients_advance(query_sum, pair_block):
            scores, key_rows, values = block_scores(query_block, pair_block, head_size)
            probability = jnp.exp(scores - max_block[:, :, None]) / total_block[:, :, None]
            prob_grad = jnp.einsum(
                "rgd,bgd->rgb", grad_block, values, preferred_element_type=jnp.float32
            )
            score_grad = (
                head_size ** (-0.5) * probability * (prob_grad - delta_block[:, :, None])
            ).astype(jnp.bfloat16)
            query_sum = query_sum + jnp.einsum(
                "rgb,bgd->rgd", score_grad, key_rows, preferred_element_type=jnp.float32
            )
            key_grad = jnp.einsum(
                "rgb,rgd->bgd", score_grad, query_block, preferred_element_type=jnp.float32
            )
            value_grad = jnp.einsum(
                "rgb,rgd->bgd",
                probability.astype(jnp.bfloat16),
                grad_block,
                preferred_element_type=jnp.float32,
            )
            return (
                query_sum,
                jnp.stack([key_grad, value_grad], axis=2).reshape(pair_block.shape[0], -1),
            )

        query_grad, pair_parts = lax.scan(
            gradients_advance, jnp.zeros(query_block.shape, jnp.float32), pair_blocks
        )
        return (pair_sum + pair_parts, query_grad)

    initial = jnp.zeros(pair_blocks.shape, jnp.float32)
    blocks = (
        split_blocks(query_rows),
        split_blocks(grad_rows),
        split_blocks(row_max),
        split_blocks(totals),
        split_blocks(deltas),
    )
    pair_grad, query_grad = lax.scan(gradients_by_rows, initial, blocks)
    return (join_blocks(query_grad), join_blocks(pair_grad))


def on_device(enc_states, norm_gain, kv_weight, queries, cotangent):
    groups = kv_weight.shape[1] // (2 * HD)
    states = enc_states.astype(jnp.float32)
    inverse_root = lax.rsqrt(jnp.mean(states * states, axis=1, keepdims=True) + eps)
    normed = (states * inverse_root * norm_gain).astype(jnp.bfloat16)
    own_pairs = jnp.dot(normed, kv_weight, preferred_element_type=jnp.float32).astype(jnp.bfloat16)
    tokens = queries.shape[0]
    query_rows = to_rows(queries, groups, HD)
    grad_rows = to_rows(cotangent, groups, HD)
    fragment = lax.all_gather(own_pairs, ("half", "seq"), axis=0, tiled=True)
    row_max = row_maxima(query_rows, fragment, HD)
    totals, accumulated = weighted_sums(query_rows, fragment, row_max, HD)
    context_rows = (accumulated / totals[:, :, None]).astype(jnp.bfloat16)
    deltas = jnp.sum(grad_rows.astype(jnp.float32) * context_rows.astype(jnp.float32), axis=2)
    query_grad, pair_grad = gradients(query_rows, grad_rows, fragment, row_max, totals, deltas, HD)
    pair_share = lax.psum_scatter(pair_grad, ("half", "seq"), scatter_dimension=0, tiled=True)
    context = from_rows(context_rows, tokens)
    d_queries = from_rows(query_grad.astype(jnp.bfloat16), tokens)
    return (context, d_queries, pair_share.astype(jnp.bfloat16))


def solution(mesh):
    placed = (
        P(("half", "seq"), None),
        P(),
        P(None, "head"),
        P(("half", "seq"), "head"),
        P(("half", "seq"), "head"),
    )
    return jax.shard_map(
        on_device,
        mesh=mesh,
        in_specs=placed,
        out_specs=(
            P(("half", "seq"), "head"),
            P(("half", "seq"), "head"),
            P(("half", "seq"), "head"),
        ),
        check_vma=False,
    )
```

profile of v0, /device:TPU:0, one launch (start us, length us, event | category | flops | bytes accessed | tf_op | source)
XLA Modules:
  0.0 438.9 jit_solution(8884652493314864029)
XLA Ops:
  7.2 5.2 %fusion.23 = f32[1024]{0:T(1024)S(1)} fusion(bf16[1024,4096]{1,0:T(8,128)(2,1)} %param.11), kind=kLoop, calls=%fused_computation.36 | loop fusion | flops 12581888 | bytes 8392704 | tf_op jit(solution)/shard_map/reduce_sum | solution.py:144
  13.6 4.0 fusion.30
  22.6 70.7 %all-gather.2.cloned.1.call-done = bf16[8192,256]{1,0:T(8,128)(2,1)} async-done(((bf16[1024,256]{1,0:T(8,128)(2,1)}), bf16[8192,256]{1,0:T(8,128)(2,1)}) %all-gather.2.cloned.1.call-update) | async-done | bytes 4194320 | tf_op jit(solution)/shard_map/all_gather | solution.py:150
  93.3 6.5 %copy.31 = bf16[8,1024,256]{1,2,0:T(8,128)(2,1)} copy(bf16[8,1024,256]{2,1,0:T(8,128)(2,1)} %bitcast.177) | data formatting | bytes 8388608
  99.8 19.5 %while.62 = (s32[]{:T(128)}, f32[1024,2]{0,1:T(2,128)S(1)}, bf16[8,1024,256]{1,2,0:T(8,128)(2,1)}, bf16[1024,2,64]{0,2,1:T(8,128)(2,1)S(1)}, s32[]{:T(128)}, /*index=5*/s32[]{:T(128)}) while((s32[]{:T(128)}, f32[1024,2]{0,1:T(2,128)S(1)}, bf16[8,1024,256]{1,2,0:T(8,128)(2,1)}, bf16[1024,2,64]{0,2,1:T(8,128)(2,1)S(1)}, s32[]{:T(128)}, ...), condition=%wide.region_3.0_spmd.clone, body=%wide.region_1.3_spmd.clone.sunk | while | flops 272631808 | bytes 1605723 | solution.py:58
  119.3 36.3 %while.63 = (s32[]{:T(128)}, f32[1024,2]{0,1:T(2,128)S(1)}, f32[1024,2,64]{0,2,1:T(8,128)S(1)}, bf16[8,1024,256]{1,2,0:T(8,128)(2,1)}, bf16[1024,2,64]{0,2,1:T(8...) while((s32[]{:T(128)}, f32[1024,2]{0,1:T(2,128)S(1)}, ...), condition=%wide.region_6.7_spmd.clone, body=%wide.region_4.0_spmd.clone.sunk | while | flops 549718016 | bytes 19710060 | solution.py:84
  157.1 2.6 multiply_reduce_fusion.1
  159.8 124.0 %while.64 = (s32[]{:T(128)}, f32[1024,2,64]{0,2,1:T(8,128)}, f32[8,1024,256]{2,1,0:T(8,128)}, bf16[8,1024,256]{1,2,0:T(8,128)(2,1)}, bf16[1024,2,64]{0,2,1:T(8,1...) while((s32[]{:T(128)}, f32[1024,2,64]{0,2,1:T(8,128)}, ...), condition=%wide.region_9.10_spmd.clone, body=%wide.region_8.9_spmd.clone.sunk | while | flops 1359478784 | bytes 51142788 | solution.py:124
  162.8 2.3 fusion.75
  177.4 2.3 fusion.75
  182.0 2.7 fusion.74
  193.0 2.3 fusion.75
  197.6 2.7 fusion.74
  208.6 2.3 fusion.75
  213.3 2.7 fusion.74
  224.2 2.3 fusion.75
  228.9 2.7 fusion.74
  239.8 2.3 fusion.75
  244.5 2.7 fusion.74
  255.5 2.3 fusion.75
  260.1 2.7 fusion.74
  271.1 2.3 fusion.75
  275.7 2.7 fusion.74
  288.5 141.5 %reduce-scatter.2.cloned.1.call-done = f32[1024,256]{1,0:T(8,128)} async-done(((f32[8192,256]{1,0:T(8,128)}), f32[1024,256]{1,0:T(8,128)}) %reduce-scatter.2.cloned.1.call-update) | async-done | bytes 1048592 | tf_op jit(solution)/shard_map/reduce_scatter | solution.py:156
  (155 shorter events, 155.8 us)
Async XLA Ops:
  7.2 5.3 %copy-start = (bf16[4096,256]{1,0:T(8,128)(2,1)S(1)}, bf16[4096,256]{1,0:T(8,128)(2,1)}, u32[]{:S(2)}) copy-start(bf16[4096,256]{1,0:T(8,128)(2,1)} %param.13) | copy-start | bytes 6291460
  7.2 86.1 %all-gather.2.cloned.1.call-start = ((), (), s32[]{:S(2)}) async-start(), calls=%async_computation.1 | async-start | bytes 4718592 | tf_op jit(solution)/shard_map/all_gather | solution.py:150
  7.2 6.4 %copy-start.1 = (bf16[1024,4096]{1,0:T(8,128)(2,1)S(1)}, bf16[1024,4096]{1,0:T(8,128)(2,1)}, u32[]{:S(2)}) copy-start(bf16[1024,4096]{1,0:T(8,128)(2,1)} %param.11) | copy-start | bytes 25165828
  13.6 4.3 copy-start.3
  17.6 412.3 %reduce-scatter.2.cloned.1.call-start = ((), (), s32[]{:S(2)}) async-start(), calls=%async_computation.2 | async-start | bytes 9437184 | tf_op jit(solution)/shard_map/reduce_scatter | solution.py:156
  283.7 1.0 copy-start.2
Sparse Core Ops, SparseCore 0:
  17.8 75.4 all-gather.1
  283.9 146.0 reduce-scatter.1
where the time goes:
time: 442 us; the launch traced here: 439 us
  waiting for transfers between devices  212 us (48%)
  matrix products  126 us (29%)
  local copies, waits for them, and re-layouts  73.6 us (17%)
  between operations  14.2 us (3%)
  other arithmetic  12 us (3%)
    reduce_scatter x1, waiting for transfers between devices, on_device(): lax.psum_scatter(pair_grad, ('half', 'seq'), scatter_dimension=0, tiled=T...  141 us
    all_gather x1, waiting for transfers between devices, on_device(): fragment = lax.all_gather(own_pairs, ('half', 'seq'), axis=0, tiled=True)  70.7 us
    dot_general x24, matrix products, block_scores(): jnp.einsum('rgd,bgd->rgb', query_block, key_rows, preferred_element_type=...  40 us
    dynamic_slice x24, local copies, waits for them, and re-layouts, row_by_rows(): return lax.scan(row_advance, initial, split_blocks(pair_rows))[0]  25.9 us
    dynamic_update_slice x16, local copies, waits for them, and re-layouts, gradients_by_rows(): lax.scan(gradients_advance, jnp.zeros(query_block.shape, jnp.float32), pa...  21 us
    dot_general x8, matrix products, gradients_advance(): jnp.einsum('rgb,bgd->rgd', score_grad, key_rows, preferred_element_type=j...  20.5 us
    dot_general x8, matrix products, gradients_advance(): jnp.einsum('rgb,rgd->bgd', probability.astype(jnp.bfloat16), grad_block,...  18.8 us
    dot_general x8, matrix products, gradients_advance(): jnp.einsum('rgd,bgd->rgb', grad_block, values, preferred_element_type=jnp...  18.3 us
  transfers between devices with their start and end apart: 2, of which 2 were waited for; matrix products, arithmetic and copies ran while one was open for 2% of the time, Pallas kernels for 0%

commit v1 on v0

v1 whole, which is shorter than its diff:
```python
import functools
import math

import jax
import jax.numpy as jnp
from jax import lax
from jax.experimental import pallas as pl
from jax.experimental.pallas import tpu as pltpu
from jax.sharding import PartitionSpec as P

HD = 64
EPS = 1e-06
LOG2E = math.log2(math.e)
SCALE = HD ** (-0.5)
KEY_ROWS = 256
VMEM_BYTES = 60 << 20
NT = (((1,), (1,)), ((), ()))

bf16 = jnp.bfloat16
f32 = jnp.float32

IN_VMEM = pl.BlockSpec(memory_space=pltpu.VMEM)
IN_PLACE = pl.BlockSpec(memory_space=pl.ANY)


def project_kernel(x_ref, gain_ref, w_ref, out_ref):
    x = x_ref[...].astype(f32)
    inverse_root = lax.rsqrt(jnp.mean(x * x, axis=1, keepdims=True) + EPS)
    normed = (x * inverse_root * gain_ref[...]).astype(bf16)
    pairs = jnp.dot(normed, w_ref[...], preferred_element_type=f32).astype(bf16)
    for g in range(out_ref.shape[0]):
        out_ref[g] = pairs[:, g * 2 * HD : (g + 1) * 2 * HD]


def project(states, gain, weight):
    rows, width = states.shape
    groups = weight.shape[1] // (2 * HD)
    block = min(rows, 256)
    return pl.pallas_call(
        project_kernel,
        grid=(rows // block,),
        in_specs=[
            pl.BlockSpec((block, width), lambda i: (i, 0)),
            pl.BlockSpec((1, width), lambda i: (0, 0)),
            pl.BlockSpec((width, weight.shape[1]), lambda i: (0, 0)),
        ],
        out_specs=pl.BlockSpec((groups, block, 2 * HD), lambda i: (0, i, 0)),
        out_shape=jax.ShapeDtypeStruct((groups, rows, 2 * HD), bf16),
        compiler_params=pltpu.CompilerParams(vmem_limit_bytes=VMEM_BYTES),
        cost_estimate=pl.CostEstimate(
            flops=2 * rows * width * weight.shape[1], bytes_accessed=2 * rows * width, transcendentals=0
        ),
        name="project",
    )(states, gain.reshape(1, width), weight)


def turn_kernel(count, *refs):
    inputs, out_ref = refs[:count], refs[count]
    chunks, _, lanes = out_ref.shape
    per_block = chunks // count
    tokens = inputs[0].shape[0]
    heads = lanes // tokens
    for s in range(count):
        turned = inputs[s][...].T
        for i in range(per_block):
            base = i * heads * HD
            out_ref[s * per_block + i] = jnp.concatenate(
                [turned[base + h * HD : base + (h + 1) * HD] for h in range(heads)], axis=1
            )


def turn(blocks, heads):
    tokens, width = blocks[0].shape
    chunks = len(blocks) * width // (heads * HD)
    return pl.pallas_call(
        functools.partial(turn_kernel, len(blocks)),
        in_specs=[IN_VMEM] * len(blocks),
        out_specs=IN_VMEM,
        out_shape=jax.ShapeDtypeStruct((chunks, HD, heads * tokens), bf16),
        compiler_params=pltpu.CompilerParams(vmem_limit_bytes=VMEM_BYTES),
        name="turn",
    )(*blocks)


def forward_kernel(dims, first, last, *refs):
    chunks, groups, per_group = dims
    refs = list(refs)
    q_ref = refs.pop(0)
    c_ref = refs.pop(0) if last else None
    kv_ref = refs.pop(0)
    past, past_acc = (None, None) if first else (refs.pop(0), refs.pop(0))
    e_hbm, top_ref, st_ref, acc_ref, value_t, scores, expo, sem = refs
    length = kv_ref.shape[1]
    lanes = q_ref.shape[2]
    pad = jnp.zeros((HD, lanes), bf16)
    steps = length // KEY_ROWS
    for g in range(groups):
        value_t[g, :HD] = kv_ref[g].T[HD:]
        value_t[g, HD:] = jnp.ones((16, length), bf16)

    def group_of(c):
        return (c // per_group) % groups

    def store(slot, c):
        return pltpu.make_async_copy(expo.at[slot], e_hbm.at[c], sem.at[slot])

    def emit(ca, cb, cc, slot, top, wait):
        largest, total = None, None
        if ca is not None:
            weights = jnp.concatenate([q_ref[ca] * jnp.asarray(SCALE, bf16), pad], axis=0)
            ga = group_of(ca)
        if cb is not None:
            low_top = top * LOG2E
            if wait:
                store(slot, cb).wait()
        if cc is not None:
            gc = group_of(cc)
        for k in range(steps):
            ks = slice(k * KEY_ROWS, (k + 1) * KEY_ROWS)
            if cb is not None:
                expo[slot, ks] = jnp.exp2(scores[ks] * LOG2E - low_top).astype(bf16)
            if ca is not None:
                s = jnp.dot(kv_ref[ga, ks], weights, preferred_element_type=f32)
                scores[ks] = s
                part = jnp.max(s.reshape(KEY_ROWS // 8, 8, lanes), axis=0)
                largest = part if largest is None else jnp.maximum(largest, part)
            if cc is not None:
                part = jnp.dot(value_t[gc, :, ks], expo[1 - slot, ks], preferred_element_type=f32)
                total = part if total is None else total + part
        if cb is not None:
            top_ref[pl.ds(cb, 1)] = top
            store(slot, cb).start()
        if cc is not None:
            m = top_ref[pl.ds(cc, 1)]
            l = total[HD : HD + 1]
            acc = total[:HD]
            if not first:
                before = past[0, pl.ds(cc, 1)]
                both = jnp.maximum(before, m)
                old, new = jnp.exp(before - both), jnp.exp(m - both)
                l = past[1, pl.ds(cc, 1)] * old + l * new
                acc = past_acc[cc] * old + acc * new
                m = both
            st_ref[0, pl.ds(cc, 1)] = m
            st_ref[1, pl.ds(cc, 1)] = l
            if last:
                st_ref[2, pl.ds(cc, 1)] = jnp.sum(c_ref[cc].astype(f32) * acc, axis=0, keepdims=True)
            acc_ref[cc] = acc
        return None if largest is None else jnp.max(largest, axis=0, keepdims=True)

    n = chunks
    top = emit(0, None, None, None, None, False)
    top = emit(1, 0, None, 0, top, False)

    def body(j, top, wait=True):
        top = emit(2 * j + 2, 2 * j + 1, 2 * j, 1, top, wait)
        return emit(2 * j + 3, 2 * j + 2, 2 * j + 1, 0, top, True)

    top = body(0, top, wait=False)
    top = lax.fori_loop(1, n // 2 - 1, body, top)
    emit(None, n - 1, n - 2, 1, top, True)
    emit(None, None, n - 1, 0, None, False)
    store(0, n - 2).wait()
    store(1, n - 1).wait()


def forward(dims, q_rows, c_rows, pairs, before):
    chunks, groups, per_group = dims
    lanes = q_rows.shape[2]
    length = pairs.shape[1]
    first, last = before is None, c_rows is not None
    args = [q_rows] + ([c_rows] if last else []) + [pairs] + ([] if first else list(before))
    size = chunks * lanes * length
    return pl.pallas_call(
        functools.partial(forward_kernel, dims, first, last),
        in_specs=[IN_VMEM] * len(args),
        out_specs=[IN_PLACE, IN_VMEM, IN_VMEM, IN_VMEM],
        out_shape=[
            jax.ShapeDtypeStruct((chunks, length, lanes), bf16),
            jax.ShapeDtypeStruct((chunks, lanes), f32),
            jax.ShapeDtypeStruct((3 if last else 2, chunks, lanes), f32),
            jax.ShapeDtypeStruct((chunks, HD, lanes), f32),
        ],
        scratch_shapes=[
            pltpu.VMEM((groups, HD + 16, length), bf16),
            pltpu.VMEM((length, lanes), f32),
            pltpu.VMEM((2, length, lanes), bf16),
            pltpu.SemaphoreType.DMA((2,)),
        ],
        compiler_params=pltpu.CompilerParams(vmem_limit_bytes=VMEM_BYTES),
        cost_estimate=pl.CostEstimate(flops=16 * size * HD, bytes_accessed=2 * size, transcendentals=size),
        name="forward",
    )(*args)


def rolled(rows, shift):
    count = rows.shape[0]
    shift = shift % count
    return rows if shift == 0 else jnp.concatenate([rows[count - shift :], rows[: count - shift]], axis=0)


def backward_kernel(dims, peers, first, last, *refs):
    chunks, groups, per_group = dims
    refs = list(refs)
    q_ref, c_ref, kv_ref, e_hbm, top_ref, own_ref = [refs.pop(0) for _ in range(6)]
    peer_refs = [refs.pop(0) for _ in range(peers)]
    acc_ref = refs.pop(0) if first else None
    past_dq = None if first else refs.pop(0)
    blocks = peers + 1
    ctx_outs = [refs.pop(0) for _ in range(blocks)] if first else None
    dq_outs = [refs.pop(0) for _ in range(blocks)] if last else [refs.pop(0)]
    dkv_ref = refs.pop(0)
    key_t, expo, score_grad, key_sum, value_sum, factor, delta, rows, sem, row_sem = refs
    length = kv_ref.shape[1]
    lanes = q_ref.shape[2]
    steps = length // KEY_ROWS
    heads = per_block_heads = lanes // rows.shape[1]
    per_block = chunks // blocks
    pad = jnp.zeros((HD, lanes), bf16)

    def group_of(c):
        return (c // per_group) % groups

    def fetch(slot, c):
        return pltpu.make_async_copy(e_hbm.at[c], expo.at[slot], sem.at[slot])

    fetch(0, 0).start()
    fetch(1, 1).start()
    for g in range(groups):
        key_t[g] = kv_ref[g].T[:HD]
    key_sum[...] = jnp.zeros_like(key_sum)
    value_sum[...] = jnp.zeros_like(value_sum)

    stats = [[own_ref[i] for i in range(3)]]
    for r in range(1, blocks):
        stats.append([rolled(peer_refs[r - 1][i], r * per_block) for i in range(3)])
    top = functools.reduce(jnp.maximum, [s[0] for s in stats])
    shares = [jnp.exp(s[0] - top) for s in stats]
    total = sum(s[1] * w for s, w in zip(stats, shares))
    delta[...] = sum(s[2] * w for s, w in zip(stats, shares)) / total
    factor[0] = jnp.exp(top_ref[...] - top) / total
    if first:
        factor[1] = shares[0] / total

    def put_rows(c, value):
        flat = jnp.concatenate([value[:, h * rows.shape[1] : (h + 1) * rows.shape[1]] for h in range(heads)], axis=0)
        offset = pl.multiple_of((c % per_block) * heads * HD, heads * HD)
        rows[c // per_block, :, pl.ds(offset, heads * HD)] = flat.astype(bf16).T

    def send_rows(outs):
        copies = [pltpu.make_async_copy(rows.at[s], outs[s], row_sem.at[s]) for s in range(blocks)]
        for copy in copies:
            copy.start()
        for copy in copies:
            copy.wait()

    if first:

        def put_context(c, _):
            put_rows(c, acc_ref[c] * factor[1, pl.ds(c, 1)])
            return 0

        lax.fori_loop(0, chunks, put_context, 0)
        send_rows(ctx_outs)

    def emit(ca, cb, slot):
        if ca is not None:
            ga = group_of(ca)
            weights = jnp.concatenate([pad, c_ref[ca]], axis=0)
            fa, da = factor[0, pl.ds(ca, 1)], delta[pl.ds(ca, 1)]
            scaled_c = (c_ref[ca].astype(f32) * fa).astype(bf16)
            fetch(slot, ca).wait()
        if cb is not None:
            gb = group_of(cb)
            fb = factor[0, pl.ds(cb, 1)] * SCALE
            scaled_q = (q_ref[cb].astype(f32) * fb).astype(bf16)
            dq = None
        for k in range(steps):
            ks = slice(k * KEY_ROWS, (k + 1) * KEY_ROWS)
            if cb is not None:
                ds = score_grad[ks]
                part = jnp.dot(key_t[gb, :, ks], ds, preferred_element_type=f32)
                dq = part if dq is None else dq + part
                key_sum[gb, :, ks] += lax.dot_general(scaled_q, ds, NT, preferred_element_type=f32)
            if ca is not None:
                e = expo[slot, ks]
                prob_grad = jnp.dot(kv_ref[ga, ks], weights, preferred_element_type=f32)
                score_grad[ks] = (e.astype(f32) * (prob_grad - da)).astype(bf16)
                value_sum[ga, :, ks] += lax.dot_general(scaled_c, e, NT, preferred_element_type=f32)
        if cb is not None:
            dq = dq * fb
            if not first:
                dq = dq + past_dq[cb]
            if last:
                put_rows(cb, dq)
            else:
                dq_outs[0][cb] = dq

    n = chunks
    emit(0, None, 0)

    def body(j, _):
        @pl.when(2 * j + 2 < n)
        def _():
            fetch(0, 2 * j + 2).start()

        emit(2 * j + 1, 2 * j, 1)

        @pl.when(2 * j + 2 < n)
        def _():
            fetch(1, 2 * j + 3).start()
            emit(2 * j + 2, 2 * j + 1, 0)

        return 0

    lax.fori_loop(0, n // 2, body, 0)
    emit(None, n - 1, None)
    if last:
        send_rows(dq_outs)
    for g in range(groups):
        both = jnp.concatenate([key_sum[g], value_sum[g]], axis=0)
        dkv_ref[:, g * 2 * HD : (g + 1) * 2 * HD] = both.T.astype(dkv_ref.dtype)


def backward(dims, q_rows, c_rows, pairs, expo, top, own, peers, acc, past_dq, last, tokens):
    chunks, groups, per_group = dims
    lanes = q_rows.shape[2]
    length = pairs.shape[1]
    first = past_dq is None
    blocks = len(peers) + 1
    width = chunks // blocks * (lanes // tokens) * HD
    args = [q_rows, c_rows, pairs, expo, top, own, *peers] + [acc if first else past_dq]
    specs = [IN_VMEM] * 3 + [IN_PLACE] + [IN_VMEM] * (len(args) - 4)
    row_block = jax.ShapeDtypeStruct((tokens, width), bf16)
    outs, out_specs = [], []
    if first:
        outs += [row_block] * blocks
        out_specs += [IN_PLACE] * blocks
    if last:
        outs += [row_block] * blocks
        out_specs += [IN_PLACE] * blocks
    else:
        outs.append(jax.ShapeDtypeStruct((chunks, HD, lanes), f32))
        out_specs.append(IN_VMEM)
    outs.append(jax.ShapeDtypeStruct((length, groups * 2 * HD), f32 if last else bf16))
    out_specs.append(IN_VMEM)
    size = chunks * lanes * length
    results = list(
        pl.pallas_call(
            functools.partial(backward_kernel, dims, len(peers), first, last),
            in_specs=specs,
            out_specs=out_specs,
            out_shape=outs,
            scratch_shapes=[
                pltpu.VMEM((groups, HD, length), bf16),
                pltpu.VMEM((2, length, lanes), bf16),
                pltpu.VMEM((length, lanes), bf16),
                pltpu.VMEM((groups, HD, length), f32),
                pltpu.VMEM((groups, HD, length), f32),
                pltpu.VMEM((2, chunks, lanes), f32),
                pltpu.VMEM((chunks, lanes), f32),
                pltpu.VMEM((blocks, tokens, width), bf16),
                pltpu.SemaphoreType.DMA((2,)),
                pltpu.SemaphoreType.DMA((blocks,)),
            ],
            compiler_params=pltpu.CompilerParams(vmem_limit_bytes=VMEM_BYTES),
            cost_estimate=pl.CostEstimate(flops=24 * size * HD, bytes_accessed=2 * size, transcendentals=0),
            name="backward",
        )(*args)
    )
    context = [results.pop(0) for _ in range(blocks)] if first else None
    dq = [results.pop(0) for _ in range(blocks)] if last else results.pop(0)
    return context, dq, results.pop(0)


def on_device(halves, seqs, enc_states, norm_gain, kv_weight, queries, cotangent):
    tokens, width = queries.shape
    groups = kv_weight.shape[1] // (2 * HD)
    per_group_heads = width // (groups * HD)
    heads = min(per_group_heads, max(1, 512 // tokens))
    per_group = per_group_heads // heads
    chunks = seqs * groups * per_group
    dims = (chunks, groups, per_group)

    def from_seq(x, shift):
        return lax.ppermute(x, "seq", [(i, (i + shift) % seqs) for i in range(seqs)])

    def from_half(x, shift):
        return lax.ppermute(x, "half", [(i, (i + shift) % halves) for i in range(halves)])

    q_blocks = [queries] + [from_seq(queries, s) for s in range(1, seqs)]
    late, *_ = lax.optimization_barrier((cotangent, *q_blocks[1:]))
    c_blocks = [late] + [from_seq(late, s) for s in range(1, seqs)]
    own_pairs = project(enc_states, norm_gain, kv_weight)
    pair_blocks = [own_pairs] + [from_half(own_pairs, s) for s in range(1, halves)]
    q_rows = turn(q_blocks, heads)
    c_rows = turn(c_blocks, heads)

    expos, tops, before = [], [], None
    for i, pairs in enumerate(pair_blocks):
        expo, top, stats, acc = forward(dims, q_rows, c_rows if i == halves - 1 else None, pairs, before)
        expos.append(expo)
        tops.append(top)
        before = (stats, acc)
    peers = [from_seq(stats, r) for r in range(1, seqs)]

    dq, sends, context_parts = None, [], None
    for i in reversed(range(halves)):
        parts, dq, dkv = backward(
            dims, q_rows, c_rows, pair_blocks[i], expos[i], tops[i], stats, peers, acc, dq, i == 0, tokens
        )
        if parts is not None:
            context_parts = parts
        sends.append(dkv if i == 0 else from_half(dkv, -i))

    def home(parts):
        arrived = [parts[0]] + [from_seq(parts[s], -s) for s in range(1, seqs)]
        return sum(x.astype(f32) for x in arrived).astype(bf16)

    context = home(context_parts)
    d_queries = home(dq)
    d_pairs = sum(x.astype(f32) for x in sends).astype(bf16)
    return (context, d_queries, d_pairs)


def solution(mesh):
    shape = mesh.shape
    rows, columns = P(("half", "seq"), None), P(("half", "seq"), "head")
    return jax.shard_map(
        functools.partial(on_device, shape["half"], shape["seq"]),
        mesh=mesh,
        in_specs=(rows, P(), P(None, "head"), columns, columns),
        out_specs=(columns, columns, columns),
        check_vma=False,
    )
```

time: 442 us -> 174 us (0.39)
  waiting for transfers between devices: 212 us -> 36.8 us
  matrix products: 126 us -> 0 us
  Pallas kernels: 0 us -> 94.7 us
  local copies, waits for them, and re-layouts: 73.6 us -> 2.88 us
  starting transfers between devices: 0.26 us -> 34.4 us
  between operations: 14.2 us -> 0.74 us
  other arithmetic: 12 us -> 3.61 us
    reduce_scatter x1 -> x0, waiting for transfers between devices: 141 us -> none  [on_device(): lax.psum_scatter(pair_grad, ('half', 'seq'), scatter_dimension=0, tiled=T...]
    dot_general x65 -> x0, matrix products: 126 us -> none  [the longest x24 40 us: block_scores(): jnp.einsum('rgd,bgd->rgb', query_block, key_rows, preferred_element_type=...]
    pallas_call x0 -> x7, Pallas kernels: none -> 94.7 us  [the longest x2 49 us: backward(): pl.pallas_call(functools.partial(backward_kernel, dims, len(peers), first...]
    all_gather x1 -> x0, waiting for transfers between devices: 70.7 us -> none  [on_device(): fragment = lax.all_gather(own_pairs, ('half', 'seq'), axis=0, tiled=True)]
    ppermute x0 -> x17, waiting for transfers between devices: none -> 36.8 us  [the longest x15 36.7 us: from_seq(): lax.ppermute(x, 'seq', [(i, (i + shift) % seqs) for i in range(seqs)])]
    ppermute x0 -> x17, starting transfers between devices: none -> 34.4 us  [the longest x15 31.5 us: from_seq(): lax.ppermute(x, 'seq', [(i, (i + shift) % seqs) for i in range(seqs)])]
    dynamic_slice x24 -> x0, local copies, waits for them, and re-layouts: 25.9 us -> none  [row_by_rows(): return lax.scan(row_advance, initial, split_blocks(pair_rows))[0]]
    dynamic_update_slice x16 -> x0, local copies, waits for them, and re-layouts: 21 us -> none  [gradients_by_rows(): lax.scan(gradients_advance, jnp.zeros(query_block.shape, jnp.float32), pa...]
  transfers between devices with their start and end apart: 2 -> 17, of which waited for: 2 -> 7; matrix products, arithmetic and copies ran while one was open for 2% -> 2% of each run, Pallas kernels for 0% -> 31%
where the time goes in v1:
time: 174 us; the launch traced here: 173 us
  Pallas kernels  94.7 us (54%)
  waiting for transfers between devices  36.8 us (21%)
  starting transfers between devices  34.4 us (20%)
  other arithmetic  3.61 us (2%)
  local copies, waits for them, and re-layouts  2.88 us (2%)
    pallas_call x2, Pallas kernels, backward(): pl.pallas_call(functools.partial(backward_kernel, dims, len(peers), first...  49 us
    ppermute x15, waiting for transfers between devices, from_seq(): lax.ppermute(x, 'seq', [(i, (i + shift) % seqs) for i in range(seqs)])  36.7 us
    pallas_call x2, Pallas kernels, forward(): pl.pallas_call(functools.partial(forward_kernel, dims, first, last), in_s...  32.4 us
    ppermute x15, starting transfers between devices, from_seq(): lax.ppermute(x, 'seq', [(i, (i + shift) % seqs) for i in range(seqs)])  31.5 us
    pallas_call x1, Pallas kernels, project(): pl.pallas_call(project_kernel, grid=(rows // block,), in_specs=[pl.BlockS...  8.29 us
    pallas_call x2, Pallas kernels, turn(): pl.pallas_call(functools.partial(turn_kernel, len(blocks)), in_specs=[IN_...  5 us
  transfers between devices with their start and end apart: 17, of which 7 were waited for; matrix products, arithmetic and copies ran while one was open for 2% of the time, Pallas kernels for 31%

profile of v1, /device:TPU:0, one launch (start us, length us, event | category | flops | bytes accessed | tf_op | source)
XLA Modules:
  0.0 173.1 jit_solution(4129196315881561686)
XLA Ops:
  0.6 4.1 %collective-permute-start.1 = (bf16[128,1024]{1,0:T(8,128)(2,1)}, bf16[128,1024]{1,0:T(8,128)(2,1)S(1)}, u32[]{:S(2)}, u32[]{:S(2)}) collective-permute-start(bf16[128,1024]{1,0:T(8,128)(2,1)} %refs_0_.1), channel_id=1, source_target_pairs={{0,8},{4,12},{8,0},{12,4},{1,9},{5,13},{9,1},{13,5},{2,10},{6,14},... | collective-permute-start | bytes 786440 | tf_op jit(solution)/shard_map/ppermute | solution.py:386
  4.8 1.6 collective-permute-start
  6.3 2.2 %collective-permute-start.2 = (bf16[128,1024]{1,0:T(8,128)(2,1)}, bf16[128,1024]{1,0:T(8,128)(2,1)S(1)}, u32[]{:S(2)}, u32[]{:S(2)}) collective-permute-start(bf16[128,1024]{1,0:T(8,128)(2,1)} %refs_0_.1), channel_id=1, source_target_pairs={{0,12},{4,0},{8,4},{12,8},{1,13},{5,1},{9,5},{13,9},{2,14},{6,2},{... | collective-permute-start | bytes 786440 | tf_op jit(solution)/shard_map/ppermute | solution.py:386
  8.6 8.3 %project.1.refs_1_.refs_2_ = bf16[2,1024,128]{2,1,0:T(8,128)(2,1)} custom-call(bf16[1024,4096]{1,0:T(8,128)(2,1)} %x_ref.1, f32[1,4096]{1,0:T(1,128)} %bitcast.1, bf16[4096,256]{1,0:T(8,128)(2,1)} %w_ref.1), custom_call_target="tpu_custom_call" | custom-call | flops 2147483648 | bytes 8388608 | tf_op jit(solution)/shard_map/project/pallas_call | solution.py:39
  18.4 5.0 %collective-permute-done.1.refs_2_ = bf16[128,1024]{1,0:T(8,128)(2,1)S(1)} collective-permute-done((bf16[128,1024]{1,0:T(8,128)(2,1)}, bf16[128,1024]{1,0:T(8,128)(2,1)S(1)}, u32[]{:S(2)}, u32[]{:S(2)}) %collective-permute-start.1) | collective-permute-done | bytes 262176 | tf_op jit(solution)/shard_map/ppermute | solution.py:386
  24.1 2.1 %collective-permute-start.5 = (bf16[128,1024]{1,0:T(8,128)(2,1)S(1)}, bf16[128,1024]{1,0:T(8,128)(2,1)S(1)}, u32[]{:S(2)}, u32[]{:S(2)}) collective-permute-start(bf16[128,1024]{1,0:T(8,128)(2,1)S(1)} %copy-done.2), channel_id=1, source_target_pairs={{0,12},{4,0},{8,4},{12,8},{1,13},{5,1},{9,5},{13,9},{2,14},{6,2},{... | collective-permute-start | bytes 786440 | tf_op jit(solution)/shard_map/ppermute | solution.py:386
  26.2 10.3 %collective-permute-start.4 = (bf16[128,1024]{1,0:T(8,128)(2,1)S(1)}, bf16[128,1024]{1,0:T(8,128)(2,1)S(1)}, u32[]{:S(2)}, u32[]{:S(2)}) collective-permute-start(bf16[128,1024]{1,0:T(8,128)(2,1)S(1)} %copy-done.2), channel_id=1, source_target_pairs={{0,8},{4,12},{8,0},{12,4},{1,9},{5,13},{9,1},{13,5},{2,10},{6,14},... | collective-permute-start | bytes 786440 | tf_op jit(solution)/shard_map/ppermute | solution.py:386
  36.5 1.9 %collective-permute-start.3 = (bf16[128,1024]{1,0:T(8,128)(2,1)S(1)}, bf16[128,1024]{1,0:T(8,128)(2,1)S(1)}, u32[]{:S(2)}, u32[]{:S(2)}) collective-permute-start(bf16[128,1024]{1,0:T(8,128)(2,1)S(1)} %copy-done.2), channel_id=1, source_target_pairs={{0,4},{4,8},{8,12},{12,0},{1,5},{5,9},{9,13},{13,1},{2,6},{6,10},{... | collective-permute-start | bytes 786440 | tf_op jit(solution)/shard_map/ppermute | solution.py:386
  38.5 2.5 %turn.2.refs_0_ = bf16[16,64,512]{2,1,0:T(8,128)(2,1)} custom-call(bf16[128,1024]{1,0:T(8,128)(2,1)} %refs_0_.1, bf16[128,1024]{1,0:T(8,128)(2,1)} %copy-done.4, bf16[128,1024]{1,0:T(8,128)(2,1)} %copy-done.3, bf16[128,1024]{1,0:T(8,128)(2,1)} %copy-done.5), custom_call_target="tpu_custom_call" | custom-call | tf_op jit(solution)/shard_map/turn/pallas_call | solution.py:75
  41.0 15.6 %forward.2 = (bf16[16,1024,512]{2,1,0:T(8,128)(2,1)}, f32[16,512]{1,0:T(8,128)}, f32[2,16,512]{2,1,0:T(8,128)}, f32[16,64,512]{2,1,0:T(8,128)}) custom-call(bf16[16,64,512]{2,1,0:T(8,128)(2,1)} %turn.2.refs_0_, bf16[2,1024,128]{2,1,0:T(8,128)(2,1)} %project.1.refs_1_.refs_2_), custom_call_target="tpu_custom_call" | custom-call | flops 8589934592 | bytes 16777216 | tf_op jit(solution)/shard_map/forward/pallas_call | solution.py:174
  56.7 3.1 %collective-permute-done.4.refs_2_ = bf16[128,1024]{1,0:T(8,128)(2,1)S(1)} collective-permute-done((bf16[128,1024]{1,0:T(8,128)(2,1)S(1)}, bf16[128,1024]{1,0:T(8,128)(2,1)S(1)}, u32[]{:S(2)}, u32[]{:S(2)}) %collective-permute-start.4) | collective-permute-done | bytes 262176 | tf_op jit(solution)/shard_map/ppermute | solution.py:386
  61.2 2.5 %turn.3.refs_1_ = bf16[16,64,512]{2,1,0:T(8,128)(2,1)} custom-call(bf16[128,1024]{1,0:T(8,128)(2,1)} %refs_0_.2, bf16[128,1024]{1,0:T(8,128)(2,1)} %copy-done.8, bf16[128,1024]{1,0:T(8,128)(2,1)} %copy-done.7, bf16[128,1024]{1,0:T(8,128)(2,1)} %copy-done.6), custom_call_target="tpu_custom_call" | custom-call | tf_op jit(solution)/shard_map/turn/pallas_call | solution.py:75
  64.5 16.8 %forward.3 = (bf16[16,1024,512]{2,1,0:T(8,128)(2,1)}, f32[16,512]{1,0:T(8,128)}, f32[3,16,512]{2,1,0:T(8,128)}, f32[16,64,512]{2,1,0:T(8,128)}) custom-call(bf16[16,64,512]{2,1,0:T(8,128)(2,1)} %turn.2.refs_0_, bf16[16,64,512]{2,1,0:T(8,128)(2,1)} %turn.3.refs_1_, bf16[2,1024,128]{2,1,0:T(8,128)(2,1)} %copy-done.9, f32[2,16,512]{2,1,0:T(8,128)} %get-tuple-element.24.refs_3_, ...), custom_call_target="tpu_custom_call" | custom-call | flops 8589934592 | bytes 16777216 | tf_op jit(solution)/shard_map/forward/pallas_call | solution.py:174
  81.4 1.9 %collective-permute-start.7 = (f32[3,16,512]{2,1,0:T(8,128)}, f32[3,16,512]{2,1,0:T(8,128)S(1)}, u32[]{:S(2)}, u32[]{:S(2)}) collective-permute-start(f32[3,16,512]{2,1,0:T(8,128)} %get-tuple-element.28.refs_5_), channel_id=1, source_target_pairs={{0,4},{4,8},{8,12},{12,0},{1,5},{5,9},{9,13},{13,1},{2,6},{6,10},{... | collective-permute-start | bytes 294920 | tf_op jit(solution)/shard_map/ppermute | solution.py:386
  83.4 4.2 %collective-permute-done.9.refs_8_ = f32[3,16,512]{2,1,0:T(8,128)S(1)} collective-permute-done((f32[3,16,512]{2,1,0:T(8,128)}, f32[3,16,512]{2,1,0:T(8,128)S(1)}, u32[]{:S(2)}, u32[]{:S(2)}) %collective-permute-start.9) | collective-permute-done | bytes 98336 | tf_op jit(solution)/shard_map/ppermute | solution.py:386
  87.6 3.3 %collective-permute-done.8.refs_7_ = f32[3,16,512]{2,1,0:T(8,128)S(1)} collective-permute-done((f32[3,16,512]{2,1,0:T(8,128)}, f32[3,16,512]{2,1,0:T(8,128)S(1)}, u32[]{:S(2)}, u32[]{:S(2)}) %collective-permute-start.8) | collective-permute-done | bytes 98336 | tf_op jit(solution)/shard_map/ppermute | solution.py:386
  91.6 24.7 %backward.2 = (bf16[128,1024]{1,0:T(8,128)(2,1)}, bf16[128,1024]{1,0:T(8,128)(2,1)}, bf16[128,1024]{1,0:T(8,128)(2,1)}, bf16[128,1024]{1,0:T(8,128)(2,1)}, f32[1...) custom-call(bf16[16,64,512]{2,1,0:T(8,128)(2,1)} %turn.2.refs_0_, bf16[16,64,512]{2,1,0:T(8,128)(2,1)} %turn.3.refs_1_, ...), custom_call_target="tpu_custom_call" | custom-call | flops 12884901888 | bytes 16777216 | tf_op jit(solution)/shard_map/backward/pallas_call | solution.py:349
  118.6 1.9 %collective-permute-start.12 = (bf16[128,1024]{1,0:T(8,128)(2,1)}, bf16[128,1024]{1,0:T(8,128)(2,1)S(1)}, u32[]{:S(2)}, u32[]{:S(2)}) collective-permute-start(bf16[128,1024]{1,0:T(8,128)(2,1)} %get-tuple-element.33), channel_id=1, source_target_pairs={{0,4},{4,8},{8,12},{12,0},{1,5},{5,9},{9,13},{13,1},{2,6},{6,10},{... | collective-permute-start | bytes 786440 | tf_op jit(solution)/shard_map/ppermute | solution.py:386
  120.6 1.5 collective-permute-start.16
  122.1 24.3 %backward.3 = (bf16[128,1024]{1,0:T(8,128)(2,1)}, bf16[128,1024]{1,0:T(8,128)(2,1)}, bf16[128,1024]{1,0:T(8,128)(2,1)}, bf16[128,1024]{1,0:T(8,128)(2,1)}, f32[1024,256]{1,0:T(8,128)}) custom-call(bf16[16,64,512]{2,1,0:T(8,128)(2,1)} %turn.2.refs_0_, bf16[16,64,512]{2,1,0:T(8,128)(2,1)} %turn.3.refs_1_, bf16[2,1024,128]{2,1,0:T(8,128)(2,1)} %project.1.refs_1_.refs_2_, ...), custom_call_target="tpu_custom_call" | custom-call | flops 12884901888 | bytes 16777216 | tf_op jit(solution)/shard_map/backward/pallas_call | solution.py:349
  146.4 1.9 %collective-permute-start.13 = (bf16[128,1024]{1,0:T(8,128)(2,1)}, bf16[128,1024]{1,0:T(8,128)(2,1)S(1)}, u32[]{:S(2)}, u32[]{:S(2)}) collective-permute-start(bf16[128,1024]{1,0:T(8,128)(2,1)} %get-tuple-element.38), channel_id=1, source_target_pairs={{0,12},{4,0},{8,4},{12,8},{1,13},{5,1},{9,5},{13,9},{2,14},{6,2},{... | collective-permute-start | bytes 786440 | tf_op jit(solution)/shard_map/ppermute | solution.py:386
  150.1 5.3 %collective-permute-done.13 = bf16[128,1024]{1,0:T(8,128)(2,1)S(1)} collective-permute-done((bf16[128,1024]{1,0:T(8,128)(2,1)}, bf16[128,1024]{1,0:T(8,128)(2,1)S(1)}, u32[]{:S(2)}, u32[]{:S(2)}) %collective-permute-start.13) | collective-permute-done | bytes 262176 | tf_op jit(solution)/shard_map/ppermute | solution.py:386
  155.4 15.0 %collective-permute-done.14 = bf16[128,1024]{1,0:T(8,128)(2,1)S(1)} collective-permute-done((bf16[128,1024]{1,0:T(8,128)(2,1)}, bf16[128,1024]{1,0:T(8,128)(2,1)S(1)}, u32[]{:S(2)}, u32[]{:S(2)}) %collective-permute-start.14) | collective-permute-done | bytes 262176 | tf_op jit(solution)/shard_map/ppermute | solution.py:386
  170.4 1.8 %add_convert_fusion.1 = bf16[128,1024]{1,0:T(8,128)(2,1)} fusion(bf16[128,1024]{1,0:T(8,128)(2,1)S(1)} %collective-permute-done.15, bf16[128,1024]{1,0:T(8,128)(2,1)S(1)} %collective-permute-done.14, bf16[128,1024]{1,0:T(8,128)(2,1)S(1)} %collective-permute-done.13, bf16[128,1024]{1,0:T(8,128)(2,1)} %get-tuple-element.37), kind=kLoop, calls=%fused_computation.1 | loop fusion | flops 1048576 | bytes 1310720 | tf_op jit(solution)/shard_map/convert_element_type | solution.py:418
  (46 shorter events, 10.2 us)
Async XLA Ops:
  0.6 22.8 %collective-permute-start.1 = (bf16[128,1024]{1,0:T(8,128)(2,1)}, bf16[128,1024]{1,0:T(8,128)(2,1)S(1)}, u32[]{:S(2)}, u32[]{:S(2)}) collective-permute-start(bf16[128,1024]{1,0:T(8,128)(2,1)} %refs_0_.1), channel_id=1, source_target_pairs={{0,8},{4,12},{8,0},{12,4},{1,9},{5,13},{9,1},{13,5},{2,10},{6,14},... | collective-permute-start | bytes 786440 | tf_op jit(solution)/shard_map/ppermute | solution.py:386
  4.8 18.7 %collective-permute-start = (bf16[128,1024]{1,0:T(8,128)(2,1)}, bf16[128,1024]{1,0:T(8,128)(2,1)S(1)}, u32[]{:S(2)}, u32[]{:S(2)}) collective-permute-start(bf16[128,1024]{1,0:T(8,128)(2,1)} %refs_0_.1), channel_id=1, source_target_pairs={{0,4},{4,8},{8,12},{12,0},{1,5},{5,9},{9,13},{13,1},{2,6},{6,10},{... | collective-permute-start | bytes 786440 | tf_op jit(solution)/shard_map/ppermute | solution.py:386
  6.3 17.8 %collective-permute-start.2 = (bf16[128,1024]{1,0:T(8,128)(2,1)}, bf16[128,1024]{1,0:T(8,128)(2,1)S(1)}, u32[]{:S(2)}, u32[]{:S(2)}) collective-permute-start(bf16[128,1024]{1,0:T(8,128)(2,1)} %refs_0_.1), channel_id=1, source_target_pairs={{0,12},{4,0},{8,4},{12,8},{1,13},{5,1},{9,5},{13,9},{2,14},{6,2},{... | collective-permute-start | bytes 786440 | tf_op jit(solution)/shard_map/ppermute | solution.py:386
  8.6 15.5 %copy-start.2 = (bf16[128,1024]{1,0:T(8,128)(2,1)S(1)}, bf16[128,1024]{1,0:T(8,128)(2,1)}, u32[]{:S(2)}) copy-start(bf16[128,1024]{1,0:T(8,128)(2,1)} %refs_0_.2) | copy-start | bytes 786436
  16.9 46.8 %collective-permute-start.6 = (bf16[2,1024,128]{2,1,0:T(8,128)(2,1)}, bf16[2,1024,128]{2,1,0:T(8,128)(2,1)S(1)}, u32[]{:S(2)}, u32[]{:S(2)}) collective-permute-start(bf16[2,1024,128]{2,1,0:T(8,128)(2,1)} %project.1.refs_1_.refs_2_), channel_id=1, source_target_pairs={{0,16},{16,0},{1,17},{17,1},{2,18},{18,2},{3,19},{19,3},{4,20},{20... | collective-permute-start | bytes 1572872 | tf_op jit(solution)/shard_map/ppermute | solution.py:389
  23.4 15.1 %copy-start.3 = (bf16[128,1024]{1,0:T(8,128)(2,1)}, bf16[128,1024]{1,0:T(8,128)(2,1)S(1)}, u32[]{:S(2)}) copy-start(bf16[128,1024]{1,0:T(8,128)(2,1)S(1)} %collective-permute-done.1.refs_2_) | copy-start | bytes 786436
  23.4 15.1 %copy-start.4 = (bf16[128,1024]{1,0:T(8,128)(2,1)}, bf16[128,1024]{1,0:T(8,128)(2,1)S(1)}, u32[]{:S(2)}) copy-start(bf16[128,1024]{1,0:T(8,128)(2,1)S(1)} %collective-permute-done.refs_1_) | copy-start | bytes 786436
  24.1 14.4 %copy-start.5 = (bf16[128,1024]{1,0:T(8,128)(2,1)}, bf16[128,1024]{1,0:T(8,128)(2,1)S(1)}, u32[]{:S(2)}) copy-start(bf16[128,1024]{1,0:T(8,128)(2,1)S(1)} %collective-permute-done.2.refs_3_) | copy-start | bytes 786436
  24.1 32.5 %collective-permute-start.5 = (bf16[128,1024]{1,0:T(8,128)(2,1)S(1)}, bf16[128,1024]{1,0:T(8,128)(2,1)S(1)}, u32[]{:S(2)}, u32[]{:S(2)}) collective-permute-start(bf16[128,1024]{1,0:T(8,128)(2,1)S(1)} %copy-done.2), channel_id=1, source_target_pairs={{0,12},{4,0},{8,4},{12,8},{1,13},{5,1},{9,5},{13,9},{2,14},{6,2},{... | collective-permute-start | bytes 786440 | tf_op jit(solution)/shard_map/ppermute | solution.py:386
  26.2 33.6 %collective-permute-start.4 = (bf16[128,1024]{1,0:T(8,128)(2,1)S(1)}, bf16[128,1024]{1,0:T(8,128)(2,1)S(1)}, u32[]{:S(2)}, u32[]{:S(2)}) collective-permute-start(bf16[128,1024]{1,0:T(8,128)(2,1)S(1)} %copy-done.2), channel_id=1, source_target_pairs={{0,8},{4,12},{8,0},{12,4},{1,9},{5,13},{9,1},{13,5},{2,10},{6,14},... | collective-permute-start | bytes 786440 | tf_op jit(solution)/shard_map/ppermute | solution.py:386
  36.5 23.3 %collective-permute-start.3 = (bf16[128,1024]{1,0:T(8,128)(2,1)S(1)}, bf16[128,1024]{1,0:T(8,128)(2,1)S(1)}, u32[]{:S(2)}, u32[]{:S(2)}) collective-permute-start(bf16[128,1024]{1,0:T(8,128)(2,1)S(1)} %copy-done.2), channel_id=1, source_target_pairs={{0,4},{4,8},{8,12},{12,0},{1,5},{5,9},{9,13},{13,1},{2,6},{6,10},{... | collective-permute-start | bytes 786440 | tf_op jit(solution)/shard_map/ppermute | solution.py:386
  81.3 6.3 %collective-permute-start.9 = (f32[3,16,512]{2,1,0:T(8,128)}, f32[3,16,512]{2,1,0:T(8,128)S(1)}, u32[]{:S(2)}, u32[]{:S(2)}) collective-permute-start(f32[3,16,512]{2,1,0:T(8,128)} %get-tuple-element.28.refs_5_), channel_id=1, source_target_pairs={{0,12},{4,0},{8,4},{12,8},{1,13},{5,1},{9,5},{13,9},{2,14},{6,2},{... | collective-permute-start | bytes 294920 | tf_op jit(solution)/shard_map/ppermute | solution.py:386
  81.4 9.6 %collective-permute-start.8 = (f32[3,16,512]{2,1,0:T(8,128)}, f32[3,16,512]{2,1,0:T(8,128)S(1)}, u32[]{:S(2)}, u32[]{:S(2)}) collective-permute-start(f32[3,16,512]{2,1,0:T(8,128)} %get-tuple-element.28.refs_5_), channel_id=1, source_target_pairs={{0,8},{4,12},{8,0},{12,4},{1,9},{5,13},{9,1},{13,5},{2,10},{6,14},... | collective-permute-start | bytes 294920 | tf_op jit(solution)/shard_map/ppermute | solution.py:386
  81.4 9.5 %collective-permute-start.7 = (f32[3,16,512]{2,1,0:T(8,128)}, f32[3,16,512]{2,1,0:T(8,128)S(1)}, u32[]{:S(2)}, u32[]{:S(2)}) collective-permute-start(f32[3,16,512]{2,1,0:T(8,128)} %get-tuple-element.28.refs_5_), channel_id=1, source_target_pairs={{0,4},{4,8},{8,12},{12,0},{1,5},{5,9},{9,13},{13,1},{2,6},{6,10},{... | collective-permute-start | bytes 294920 | tf_op jit(solution)/shard_map/ppermute | solution.py:386
  87.6 3.3 %copy-start.10 = (f32[3,16,512]{2,1,0:T(8,128)}, f32[3,16,512]{2,1,0:T(8,128)S(1)}, u32[]{:S(2)}) copy-start(f32[3,16,512]{2,1,0:T(8,128)S(1)} %collective-permute-done.9.refs_8_) | copy-start | bytes 294916
  116.3 32.1 %collective-permute-start.10 = (bf16[128,1024]{1,0:T(8,128)(2,1)}, bf16[128,1024]{1,0:T(8,128)(2,1)S(1)}, u32[]{:S(2)}, u32[]{:S(2)}) collective-permute-start(bf16[128,1024]{1,0:T(8,128)(2,1)} %get-tuple-element.31), channel_id=1, source_target_pairs={{0,12},{4,0},{8,4},{12,8},{1,13},{5,1},{9,5},{13,9},{2,14},{6,2},{... | collective-permute-start | bytes 786440 | tf_op jit(solution)/shard_map/ppermute | solution.py:386
  117.7 30.9 %collective-permute-start.11 = (bf16[128,1024]{1,0:T(8,128)(2,1)}, bf16[128,1024]{1,0:T(8,128)(2,1)S(1)}, u32[]{:S(2)}, u32[]{:S(2)}) collective-permute-start(bf16[128,1024]{1,0:T(8,128)(2,1)} %get-tuple-element.32), channel_id=1, source_target_pairs={{0,8},{4,12},{8,0},{12,4},{1,9},{5,13},{9,1},{13,5},{2,10},{6,14},... | collective-permute-start | bytes 786440 | tf_op jit(solution)/shard_map/ppermute | solution.py:386
  118.6 30.6 %collective-permute-start.12 = (bf16[128,1024]{1,0:T(8,128)(2,1)}, bf16[128,1024]{1,0:T(8,128)(2,1)S(1)}, u32[]{:S(2)}, u32[]{:S(2)}) collective-permute-start(bf16[128,1024]{1,0:T(8,128)(2,1)} %get-tuple-element.33), channel_id=1, source_target_pairs={{0,4},{4,8},{8,12},{12,0},{1,5},{5,9},{9,13},{13,1},{2,6},{6,10},{... | collective-permute-start | bytes 786440 | tf_op jit(solution)/shard_map/ppermute | solution.py:386
  120.6 51.6 %collective-permute-start.16 = (bf16[1024,256]{1,0:T(8,128)(2,1)}, bf16[1024,256]{1,0:T(8,128)(2,1)S(1)}, u32[]{:S(2)}, u32[]{:S(2)}) collective-permute-start(bf16[1024,256]{1,0:T(8,128)(2,1)} %get-tuple-element.41), channel_id=1, source_target_pairs={{0,16},{16,0},{1,17},{17,1},{2,18},{18,2},{3,19},{19,3},{4,20},{20... | collective-permute-start | bytes 1572872 | tf_op jit(solution)/shard_map/ppermute | solution.py:389
  122.1 27.2 %copy-start.1 = (bf16[128,1024]{1,0:T(8,128)(2,1)S(1)}, bf16[128,1024]{1,0:T(8,128)(2,1)}, u32[]{:S(2)}) copy-start(bf16[128,1024]{1,0:T(8,128)(2,1)} %get-tuple-element.30) | copy-start | bytes 786436
  146.4 25.8 %copy-start = (f32[1024,256]{1,0:T(8,128)S(1)}, f32[1024,256]{1,0:T(8,128)}, u32[]{:S(2)}) copy-start(f32[1024,256]{1,0:T(8,128)} %get-tuple-element.42) | copy-start | bytes 3145732
  146.4 9.0 %collective-permute-start.13 = (bf16[128,1024]{1,0:T(8,128)(2,1)}, bf16[128,1024]{1,0:T(8,128)(2,1)S(1)}, u32[]{:S(2)}, u32[]{:S(2)}) collective-permute-start(bf16[128,1024]{1,0:T(8,128)(2,1)} %get-tuple-element.38), channel_id=1, source_target_pairs={{0,12},{4,0},{8,4},{12,8},{1,13},{5,1},{9,5},{13,9},{2,14},{6,2},{... | collective-permute-start | bytes 786440 | tf_op jit(solution)/shard_map/ppermute | solution.py:386
  148.4 22.0 %collective-permute-start.14 = (bf16[128,1024]{1,0:T(8,128)(2,1)}, bf16[128,1024]{1,0:T(8,128)(2,1)S(1)}, u32[]{:S(2)}, u32[]{:S(2)}) collective-permute-start(bf16[128,1024]{1,0:T(8,128)(2,1)} %get-tuple-element.39), channel_id=1, source_target_pairs={{0,8},{4,12},{8,0},{12,4},{1,9},{5,13},{9,1},{13,5},{2,10},{6,14},... | collective-permute-start | bytes 786440 | tf_op jit(solution)/shard_map/ppermute | solution.py:386
  148.6 21.8 %collective-permute-start.15 = (bf16[128,1024]{1,0:T(8,128)(2,1)}, bf16[128,1024]{1,0:T(8,128)(2,1)S(1)}, u32[]{:S(2)}, u32[]{:S(2)}) collective-permute-start(bf16[128,1024]{1,0:T(8,128)(2,1)} %get-tuple-element.40), channel_id=1, source_target_pairs={{0,4},{4,8},{8,12},{12,0},{1,5},{5,9},{9,13},{13,1},{2,6},{6,10},{... | collective-permute-start | bytes 786440 | tf_op jit(solution)/shard_map/ppermute | solution.py:386
  (6 other events, 6.7 us)

commit v2 on v1

--- a/solution.py
+++ b/solution.py
@@ -379,7 +379,7 @@
     per_group_heads = width // (groups * HD)
     heads = min(per_group_heads, max(1, 512 // tokens))
     per_group = per_group_heads // heads
-    chunks = seqs * groups * per_group
+    chunks = halves * groups * per_group
     dims = (chunks, groups, per_group)
 
     def from_seq(x, shift):
@@ -388,33 +388,33 @@
     def from_half(x, shift):
         return lax.ppermute(x, "half", [(i, (i + shift) % halves) for i in range(halves)])
 
-    q_blocks = [queries] + [from_seq(queries, s) for s in range(1, seqs)]
-    late, *_ = lax.optimization_barrier((cotangent, *q_blocks[1:]))
-    c_blocks = [late] + [from_seq(late, s) for s in range(1, seqs)]
+    q_blocks = [queries] + [from_half(queries, s) for s in range(1, halves)]
+    c_blocks = [cotangent] + [from_half(cotangent, s) for s in range(1, halves)]
     own_pairs = project(enc_states, norm_gain, kv_weight)
-    pair_blocks = [own_pairs] + [from_half(own_pairs, s) for s in range(1, halves)]
+    order = sorted(range(seqs), key=lambda s: min(s, seqs - s))
+    pair_blocks = [own_pairs] + [from_seq(own_pairs, s) for s in order[1:]]
     q_rows = turn(q_blocks, heads)
     c_rows = turn(c_blocks, heads)
 
     expos, tops, before = [], [], None
     for i, pairs in enumerate(pair_blocks):
-        expo, top, stats, acc = forward(dims, q_rows, c_rows if i == halves - 1 else None, pairs, before)
+        expo, top, stats, acc = forward(dims, q_rows, c_rows if i == seqs - 1 else None, pairs, before)
         expos.append(expo)
         tops.append(top)
         before = (stats, acc)
-    peers = [from_seq(stats, r) for r in range(1, seqs)]
+    peers = [from_half(stats, r) for r in range(1, halves)]
 
     dq, sends, context_parts = None, [], None
-    for i in reversed(range(halves)):
+    for i in reversed(range(seqs)):
         parts, dq, dkv = backward(
             dims, q_rows, c_rows, pair_blocks[i], expos[i], tops[i], stats, peers, acc, dq, i == 0, tokens
         )
         if parts is not None:
             context_parts = parts
-        sends.append(dkv if i == 0 else from_half(dkv, -i))
+        sends.append(dkv if i == 0 else from_seq(dkv, -order[i]))
 
     def home(parts):
-        arrived = [parts[0]] + [from_seq(parts[s], -s) for s in range(1, seqs)]
+        arrived = [parts[0]] + [from_half(parts[s], -s) for s in range(1, halves)]
         return sum(x.astype(f32) for x in arrived).astype(bf16)
 
     context = home(context_parts)

time: 174 us -> 166 us (0.954)
  waiting for transfers between devices: 36.8 us -> 23.7 us
  Pallas kernels: 94.7 us -> 106 us
  starting transfers between devices: 34.4 us -> 24.8 us
    ppermute x15 -> x6, waiting for transfers between devices: 36.7 us -> 15.6 us  [from_seq(): lax.ppermute(x, 'seq', [(i, (i + shift) % seqs) for i in range(seqs)])]
    ppermute x15 -> x6, starting transfers between devices: 31.5 us -> 18.5 us  [from_seq(): lax.ppermute(x, 'seq', [(i, (i + shift) % seqs) for i in range(seqs)])]
    ppermute x2 -> x5, waiting for transfers between devices: 0.01 us -> 8.09 us  [from_half(): lax.ppermute(x, 'half', [(i, (i + shift) % halves) for i in range(halves)])]
    pallas_call x2 -> x4, Pallas kernels: 32.4 us -> 38.6 us  [forward(): pl.pallas_call(functools.partial(forward_kernel, dims, first, last), in_s...]
    pallas_call x2 -> x4, Pallas kernels: 49 us -> 55.1 us  [backward(): pl.pallas_call(functools.partial(backward_kernel, dims, len(peers), first...]
    ppermute x2 -> x5, starting transfers between devices: 2.97 us -> 6.33 us  [from_half(): lax.ppermute(x, 'half', [(i, (i + shift) % halves) for i in range(halves)])]
    unnamed x26 -> x20, local copies, waits for them, and re-layouts: 2.88 us -> 4.44 us
  transfers between devices with their start and end apart: 17 -> 11, of which waited for: 7 -> 4; matrix products, arithmetic and copies ran while one was open for 2% -> 2% of each run, Pallas kernels for 31% -> 50%
where the time goes in v2:
time: 166 us; the launch traced here: 164 us
  Pallas kernels  106 us (64%)
  starting transfers between devices  24.8 us (15%)
  waiting for transfers between devices  23.7 us (14%)
  other arithmetic  4.73 us (3%)
  local copies, waits for them, and re-layouts  4.44 us (3%)
    pallas_call x4, Pallas kernels, backward(): pl.pallas_call(functools.partial(backward_kernel, dims, len(peers), first...  55.1 us
    pallas_call x4, Pallas kernels, forward(): pl.pallas_call(functools.partial(forward_kernel, dims, first, last), in_s...  38.6 us
    ppermute x6, starting transfers between devices, from_seq(): lax.ppermute(x, 'seq', [(i, (i + shift) % seqs) for i in range(seqs)])  18.5 us
    ppermute x6, waiting for transfers between devices, from_seq(): lax.ppermute(x, 'seq', [(i, (i + shift) % seqs) for i in range(seqs)])  15.6 us
    pallas_call x1, Pallas kernels, project(): pl.pallas_call(project_kernel, grid=(rows // block,), in_specs=[pl.BlockS...  8.26 us
    ppermute x5, waiting for transfers between devices, from_half(): lax.ppermute(x, 'half', [(i, (i + shift) % halves) for i in range(halves)])  8.09 us
    ppermute x5, starting transfers between devices, from_half(): lax.ppermute(x, 'half', [(i, (i + shift) % halves) for i in range(halves)])  6.33 us
    unnamed x20, local copies, waits for them, and re-layouts  4.44 us
  transfers between devices with their start and end apart: 11, of which 4 were waited for; matrix products, arithmetic and copies ran while one was open for 2% of the time, Pallas kernels for 50%

profile of v2, /device:TPU:0, one launch (start us, length us, event | category | flops | bytes accessed | tf_op | source)
XLA Modules:
  0.0 164.5 jit_solution(16685550947106037811)
XLA Ops:
  0.6 3.0 %collective-permute-start = (bf16[128,1024]{1,0:T(8,128)(2,1)}, bf16[128,1024]{1,0:T(8,128)(2,1)S(1)}, u32[]{:S(2)}, u32[]{:S(2)}) collective-permute-start(bf16[128,1024]{1,0:T(8,128)(2,1)} %refs_0_.2), channel_id=1, source_target_pairs={{0,16},{16,0},{1,17},{17,1},{2,18},{18,2},{3,19},{19,3},{4,20},{20... | collective-permute-start | bytes 786440 | tf_op jit(solution)/shard_map/ppermute | solution.py:389
  3.7 8.3 %project.1.refs_1_.refs_2_ = bf16[2,1024,128]{2,1,0:T(8,128)(2,1)} custom-call(bf16[1024,4096]{1,0:T(8,128)(2,1)} %x_ref.1, f32[1,4096]{1,0:T(1,128)} %bitcast.1, bf16[4096,256]{1,0:T(8,128)(2,1)} %w_ref.1), custom_call_target="tpu_custom_call" | custom-call | flops 2147483648 | bytes 8388608 | tf_op jit(solution)/shard_map/project/pallas_call | solution.py:39
  11.9 1.6 collective-permute-start.4
  13.5 2.3 %collective-permute-start.3 = (bf16[2,1024,128]{2,1,0:T(8,128)(2,1)}, bf16[2,1024,128]{2,1,0:T(8,128)(2,1)S(1)}, u32[]{:S(2)}, u32[]{:S(2)}) collective-permute-start(bf16[2,1024,128]{2,1,0:T(8,128)(2,1)} %project.1.refs_1_.refs_2_), channel_id=1, source_target_pairs={{0,12},{4,0},{8,4},{12,8},{1,13},{5,1},{9,5},{13,9},{2,14},{6,2},{... | collective-permute-start | bytes 1572872 | tf_op jit(solution)/shard_map/ppermute | solution.py:386
  17.8 2.0 %turn.2.refs_0_ = bf16[8,64,512]{2,1,0:T(8,128)(2,1)} custom-call(bf16[128,1024]{1,0:T(8,128)(2,1)} %refs_0_.2, bf16[128,1024]{1,0:T(8,128)(2,1)} %copy-done.2), custom_call_target="tpu_custom_call" | custom-call | tf_op jit(solution)/shard_map/turn/pallas_call | solution.py:75
  19.8 9.4 %forward.4 = (bf16[8,1024,512]{2,1,0:T(8,128)(2,1)}, f32[8,512]{1,0:T(8,128)}, f32[2,8,512]{2,1,0:T(8,128)}, f32[8,64,512]{2,1,0:T(8,128)}) custom-call(bf16[8,64,512]{2,1,0:T(8,128)(2,1)} %turn.2.refs_0_, bf16[2,1024,128]{2,1,0:T(8,128)(2,1)} %project.1.refs_1_.refs_2_), custom_call_target="tpu_custom_call" | custom-call | flops 4294967296 | bytes 8388608 | tf_op jit(solution)/shard_map/forward/pallas_call | solution.py:174
  29.9 2.0 %turn.3.refs_1_ = bf16[8,64,512]{2,1,0:T(8,128)(2,1)} custom-call(bf16[128,1024]{1,0:T(8,128)(2,1)} %refs_0_.3, bf16[128,1024]{1,0:T(8,128)(2,1)} %copy-done.3), custom_call_target="tpu_custom_call" | custom-call | tf_op jit(solution)/shard_map/turn/pallas_call | solution.py:75
  32.7 9.6 %forward.5 = (bf16[8,1024,512]{2,1,0:T(8,128)(2,1)}, f32[8,512]{1,0:T(8,128)}, f32[2,8,512]{2,1,0:T(8,128)}, f32[8,64,512]{2,1,0:T(8,128)}) custom-call(bf16[8,64,512]{2,1,0:T(8,128)(2,1)} %turn.2.refs_0_, bf16[2,1024,128]{2,1,0:T(8,128)(2,1)} %copy-done.4, f32[2,8,512]{2,1,0:T(8,128)} %get-tuple-element.30.refs_2_, f32[8,64,512]{2,1,0:T(8,128)} %get-tuple-element.31.refs_3_), custom_call_target="tpu_custom_call" | custom-call | flops 4294967296 | bytes 8388608 | tf_op jit(solution)/shard_map/forward/pallas_call | solution.py:174
  43.2 9.6 %forward.6 = (bf16[8,1024,512]{2,1,0:T(8,128)(2,1)}, f32[8,512]{1,0:T(8,128)}, f32[2,8,512]{2,1,0:T(8,128)}, f32[8,64,512]{2,1,0:T(8,128)}) custom-call(bf16[8,64,512]{2,1,0:T(8,128)(2,1)} %turn.2.refs_0_, bf16[2,1024,128]{2,1,0:T(8,128)(2,1)} %copy-done.5, f32[2,8,512]{2,1,0:T(8,128)} %get-tuple-element.32.refs_2_, f32[8,64,512]{2,1,0:T(8,128)} %get-tuple-element.33.refs_3_), custom_call_target="tpu_custom_call" | custom-call | flops 4294967296 | bytes 8388608 | tf_op jit(solution)/shard_map/forward/pallas_call | solution.py:174
  52.8 8.3 %collective-permute-done.2.refs_2_ = bf16[2,1024,128]{2,1,0:T(8,128)(2,1)S(1)} collective-permute-done((bf16[2,1024,128]{2,1,0:T(8,128)(2,1)}, bf16[2,1024,128]{2,1,0:T(8,128)(2,1)S(1)}, u32[]{:S(2)}, u32[]{:S(2)}) %collective-permute-start.2) | collective-permute-done | bytes 524320 | tf_op jit(solution)/shard_map/ppermute | solution.py:386
  61.9 10.0 %forward.7 = (bf16[8,1024,512]{2,1,0:T(8,128)(2,1)}, f32[8,512]{1,0:T(8,128)}, f32[3,8,512]{2,1,0:T(8,128)}, f32[8,64,512]{2,1,0:T(8,128)}) custom-call(bf16[8,64,512]{2,1,0:T(8,128)(2,1)} %turn.2.refs_0_, bf16[8,64,512]{2,1,0:T(8,128)(2,1)} %turn.3.refs_1_, bf16[2,1024,128]{2,1,0:T(8,128)(2,1)} %copy-done.7, f32[2,8,512]{2,1,0:T(8,128)} %get-tuple-element.34.refs_3_, ...), custom_call_target="tpu_custom_call" | custom-call | flops 4294967296 | bytes 8388608 | tf_op jit(solution)/shard_map/forward/pallas_call | solution.py:174
  72.5 3.8 %collective-permute-done.5.refs_6_ = f32[3,8,512]{2,1,0:T(8,128)S(1)} collective-permute-done((f32[3,8,512]{2,1,0:T(8,128)}, f32[3,8,512]{2,1,0:T(8,128)S(1)}, u32[]{:S(2)}, u32[]{:S(2)}) %collective-permute-start.5) | collective-permute-done | bytes 49184 | tf_op jit(solution)/shard_map/ppermute | solution.py:389
  76.8 13.7 %backward.4 = (bf16[128,1024]{1,0:T(8,128)(2,1)}, bf16[128,1024]{1,0:T(8,128)(2,1)}, f32[8,64,512]{2,1,0:T(8,128)}, bf16[1024,256]{1,0:T(8,128)(2,1)}) custom-call(bf16[8,64,512]{2,1,0:T(8,128)(2,1)} %turn.2.refs_0_, bf16[8,64,512]{2,1,0:T(8,128)(2,1)} %turn.3.refs_1_, bf16[2,1024,128]{2,1,0:T(8,128)(2,1)} %copy-done.7, ...), custom_call_target="tpu_custom_call" | custom-call | flops 6442450944 | bytes 8388608 | tf_op jit(solution)/shard_map/backward/pallas_call | solution.py:349
  91.1 13.4 %backward.5 = (f32[8,64,512]{2,1,0:T(8,128)}, bf16[1024,256]{1,0:T(8,128)(2,1)}) custom-call(bf16[8,64,512]{2,1,0:T(8,128)(2,1)} %turn.2.refs_0_, bf16[8,64,512]{2,1,0:T(8,128)(2,1)} %turn.3.refs_1_, bf16[2,1024,128]{2,1,0:T(8,128)(2,1)} %copy-done.5, bf16[8,1024,512]{2,1,0:T(8,128)(2,1)} %get-tuple-element.46.refs_3_, f32[8,512]{1,0:T(8,128)} %get-tuple-element.47.refs_4_, ...), custom_call_target="tpu_custom_call" | custom-call | flops 6442450944 | bytes 8388608 | tf_op jit(solution)/shard_map/backward/pallas_call | solution.py:349
  104.5 13.4 %backward.6 = (f32[8,64,512]{2,1,0:T(8,128)}, bf16[1024,256]{1,0:T(8,128)(2,1)}) custom-call(bf16[8,64,512]{2,1,0:T(8,128)(2,1)} %turn.2.refs_0_, bf16[8,64,512]{2,1,0:T(8,128)(2,1)} %turn.3.refs_1_, bf16[2,1024,128]{2,1,0:T(8,128)(2,1)} %copy-done.4, bf16[8,1024,512]{2,1,0:T(8,128)(2,1)} %get-tuple-element.44.refs_3_, f32[8,512]{1,0:T(8,128)} %get-tuple-element.45.refs_4_, ...), custom_call_target="tpu_custom_call" | custom-call | flops 6442450944 | bytes 8388608 | tf_op jit(solution)/shard_map/backward/pallas_call | solution.py:349
  117.9 1.7 %collective-permute-start.10 = (bf16[1024,256]{1,0:T(8,128)(2,1)}, bf16[1024,256]{1,0:T(8,128)(2,1)S(1)}, u32[]{:S(2)}, u32[]{:S(2)}) collective-permute-start(bf16[1024,256]{1,0:T(8,128)(2,1)} %get-tuple-element.55), channel_id=1, source_target_pairs={{0,12},{4,0},{8,4},{12,8},{1,13},{5,1},{9,5},{13,9},{2,14},{6,2},{... | collective-permute-start | bytes 1572872 | tf_op jit(solution)/shard_map/ppermute | solution.py:386
  119.6 8.4 %collective-permute-start.9 = (bf16[1024,256]{1,0:T(8,128)(2,1)S(1)}, bf16[1024,256]{1,0:T(8,128)(2,1)S(1)}, u32[]{:S(2)}, u32[]{:S(2)}) collective-permute-start(bf16[1024,256]{1,0:T(8,128)(2,1)S(1)} %copy-done.8), channel_id=1, source_target_pairs={{0,4},{4,8},{8,12},{12,0},{1,5},{5,9},{9,13},{13,1},{2,6},{6,10},{... | collective-permute-start | bytes 1572872 | tf_op jit(solution)/shard_map/ppermute | solution.py:386
  128.1 3.8 %collective-permute-start.8 = (bf16[1024,256]{1,0:T(8,128)(2,1)S(1)}, bf16[1024,256]{1,0:T(8,128)(2,1)S(1)}, u32[]{:S(2)}, u32[]{:S(2)}) collective-permute-start(bf16[1024,256]{1,0:T(8,128)(2,1)S(1)} %copy-done.6), channel_id=1, source_target_pairs={{0,8},{4,12},{8,0},{12,4},{1,9},{5,13},{9,1},{13,5},{2,10},{6,14},... | collective-permute-start | bytes 1572872 | tf_op jit(solution)/shard_map/ppermute | solution.py:386
  131.8 14.7 %backward.7 = (bf16[128,1024]{1,0:T(8,128)(2,1)}, bf16[128,1024]{1,0:T(8,128)(2,1)}, f32[1024,256]{1,0:T(8,128)}) custom-call(bf16[8,64,512]{2,1,0:T(8,128)(2,1)} %turn.2.refs_0_, bf16[8,64,512]{2,1,0:T(8,128)(2,1)} %turn.3.refs_1_, bf16[2,1024,128]{2,1,0:T(8,128)(2,1)} %project.1.refs_1_.refs_2_, bf16[8,1024,512]{2,1,0:T(8,128)(2,1)} %get-tuple-element.42.refs_3_, ...), custom_call_target="tpu_custom_call" | custom-call | flops 6442450944 | bytes 8388608 | tf_op jit(solution)/shard_map/backward/pallas_call | solution.py:349
  146.5 1.6 collective-permute-start.7
  148.9 4.3 %collective-permute-done.7 = bf16[128,1024]{1,0:T(8,128)(2,1)S(1)} collective-permute-done((bf16[128,1024]{1,0:T(8,128)(2,1)}, bf16[128,1024]{1,0:T(8,128)(2,1)S(1)}, u32[]{:S(2)}, u32[]{:S(2)}) %collective-permute-start.7) | collective-permute-done | bytes 262176 | tf_op jit(solution)/shard_map/ppermute | solution.py:389
  153.2 1.7 %add_convert_fusion.1 = bf16[128,1024]{1,0:T(8,128)(2,1)} fusion(bf16[128,1024]{1,0:T(8,128)(2,1)S(1)} %collective-permute-done.7, bf16[128,1024]{1,0:T(8,128)(2,1)} %get-tuple-element.51), kind=kLoop, calls=%fused_computation.1 | loop fusion | flops 524288 | bytes 786432 | tf_op jit(solution)/shard_map/convert_element_type | solution.py:418
  154.9 7.4 %collective-permute-done.8 = bf16[1024,256]{1,0:T(8,128)(2,1)S(1)} collective-permute-done((bf16[1024,256]{1,0:T(8,128)(2,1)S(1)}, bf16[1024,256]{1,0:T(8,128)(2,1)S(1)}, u32[]{:S(2)}, u32[]{:S(2)}) %collective-permute-start.8) | collective-permute-done | bytes 524320 | tf_op jit(solution)/shard_map/ppermute | solution.py:386
  162.2 2.2 %add_convert_fusion = bf16[1024,256]{1,0:T(8,128)(2,1)} fusion(f32[1024,256]{1,0:T(8,128)} %get-tuple-element.56, bf16[1024,256]{1,0:T(8,128)(2,1)S(1)} %collective-permute-done.10, bf16[1024,256]{1,0:T(8,128)(2,1)S(1)} %collective-permute-done.9, bf16[1024,256]{1,0:T(8,128)(2,1)S(1)} %collective-permute-done.8), kind=kLoop, calls=%fused_computation | loop fusion | flops 1835008 | bytes 3145728 | tf_op jit(solution)/shard_map/convert_element_type | solution.py:422
  (32 shorter events, 7.8 us)
Async XLA Ops:
  0.6 15.9 %copy-start.1 = (bf16[128,1024]{1,0:T(8,128)(2,1)S(1)}, bf16[128,1024]{1,0:T(8,128)(2,1)}, u32[]{:S(2)}) copy-start(bf16[128,1024]{1,0:T(8,128)(2,1)} %refs_0_.3) | copy-start | bytes 786436
  0.6 16.4 %collective-permute-start = (bf16[128,1024]{1,0:T(8,128)(2,1)}, bf16[128,1024]{1,0:T(8,128)(2,1)S(1)}, u32[]{:S(2)}, u32[]{:S(2)}) collective-permute-start(bf16[128,1024]{1,0:T(8,128)(2,1)} %refs_0_.2), channel_id=1, source_target_pairs={{0,16},{16,0},{1,17},{17,1},{2,18},{18,2},{3,19},{19,3},{4,20},{20... | collective-permute-start | bytes 786440 | tf_op jit(solution)/shard_map/ppermute | solution.py:389
  11.9 20.0 %collective-permute-start.4 = (bf16[2,1024,128]{2,1,0:T(8,128)(2,1)}, bf16[2,1024,128]{2,1,0:T(8,128)(2,1)S(1)}, u32[]{:S(2)}, u32[]{:S(2)}) collective-permute-start(bf16[2,1024,128]{2,1,0:T(8,128)(2,1)} %project.1.refs_1_.refs_2_), channel_id=1, source_target_pairs={{0,4},{4,8},{8,12},{12,0},{1,5},{5,9},{9,13},{13,1},{2,6},{6,10},{... | collective-permute-start | bytes 1572872 | tf_op jit(solution)/shard_map/ppermute | solution.py:386
  13.5 28.9 %collective-permute-start.3 = (bf16[2,1024,128]{2,1,0:T(8,128)(2,1)}, bf16[2,1024,128]{2,1,0:T(8,128)(2,1)S(1)}, u32[]{:S(2)}, u32[]{:S(2)}) collective-permute-start(bf16[2,1024,128]{2,1,0:T(8,128)(2,1)} %project.1.refs_1_.refs_2_), channel_id=1, source_target_pairs={{0,12},{4,0},{8,4},{12,8},{1,13},{5,1},{9,5},{13,9},{2,14},{6,2},{... | collective-permute-start | bytes 1572872 | tf_op jit(solution)/shard_map/ppermute | solution.py:386
  15.8 45.3 %collective-permute-start.2 = (bf16[2,1024,128]{2,1,0:T(8,128)(2,1)}, bf16[2,1024,128]{2,1,0:T(8,128)(2,1)S(1)}, u32[]{:S(2)}, u32[]{:S(2)}) collective-permute-start(bf16[2,1024,128]{2,1,0:T(8,128)(2,1)} %project.1.refs_1_.refs_2_), channel_id=1, source_target_pairs={{0,8},{4,12},{8,0},{12,4},{1,9},{5,13},{9,1},{13,5},{2,10},{6,14},... | collective-permute-start | bytes 1572872 | tf_op jit(solution)/shard_map/ppermute | solution.py:386
  16.5 12.7 %collective-permute-start.1 = (bf16[128,1024]{1,0:T(8,128)(2,1)S(1)}, bf16[128,1024]{1,0:T(8,128)(2,1)S(1)}, u32[]{:S(2)}, u32[]{:S(2)}) collective-permute-start(bf16[128,1024]{1,0:T(8,128)(2,1)S(1)} %copy-done.1), channel_id=1, source_target_pairs={{0,16},{16,0},{1,17},{17,1},{2,18},{18,2},{3,19},{19,3},{4,20},{20... | collective-permute-start | bytes 786440 | tf_op jit(solution)/shard_map/ppermute | solution.py:389
  17.1 0.7 copy-start.2
  29.2 0.7 copy-start.3
  31.9 0.8 copy-start.4
  42.4 0.8 copy-start.5
  61.1 0.8 copy-start.7
  71.9 4.4 %collective-permute-start.5 = (f32[3,8,512]{2,1,0:T(8,128)}, f32[3,8,512]{2,1,0:T(8,128)S(1)}, u32[]{:S(2)}, u32[]{:S(2)}) collective-permute-start(f32[3,8,512]{2,1,0:T(8,128)} %get-tuple-element.38.refs_5_), channel_id=1, source_target_pairs={{0,16},{16,0},{1,17},{17,1},{2,18},{18,2},{3,19},{19,3},{4,20},{20... | collective-permute-start | bytes 147464 | tf_op jit(solution)/shard_map/ppermute | solution.py:389
  76.2 0.6 copy-start.9
  90.5 57.6 %collective-permute-start.6 = (bf16[128,1024]{1,0:T(8,128)(2,1)}, bf16[128,1024]{1,0:T(8,128)(2,1)S(1)}, u32[]{:S(2)}, u32[]{:S(2)}) collective-permute-start(bf16[128,1024]{1,0:T(8,128)(2,1)} %get-tuple-element.41), channel_id=1, source_target_pairs={{0,16},{16,0},{1,17},{17,1},{2,18},{18,2},{3,19},{19,3},{4,20},{20... | collective-permute-start | bytes 786440 | tf_op jit(solution)/shard_map/ppermute | solution.py:389
  104.5 15.1 %copy-start.8 = (bf16[1024,256]{1,0:T(8,128)(2,1)S(1)}, bf16[1024,256]{1,0:T(8,128)(2,1)}, u32[]{:S(2)}) copy-start(bf16[1024,256]{1,0:T(8,128)(2,1)} %get-tuple-element.54) | copy-start | bytes 1572868
  104.5 23.5 %copy-start.6 = (bf16[1024,256]{1,0:T(8,128)(2,1)S(1)}, bf16[1024,256]{1,0:T(8,128)(2,1)}, u32[]{:S(2)}) copy-start(bf16[1024,256]{1,0:T(8,128)(2,1)} %get-tuple-element.53) | copy-start | bytes 1572868
  117.9 37.0 %collective-permute-start.10 = (bf16[1024,256]{1,0:T(8,128)(2,1)}, bf16[1024,256]{1,0:T(8,128)(2,1)S(1)}, u32[]{:S(2)}, u32[]{:S(2)}) collective-permute-start(bf16[1024,256]{1,0:T(8,128)(2,1)} %get-tuple-element.55), channel_id=1, source_target_pairs={{0,12},{4,0},{8,4},{12,8},{1,13},{5,1},{9,5},{13,9},{2,14},{6,2},{... | collective-permute-start | bytes 1572872 | tf_op jit(solution)/shard_map/ppermute | solution.py:386
  119.6 35.3 %collective-permute-start.9 = (bf16[1024,256]{1,0:T(8,128)(2,1)S(1)}, bf16[1024,256]{1,0:T(8,128)(2,1)S(1)}, u32[]{:S(2)}, u32[]{:S(2)}) collective-permute-start(bf16[1024,256]{1,0:T(8,128)(2,1)S(1)} %copy-done.8), channel_id=1, source_target_pairs={{0,4},{4,8},{8,12},{12,0},{1,5},{5,9},{9,13},{13,1},{2,6},{6,10},{... | collective-permute-start | bytes 1572872 | tf_op jit(solution)/shard_map/ppermute | solution.py:386
  128.1 34.2 %collective-permute-start.8 = (bf16[1024,256]{1,0:T(8,128)(2,1)S(1)}, bf16[1024,256]{1,0:T(8,128)(2,1)S(1)}, u32[]{:S(2)}, u32[]{:S(2)}) collective-permute-start(bf16[1024,256]{1,0:T(8,128)(2,1)S(1)} %copy-done.6), channel_id=1, source_target_pairs={{0,8},{4,12},{8,0},{12,4},{1,9},{5,13},{9,1},{13,5},{2,10},{6,14},... | collective-permute-start | bytes 1572872 | tf_op jit(solution)/shard_map/ppermute | solution.py:386
  131.8 16.2 %copy-start = (bf16[128,1024]{1,0:T(8,128)(2,1)S(1)}, bf16[128,1024]{1,0:T(8,128)(2,1)}, u32[]{:S(2)}) copy-start(bf16[128,1024]{1,0:T(8,128)(2,1)} %get-tuple-element.40) | copy-start | bytes 786436
  146.5 6.6 %collective-permute-start.7 = (bf16[128,1024]{1,0:T(8,128)(2,1)}, bf16[128,1024]{1,0:T(8,128)(2,1)S(1)}, u32[]{:S(2)}, u32[]{:S(2)}) collective-permute-start(bf16[128,1024]{1,0:T(8,128)(2,1)} %get-tuple-element.52), channel_id=1, source_target_pairs={{0,16},{16,0},{1,17},{17,1},{2,18},{18,2},{3,19},{19,3},{4,20},{20... | collective-permute-start | bytes 786440 | tf_op jit(solution)/shard_map/ppermute | solution.py:389

commit v3 on v2

--- a/solution.py
+++ b/solution.py
@@ -8,12 +8,13 @@
 from jax.experimental.pallas import tpu as pltpu
 from jax.sharding import PartitionSpec as P
 
+
 HD = 64
 EPS = 1e-06
 LOG2E = math.log2(math.e)
 SCALE = HD ** (-0.5)
 KEY_ROWS = 256
-VMEM_BYTES = 60 << 20
+VMEM_BYTES = 14 << 20
 NT = (((1,), (1,)), ((), ()))
 
 bf16 = jnp.bfloat16
@@ -46,7 +47,7 @@
         ],
         out_specs=pl.BlockSpec((groups, block, 2 * HD), lambda i: (0, i, 0)),
         out_shape=jax.ShapeDtypeStruct((groups, rows, 2 * HD), bf16),
-        compiler_params=pltpu.CompilerParams(vmem_limit_bytes=VMEM_BYTES),
+        compiler_params=pltpu.CompilerParams(vmem_limit_bytes=60 << 20),
         cost_estimate=pl.CostEstimate(
             flops=2 * rows * width * weight.shape[1], bytes_accessed=2 * rows * width, transcendentals=0
         ),
@@ -82,14 +83,26 @@
     )(*blocks)
 
 
-def forward_kernel(dims, first, last, *refs):
+def gathered(piece_refs, whole_ref):
+    if len(piece_refs) == 1:
+        return piece_refs[0]
+    begin = 0
+    for piece in piece_refs:
+        rows = piece.shape[1]
+        whole_ref[:, begin : begin + rows] = piece[...]
+        begin += rows
+    return whole_ref
+
+
+def forward_kernel(dims, pieces, first, last, *refs):
     chunks, groups, per_group = dims
     refs = list(refs)
     q_ref = refs.pop(0)
     c_ref = refs.pop(0) if last else None
-    kv_ref = refs.pop(0)
+    piece_refs = [refs.pop(0) for _ in range(pieces)]
     past, past_acc = (None, None) if first else (refs.pop(0), refs.pop(0))
-    e_hbm, top_ref, st_ref, acc_ref, value_t, scores, expo, sem = refs
+    e_hbm, top_ref, st_ref, acc_ref, whole_ref, value_t, scores, expo, sem = refs
+    kv_ref = gathered(piece_refs, whole_ref)
     length = kv_ref.shape[1]
     lanes = q_ref.shape[2]
     pad = jnp.zeros((HD, lanes), bf16)
@@ -165,14 +178,14 @@
 
 
 def forward(dims, q_rows, c_rows, pairs, before):
-    chunks, groups, per_group = dims
+    chunks, groups, _ = dims
     lanes = q_rows.shape[2]
-    length = pairs.shape[1]
+    length = sum(p.shape[1] for p in pairs)
     first, last = before is None, c_rows is not None
-    args = [q_rows] + ([c_rows] if last else []) + [pairs] + ([] if first else list(before))
+    args = [q_rows] + ([c_rows] if last else []) + pairs + ([] if first else list(before))
     size = chunks * lanes * length
     return pl.pallas_call(
-        functools.partial(forward_kernel, dims, first, last),
+        functools.partial(forward_kernel, dims, len(pairs), first, last),
         in_specs=[IN_VMEM] * len(args),
         out_specs=[IN_PLACE, IN_VMEM, IN_VMEM, IN_VMEM],
         out_shape=[
@@ -182,6 +195,7 @@
             jax.ShapeDtypeStruct((chunks, HD, lanes), f32),
         ],
         scratch_shapes=[
+            pltpu.VMEM((groups, length, 2 * HD), bf16),
             pltpu.VMEM((groups, HD + 16, length), bf16),
             pltpu.VMEM((length, lanes), f32),
             pltpu.VMEM((2, length, lanes), bf16),
@@ -199,10 +213,12 @@
     return rows if shift == 0 else jnp.concatenate([rows[count - shift :], rows[: count - shift]], axis=0)
 
 
-def backward_kernel(dims, peers, first, last, *refs):
+def backward_kernel(dims, pieces, peers, first, last, *refs):
     chunks, groups, per_group = dims
     refs = list(refs)
-    q_ref, c_ref, kv_ref, e_hbm, top_ref, own_ref = [refs.pop(0) for _ in range(6)]
+    q_ref, c_ref = refs.pop(0), refs.pop(0)
+    piece_refs = [refs.pop(0) for _ in range(pieces)]
+    e_hbm, top_ref, own_ref = [refs.pop(0) for _ in range(3)]
     peer_refs = [refs.pop(0) for _ in range(peers)]
     acc_ref = refs.pop(0) if first else None
     past_dq = None if first else refs.pop(0)
@@ -210,11 +226,12 @@
     ctx_outs = [refs.pop(0) for _ in range(blocks)] if first else None
     dq_outs = [refs.pop(0) for _ in range(blocks)] if last else [refs.pop(0)]
     dkv_ref = refs.pop(0)
-    key_t, expo, score_grad, key_sum, value_sum, factor, delta, rows, sem, row_sem = refs
+    whole_ref, key_t, expo, score_grad, key_sum, value_sum, factor, delta, rows, sem, row_sem = refs
+    kv_ref = gathered(piece_refs, whole_ref)
     length = kv_ref.shape[1]
     lanes = q_ref.shape[2]
     steps = length // KEY_ROWS
-    heads = per_block_heads = lanes // rows.shape[1]
+    heads = lanes // rows.shape[1]
     per_block = chunks // blocks
     pad = jnp.zeros((HD, lanes), bf16)
 
@@ -323,14 +340,15 @@
 
 
 def backward(dims, q_rows, c_rows, pairs, expo, top, own, peers, acc, past_dq, last, tokens):
-    chunks, groups, per_group = dims
+    chunks, groups, _ = dims
     lanes = q_rows.shape[2]
-    length = pairs.shape[1]
+    length = sum(p.shape[1] for p in pairs)
     first = past_dq is None
     blocks = len(peers) + 1
     width = chunks // blocks * (lanes // tokens) * HD
-    args = [q_rows, c_rows, pairs, expo, top, own, *peers] + [acc if first else past_dq]
-    specs = [IN_VMEM] * 3 + [IN_PLACE] + [IN_VMEM] * (len(args) - 4)
+    args = [q_rows, c_rows, *pairs, expo, top, own, *peers] + [acc if first else past_dq]
+    specs = [IN_VMEM] * len(args)
+    specs[2 + len(pairs)] = IN_PLACE
     row_block = jax.ShapeDtypeStruct((tokens, width), bf16)
     outs, out_specs = [], []
     if first:
@@ -347,11 +365,12 @@
     size = chunks * lanes * length
     results = list(
         pl.pallas_call(
-            functools.partial(backward_kernel, dims, len(peers), first, last),
+            functools.partial(backward_kernel, dims, len(pairs), len(peers), first, last),
             in_specs=specs,
             out_specs=out_specs,
             out_shape=outs,
             scratch_shapes=[
+                pltpu.VMEM((groups, length, 2 * HD), bf16),
                 pltpu.VMEM((groups, HD, length), bf16),
                 pltpu.VMEM((2, length, lanes), bf16),
                 pltpu.VMEM((length, lanes), bf16),
@@ -392,7 +411,14 @@
     c_blocks = [cotangent] + [from_half(cotangent, s) for s in range(1, halves)]
     own_pairs = project(enc_states, norm_gain, kv_weight)
     order = sorted(range(seqs), key=lambda s: min(s, seqs - s))
-    pair_blocks = [own_pairs] + [from_seq(own_pairs, s) for s in order[1:]]
+    pair_blocks = [[own_pairs]]
+    for s in order[1:]:
+        if seqs > 2 and 2 * s == seqs:
+            low, high = pair_blocks[order.index(s - 1)][0], pair_blocks[order.index(s + 1)][0]
+            middle = low.shape[1] // 2
+            pair_blocks.append([from_seq(low[:, :middle], 1), from_seq(high[:, middle:], -1)])
+        else:
+            pair_blocks.append([from_seq(own_pairs, s)])
     q_rows = turn(q_blocks, heads)
     c_rows = turn(c_blocks, heads)
 
@@ -426,8 +452,12 @@
 def solution(mesh):
     shape = mesh.shape
     rows, columns = P(("half", "seq"), None), P(("half", "seq"), "head")
+
+    def body(*args):
+        return on_device(shape["half"], shape["seq"], *args)
+
     return jax.shard_map(
-        functools.partial(on_device, shape["half"], shape["seq"]),
+        body,
         mesh=mesh,
         in_specs=(rows, P(), P(None, "head"), columns, columns),
         out_specs=(columns, columns, columns),

time: 166 us -> 139 us (0.84)
  Pallas kernels: 106 us -> 70.5 us
  waiting for transfers between devices: 23.7 us -> 43.6 us
  starting transfers between devices: 24.8 us -> 19.9 us
  local copies, waits for them, and re-layouts: 4.44 us -> 1.09 us
  other arithmetic: 4.73 us -> 2.58 us
    pallas_call x8, Pallas kernels: 93.7 us -> 61.9 us  [the longest x4 38.9 us: backward(): pl.pallas_call(functools.partial(backward_kernel, dims, len(pairs), len(p...]
    ppermute x6 -> x7, waiting for transfers between devices: 15.6 us -> 35.9 us  [from_seq(): lax.ppermute(x, 'seq', [(i, (i + shift) % seqs) for i in range(seqs)])]
    ppermute x6 -> x7, starting transfers between devices: 18.5 us -> 13.1 us  [from_seq(): lax.ppermute(x, 'seq', [(i, (i + shift) % seqs) for i in range(seqs)])]
    pallas_call x2, Pallas kernels: 4.02 us -> 0.36 us  [turn(): pl.pallas_call(functools.partial(turn_kernel, len(blocks)), in_specs=[IN_...]
    unnamed x20 -> x8, local copies, waits for them, and re-layouts: 4.44 us -> 1.05 us
  transfers between devices with their start and end apart: 11 -> 12, of which waited for: 4 -> 7; matrix products, arithmetic and copies ran while one was open for 2% -> 1% of each run, Pallas kernels for 50% -> 39%
where the time goes in v3:
time: 139 us; the launch traced here: 138 us
  Pallas kernels  70.5 us (51%)
  waiting for transfers between devices  43.6 us (31%)
  starting transfers between devices  19.9 us (14%)
  other arithmetic  2.58 us (2%)
    pallas_call x4, Pallas kernels, backward(): pl.pallas_call(functools.partial(backward_kernel, dims, len(pairs), len(p...  38.9 us
    ppermute x7, waiting for transfers between devices, from_seq(): lax.ppermute(x, 'seq', [(i, (i + shift) % seqs) for i in range(seqs)])  35.9 us
    pallas_call x4, Pallas kernels, forward(): pl.pallas_call(functools.partial(forward_kernel, dims, len(pairs), first,...  23 us
    ppermute x7, starting transfers between devices, from_seq(): lax.ppermute(x, 'seq', [(i, (i + shift) % seqs) for i in range(seqs)])  13.1 us
    pallas_call x1, Pallas kernels, project(): pl.pallas_call(project_kernel, grid=(rows // block,), in_specs=[pl.BlockS...  8.24 us
    ppermute x5, waiting for transfers between devices, from_half(): lax.ppermute(x, 'half', [(i, (i + shift) % halves) for i in range(halves)])  7.67 us
    ppermute x5, starting transfers between devices, from_half(): lax.ppermute(x, 'half', [(i, (i + shift) % halves) for i in range(halves)])  6.82 us
  transfers between devices with their start and end apart: 12, of which 7 were waited for; matrix products, arithmetic and copies ran while one was open for 1% of the time, Pallas kernels for 39%

profile of v3, /device:TPU:0, one launch (start us, length us, event | category | flops | bytes accessed | tf_op | source)
XLA Modules:
  0.0 138.4 jit_solution(3517108364533869883)
XLA Ops:
  0.7 3.0 %collective-permute-start = (bf16[128,1024]{1,0:T(8,128)(2,1)}, bf16[128,1024]{1,0:T(8,128)(2,1)S(1)}, u32[]{:S(2)}, u32[]{:S(2)}) collective-permute-start(bf16[128,1024]{1,0:T(8,128)(2,1)} %refs_0_.2), channel_id=1, source_target_pairs={{0,16},{16,0},{1,17},{17,1},{2,18},{18,2},{3,19},{19,3},{4,20},{20... | collective-permute-start | bytes 786440 | tf_op jit(solution)/shard_map/ppermute | solution.py:408
  3.8 8.2 %project.1.refs_1_.refs_2_ = bf16[2,1024,128]{2,1,0:T(8,128)(2,1)} custom-call(bf16[1024,4096]{1,0:T(8,128)(2,1)} %x_ref.1, f32[1,4096]{1,0:T(1,128)} %bitcast.1, bf16[4096,256]{1,0:T(8,128)(2,1)} %w_ref.1), custom_call_target="tpu_custom_call" | custom-call | flops 2147483648 | bytes 8388608 | tf_op jit(solution)/shard_map/project/pallas_call | solution.py:40
  12.0 4.1 %collective-permute-start.4 = (bf16[2,1024,128]{2,1,0:T(8,128)(2,1)}, bf16[2,1024,128]{2,1,0:T(8,128)(2,1)S(1)}, u32[]{:S(2)}, u32[]{:S(2)}) collective-permute-start(bf16[2,1024,128]{2,1,0:T(8,128)(2,1)} %project.1.refs_1_.refs_2_), channel_id=1, source_target_pairs={{0,12},{4,0},{8,4},{12,8},{1,13},{5,1},{9,5},{13,9},{2,14},{6,2},{... | collective-permute-start | bytes 1572872 | tf_op jit(solution)/shard_map/ppermute | solution.py:405
  16.5 1.0 copy-done
  17.5 5.5 %forward.4 = (bf16[8,1024,512]{2,1,0:T(8,128)(2,1)S(1)}, f32[8,512]{1,0:T(8,128)S(1)}, f32[2,8,512]{2,1,0:T(8,128)S(1)}, f32[8,64,512]{2,1,0:T(8,128)S(1)}) custom-call(bf16[8,64,512]{2,1,0:T(8,128)(2,1)S(1)} %turn.2.refs_0_, bf16[2,1024,128]{2,1,0:T(8,128)(2,1)S(1)} %copy-done), custom_call_target="tpu_custom_call" | custom-call | flops 4294967296 | bytes 8388608 | tf_op jit(solution)/shard_map/forward/pallas_call | solution.py:187
  23.1 5.6 %collective-permute-done.4.refs_1_.refs_2_ = bf16[2,1024,128]{2,1,0:T(8,128)(2,1)S(1)} collective-permute-done((bf16[2,1024,128]{2,1,0:T(8,128)(2,1)}, bf16[2,1024,128]{2,1,0:T(8,128)(2,1)S(1)}, u32[]{:S(2)}, u32[]{:S(2)}) %collective-permute-start.4) | collective-permute-done | bytes 524320 | tf_op jit(solution)/shard_map/ppermute | solution.py:405
  28.7 4.2 %collective-permute-start.5 = (bf16[2,512,128]{2,1,0:T(8,128)(2,1)S(1)}, bf16[2,512,128]{2,1,0:T(8,128)(2,1)S(1)}, u32[]{:S(2)}, u32[]{:S(2)}) collective-permute-start(bf16[2,512,128]{2,1,0:T(8,128)(2,1)S(1)} %slice.9), channel_id=1, source_target_pairs={{0,12},{4,0},{8,4},{12,8},{1,13},{5,1},{9,5},{13,9},{2,14},{6,2},{... | collective-permute-start | bytes 786440 | tf_op jit(solution)/shard_map/ppermute | solution.py:405
  33.0 7.8 %collective-permute-done.2.refs_1_.refs_2_ = bf16[2,1024,128]{2,1,0:T(8,128)(2,1)S(1)} collective-permute-done((bf16[2,1024,128]{2,1,0:T(8,128)(2,1)}, bf16[2,1024,128]{2,1,0:T(8,128)(2,1)S(1)}, u32[]{:S(2)}, u32[]{:S(2)}) %collective-permute-start.2) | collective-permute-done | bytes 524320 | tf_op jit(solution)/shard_map/ppermute | solution.py:405
  40.8 1.8 %collective-permute-start.3 = (bf16[2,512,128]{2,1,0:T(8,128)(2,1)S(1)}, bf16[2,512,128]{2,1,0:T(8,128)(2,1)S(1)}, u32[]{:S(2)}, u32[]{:S(2)}) collective-permute-start(bf16[2,512,128]{2,1,0:T(8,128)(2,1)S(1)} %slice.8), channel_id=1, source_target_pairs={{0,4},{4,8},{8,12},{12,0},{1,5},{5,9},{9,13},{13,1},{2,6},{6,10},{... | collective-permute-start | bytes 786440 | tf_op jit(solution)/shard_map/ppermute | solution.py:405
  42.6 5.8 %forward.5 = (bf16[8,1024,512]{2,1,0:T(8,128)(2,1)S(1)}, f32[8,512]{1,0:T(8,128)S(1)}, f32[2,8,512]{2,1,0:T(8,128)S(1)}, f32[8,64,512]{2,1,0:T(8,128)S(1)}) custom-call(bf16[8,64,512]{2,1,0:T(8,128)(2,1)S(1)} %turn.2.refs_0_, bf16[2,1024,128]{2,1,0:T(8,128)(2,1)S(1)} %collective-permute-done.2.refs_1_.refs_2_, f32[2,8,512]{2,1,0:T(8,128)S(1)} %get-tuple-element.30.refs_2_, ...), custom_call_target="tpu_custom_call" | custom-call | flops 4294967296 | bytes 8388608 | tf_op jit(solution)/shard_map/forward/pallas_call | solution.py:187
  48.3 5.8 %forward.6 = (bf16[8,1024,512]{2,1,0:T(8,128)(2,1)S(1)}, f32[8,512]{1,0:T(8,128)S(1)}, f32[2,8,512]{2,1,0:T(8,128)S(1)}, f32[8,64,512]{2,1,0:T(8,128)S(1)}) custom-call(bf16[8,64,512]{2,1,0:T(8,128)(2,1)S(1)} %turn.2.refs_0_, bf16[2,1024,128]{2,1,0:T(8,128)(2,1)S(1)} %collective-permute-done.4.refs_1_.refs_2_, f32[2,8,512]{2,1,0:T(8,128)S(1)} %get-tuple-element.32.refs_2_, ...), custom_call_target="tpu_custom_call" | custom-call | flops 4294967296 | bytes 8388608 | tf_op jit(solution)/shard_map/forward/pallas_call | solution.py:187
  54.2 5.9 %forward.7 = (bf16[8,1024,512]{2,1,0:T(8,128)(2,1)S(1)}, f32[8,512]{1,0:T(8,128)S(1)}, f32[3,8,512]{2,1,0:T(8,128)S(1)}, f32[8,64,512]{2,1,0:T(8,128)S(1)}) custom-call(bf16[8,64,512]{2,1,0:T(8,128)(2,1)S(1)} %turn.2.refs_0_, bf16[8,64,512]{2,1,0:T(8,128)(2,1)S(1)} %turn.3.refs_1_, bf16[2,512,128]{2,1,0:T(8,128)(2,1)S(1)} %collective-permute-done.3.refs_2_, ...), custom_call_target="tpu_custom_call" | custom-call | flops 4294967296 | bytes 8388608 | tf_op jit(solution)/shard_map/forward/pallas_call | solution.py:187
  60.1 1.6 %collective-permute-start.6 = (f32[3,8,512]{2,1,0:T(8,128)S(1)}, f32[3,8,512]{2,1,0:T(8,128)S(1)}, u32[]{:S(2)}, u32[]{:S(2)}) collective-permute-start(f32[3,8,512]{2,1,0:T(8,128)S(1)} %get-tuple-element.38.refs_6_.refs_5_), channel_id=1, source_target_pairs={{0,16},{16,0},{1,17},{17,1},{2,18},{18,2},{3,19},{19,3},{4,20},{20... | collective-permute-start | bytes 147464 | tf_op jit(solution)/shard_map/ppermute | solution.py:408
  61.6 2.6 %collective-permute-done.6.refs_7_.refs_6_ = f32[3,8,512]{2,1,0:T(8,128)S(1)} collective-permute-done((f32[3,8,512]{2,1,0:T(8,128)S(1)}, f32[3,8,512]{2,1,0:T(8,128)S(1)}, u32[]{:S(2)}, u32[]{:S(2)}) %collective-permute-start.6) | collective-permute-done | bytes 49184 | tf_op jit(solution)/shard_map/ppermute | solution.py:408
  64.2 10.3 %backward.4 = (bf16[128,1024]{1,0:T(8,128)(2,1)S(1)}, bf16[128,1024]{1,0:T(8,128)(2,1)S(1)}, f32[8,64,512]{2,1,0:T(8,128)S(1)}, bf16[1024,256]{1,0:T(8,128)(2,1)S(1)}) custom-call(bf16[8,64,512]{2,1,0:T(8,128)(2,1)S(1)} %turn.2.refs_0_, bf16[8,64,512]{2,1,0:T(8,128)(2,1)S(1)} %turn.3.refs_1_, bf16[2,512,128]{2,1,0:T(8,128)(2,1)S(1)} %collective-permute-done.3.refs_2_, ...), custom_call_target="tpu_custom_call" | custom-call | flops 6442450944 | bytes 8388608 | tf_op jit(solution)/shard_map/backward/pallas_call | solution.py:367
  74.5 1.6 %collective-permute-start.7 = (bf16[128,1024]{1,0:T(8,128)(2,1)S(1)}, bf16[128,1024]{1,0:T(8,128)(2,1)S(1)}, u32[]{:S(2)}, u32[]{:S(2)}) collective-permute-start(bf16[128,1024]{1,0:T(8,128)(2,1)S(1)} %get-tuple-element.41), channel_id=1, source_target_pairs={{0,16},{16,0},{1,17},{17,1},{2,18},{18,2},{3,19},{19,3},{4,20},{20... | collective-permute-start | bytes 786440 | tf_op jit(solution)/shard_map/ppermute | solution.py:408
  76.1 9.4 %backward.5 = (f32[8,64,512]{2,1,0:T(8,128)S(1)}, bf16[1024,256]{1,0:T(8,128)(2,1)S(1)}) custom-call(bf16[8,64,512]{2,1,0:T(8,128)(2,1)S(1)} %turn.2.refs_0_, bf16[8,64,512]{2,1,0:T(8,128)(2,1)S(1)} %turn.3.refs_1_, bf16[2,1024,128]{2,1,0:T(8,128)(2,1)S(1)} %collective-permute-done.4.refs_1_.refs_2_, bf16[8,1024,512]{2,1,0:T(8,128)(2,1)S(1)} %get-tuple-element.46.refs_3_, ...), custom_call_target="tpu_custom_call" | custom-call | flops 6442450944 | bytes 8388608 | tf_op jit(solution)/shard_map/backward/pallas_call | solution.py:367
  85.5 9.4 %backward.6 = (f32[8,64,512]{2,1,0:T(8,128)S(1)}, bf16[1024,256]{1,0:T(8,128)(2,1)S(1)}) custom-call(bf16[8,64,512]{2,1,0:T(8,128)(2,1)S(1)} %turn.2.refs_0_, bf16[8,64,512]{2,1,0:T(8,128)(2,1)S(1)} %turn.3.refs_1_, bf16[2,1024,128]{2,1,0:T(8,128)(2,1)S(1)} %collective-permute-done.2.refs_1_.refs_2_, bf16[8,1024,512]{2,1,0:T(8,128)(2,1)S(1)} %get-tuple-element.44.refs_3_, ...), custom_call_target="tpu_custom_call" | custom-call | flops 6442450944 | bytes 8388608 | tf_op jit(solution)/shard_map/backward/pallas_call | solution.py:367
  94.9 2.3 %collective-permute-start.11 = (bf16[1024,256]{1,0:T(8,128)(2,1)S(1)}, bf16[1024,256]{1,0:T(8,128)(2,1)S(1)}, u32[]{:S(2)}, u32[]{:S(2)}) collective-permute-start(bf16[1024,256]{1,0:T(8,128)(2,1)S(1)} %get-tuple-element.55), channel_id=1, source_target_pairs={{0,12},{4,0},{8,4},{12,8},{1,13},{5,1},{9,5},{13,9},{2,14},{6,2},{... | collective-permute-start | bytes 1572872 | tf_op jit(solution)/shard_map/ppermute | solution.py:405
  97.9 9.8 %backward.7 = (bf16[128,1024]{1,0:T(8,128)(2,1)S(1)}, bf16[128,1024]{1,0:T(8,128)(2,1)S(1)}, f32[1024,256]{1,0:T(8,128)S(1)}) custom-call(bf16[8,64,512]{2,1,0:T(8,128)(2,1)S(1)} %turn.2.refs_0_, bf16[8,64,512]{2,1,0:T(8,128)(2,1)S(1)} %turn.3.refs_1_, bf16[2,1024,128]{2,1,0:T(8,128)(2,1)S(1)} %copy-done.1, ...), custom_call_target="tpu_custom_call" | custom-call | flops 6442450944 | bytes 8388608 | tf_op jit(solution)/shard_map/backward/pallas_call | solution.py:367
  109.0 5.1 %collective-permute-done.8 = bf16[128,1024]{1,0:T(8,128)(2,1)S(1)} collective-permute-done((bf16[128,1024]{1,0:T(8,128)(2,1)S(1)}, bf16[128,1024]{1,0:T(8,128)(2,1)S(1)}, u32[]{:S(2)}, u32[]{:S(2)}) %collective-permute-start.8) | collective-permute-done | bytes 262176 | tf_op jit(solution)/shard_map/ppermute | solution.py:408
  115.3 5.9 %collective-permute-done.10 = bf16[1024,256]{1,0:T(8,128)(2,1)S(1)} collective-permute-done((bf16[1024,256]{1,0:T(8,128)(2,1)S(1)}, bf16[1024,256]{1,0:T(8,128)(2,1)S(1)}, u32[]{:S(2)}, u32[]{:S(2)}) %collective-permute-start.10) | collective-permute-done | bytes 524320 | tf_op jit(solution)/shard_map/ppermute | solution.py:405
  121.2 16.1 %collective-permute-done.9 = bf16[1024,256]{1,0:T(8,128)(2,1)S(1)} collective-permute-done((bf16[1024,256]{1,0:T(8,128)(2,1)S(1)}, bf16[1024,256]{1,0:T(8,128)(2,1)S(1)}, u32[]{:S(2)}, u32[]{:S(2)}) %collective-permute-start.9) | collective-permute-done | bytes 524320 | tf_op jit(solution)/shard_map/ppermute | solution.py:405
  137.3 1.0 add_convert_fusion
  (24 shorter events, 3.7 us)
Async XLA Ops:
  0.6 15.5 %copy-start.2 = (bf16[128,1024]{1,0:T(8,128)(2,1)S(1)}, bf16[128,1024]{1,0:T(8,128)(2,1)}, u32[]{:S(2)}) copy-start(bf16[128,1024]{1,0:T(8,128)(2,1)} %refs_0_.2) | copy-start | bytes 786436
  0.6 15.6 %copy-start.3 = (bf16[128,1024]{1,0:T(8,128)(2,1)S(1)}, bf16[128,1024]{1,0:T(8,128)(2,1)}, u32[]{:S(2)}) copy-start(bf16[128,1024]{1,0:T(8,128)(2,1)} %refs_0_.3) | copy-start | bytes 786436
  0.7 15.4 %collective-permute-start = (bf16[128,1024]{1,0:T(8,128)(2,1)}, bf16[128,1024]{1,0:T(8,128)(2,1)S(1)}, u32[]{:S(2)}, u32[]{:S(2)}) collective-permute-start(bf16[128,1024]{1,0:T(8,128)(2,1)} %refs_0_.2), channel_id=1, source_target_pairs={{0,16},{16,0},{1,17},{17,1},{2,18},{18,2},{3,19},{19,3},{4,20},{20... | collective-permute-start | bytes 786440 | tf_op jit(solution)/shard_map/ppermute | solution.py:408
  3.7 12.6 %collective-permute-start.1 = (bf16[128,1024]{1,0:T(8,128)(2,1)}, bf16[128,1024]{1,0:T(8,128)(2,1)S(1)}, u32[]{:S(2)}, u32[]{:S(2)}) collective-permute-start(bf16[128,1024]{1,0:T(8,128)(2,1)} %refs_0_.3), channel_id=1, source_target_pairs={{0,16},{16,0},{1,17},{17,1},{2,18},{18,2},{3,19},{19,3},{4,20},{20... | collective-permute-start | bytes 786440 | tf_op jit(solution)/shard_map/ppermute | solution.py:408
  12.0 16.7 %collective-permute-start.4 = (bf16[2,1024,128]{2,1,0:T(8,128)(2,1)}, bf16[2,1024,128]{2,1,0:T(8,128)(2,1)S(1)}, u32[]{:S(2)}, u32[]{:S(2)}) collective-permute-start(bf16[2,1024,128]{2,1,0:T(8,128)(2,1)} %project.1.refs_1_.refs_2_), channel_id=1, source_target_pairs={{0,12},{4,0},{8,4},{12,8},{1,13},{5,1},{9,5},{13,9},{2,14},{6,2},{... | collective-permute-start | bytes 1572872 | tf_op jit(solution)/shard_map/ppermute | solution.py:405
  16.1 24.7 %collective-permute-start.2 = (bf16[2,1024,128]{2,1,0:T(8,128)(2,1)}, bf16[2,1024,128]{2,1,0:T(8,128)(2,1)S(1)}, u32[]{:S(2)}, u32[]{:S(2)}) collective-permute-start(bf16[2,1024,128]{2,1,0:T(8,128)(2,1)} %project.1.refs_1_.refs_2_), channel_id=1, source_target_pairs={{0,4},{4,8},{8,12},{12,0},{1,5},{5,9},{9,13},{13,1},{2,6},{6,10},{... | collective-permute-start | bytes 1572872 | tf_op jit(solution)/shard_map/ppermute | solution.py:405
  16.5 1.0 copy-start
  28.7 25.4 %collective-permute-start.5 = (bf16[2,512,128]{2,1,0:T(8,128)(2,1)S(1)}, bf16[2,512,128]{2,1,0:T(8,128)(2,1)S(1)}, u32[]{:S(2)}, u32[]{:S(2)}) collective-permute-start(bf16[2,512,128]{2,1,0:T(8,128)(2,1)S(1)} %slice.9), channel_id=1, source_target_pairs={{0,12},{4,0},{8,4},{12,8},{1,13},{5,1},{9,5},{13,9},{2,14},{6,2},{... | collective-permute-start | bytes 786440 | tf_op jit(solution)/shard_map/ppermute | solution.py:405
  40.8 13.4 %collective-permute-start.3 = (bf16[2,512,128]{2,1,0:T(8,128)(2,1)S(1)}, bf16[2,512,128]{2,1,0:T(8,128)(2,1)S(1)}, u32[]{:S(2)}, u32[]{:S(2)}) collective-permute-start(bf16[2,512,128]{2,1,0:T(8,128)(2,1)S(1)} %slice.8), channel_id=1, source_target_pairs={{0,4},{4,8},{8,12},{12,0},{1,5},{5,9},{9,13},{13,1},{2,6},{6,10},{... | collective-permute-start | bytes 786440 | tf_op jit(solution)/shard_map/ppermute | solution.py:405
  60.1 4.2 %collective-permute-start.6 = (f32[3,8,512]{2,1,0:T(8,128)S(1)}, f32[3,8,512]{2,1,0:T(8,128)S(1)}, u32[]{:S(2)}, u32[]{:S(2)}) collective-permute-start(f32[3,8,512]{2,1,0:T(8,128)S(1)} %get-tuple-element.38.refs_6_.refs_5_), channel_id=1, source_target_pairs={{0,16},{16,0},{1,17},{17,1},{2,18},{18,2},{3,19},{19,3},{4,20},{20... | collective-permute-start | bytes 147464 | tf_op jit(solution)/shard_map/ppermute | solution.py:408
  74.5 33.8 %collective-permute-start.7 = (bf16[128,1024]{1,0:T(8,128)(2,1)S(1)}, bf16[128,1024]{1,0:T(8,128)(2,1)S(1)}, u32[]{:S(2)}, u32[]{:S(2)}) collective-permute-start(bf16[128,1024]{1,0:T(8,128)(2,1)S(1)} %get-tuple-element.41), channel_id=1, source_target_pairs={{0,16},{16,0},{1,17},{17,1},{2,18},{18,2},{3,19},{19,3},{4,20},{20... | collective-permute-start | bytes 786440 | tf_op jit(solution)/shard_map/ppermute | solution.py:408
  85.5 12.4 %copy-start.1 = (bf16[2,1024,128]{2,1,0:T(8,128)(2,1)S(1)}, bf16[2,1024,128]{2,1,0:T(8,128)(2,1)}, u32[]{:S(2)}) copy-start(bf16[2,1024,128]{2,1,0:T(8,128)(2,1)} %project.1.refs_1_.refs_2_) | copy-start | bytes 1572868
  94.9 20.4 %collective-permute-start.11 = (bf16[1024,256]{1,0:T(8,128)(2,1)S(1)}, bf16[1024,256]{1,0:T(8,128)(2,1)S(1)}, u32[]{:S(2)}, u32[]{:S(2)}) collective-permute-start(bf16[1024,256]{1,0:T(8,128)(2,1)S(1)} %get-tuple-element.55), channel_id=1, source_target_pairs={{0,12},{4,0},{8,4},{12,8},{1,13},{5,1},{9,5},{13,9},{2,14},{6,2},{... | collective-permute-start | bytes 1572872 | tf_op jit(solution)/shard_map/ppermute | solution.py:405
  97.3 24.0 %collective-permute-start.10 = (bf16[1024,256]{1,0:T(8,128)(2,1)S(1)}, bf16[1024,256]{1,0:T(8,128)(2,1)S(1)}, u32[]{:S(2)}, u32[]{:S(2)}) collective-permute-start(bf16[1024,256]{1,0:T(8,128)(2,1)S(1)} %get-tuple-element.54), channel_id=1, source_target_pairs={{0,4},{4,8},{8,12},{12,0},{1,5},{5,9},{9,13},{13,1},{2,6},{6,10},{... | collective-permute-start | bytes 1572872 | tf_op jit(solution)/shard_map/ppermute | solution.py:405
  97.3 40.1 %collective-permute-start.9 = (bf16[1024,256]{1,0:T(8,128)(2,1)S(1)}, bf16[1024,256]{1,0:T(8,128)(2,1)S(1)}, u32[]{:S(2)}, u32[]{:S(2)}) collective-permute-start(bf16[1024,256]{1,0:T(8,128)(2,1)S(1)} %get-tuple-element.53), channel_id=1, source_target_pairs={{0,8},{4,12},{8,0},{12,4},{1,9},{5,13},{9,1},{13,5},{2,10},{6,14},... | collective-permute-start | bytes 1572872 | tf_op jit(solution)/shard_map/ppermute | solution.py:405
  107.7 6.4 %collective-permute-start.8 = (bf16[128,1024]{1,0:T(8,128)(2,1)S(1)}, bf16[128,1024]{1,0:T(8,128)(2,1)S(1)}, u32[]{:S(2)}, u32[]{:S(2)}) collective-permute-start(bf16[128,1024]{1,0:T(8,128)(2,1)S(1)} %get-tuple-element.52), channel_id=1, source_target_pairs={{0,16},{16,0},{1,17},{17,1},{2,18},{18,2},{3,19},{19,3},{4,20},{20... | collective-permute-start | bytes 786440 | tf_op jit(solution)/shard_map/ppermute | solution.py:408

commit v4 on v3

--- a/solution.py
+++ b/solution.py
@@ -398,49 +398,62 @@
     per_group_heads = width // (groups * HD)
     heads = min(per_group_heads, max(1, 512 // tokens))
     per_group = per_group_heads // heads
-    chunks = halves * groups * per_group
+    chunks = seqs // max(1, seqs // 2) * groups * per_group
     dims = (chunks, groups, per_group)
 
-    def from_seq(x, shift):
-        return lax.ppermute(x, "seq", [(i, (i + shift) % seqs) for i in range(seqs)])
-
-    def from_half(x, shift):
-        return lax.ppermute(x, "half", [(i, (i + shift) % halves) for i in range(halves)])
-
-    q_blocks = [queries] + [from_half(queries, s) for s in range(1, halves)]
-    c_blocks = [cotangent] + [from_half(cotangent, s) for s in range(1, halves)]
+    near = max(1, seqs // 2)
+    fars = seqs // near
+
+    def from_far(x, shift):
+        return lax.ppermute(x, "seq", [(i, (i + shift * near) % seqs) for i in range(seqs)])
+
+    def from_near(x, a, b):
+        pairs = []
+        for h in range(halves):
+            for i in range(seqs):
+                to = (h + a) % halves * seqs + i // near * near + (i + b) % near
+                pairs.append((h * seqs + i, to))
+        return lax.ppermute(x, ("half", "seq"), pairs)
+
+    q_blocks = [queries] + [from_far(queries, s) for s in range(1, fars)]
+    late, *_ = lax.optimization_barrier((cotangent, *q_blocks[1:]))
+    c_blocks = [late] + [from_far(late, s) for s in range(1, fars)]
     own_pairs = project(enc_states, norm_gain, kv_weight)
-    order = sorted(range(seqs), key=lambda s: min(s, seqs - s))
-    pair_blocks = [[own_pairs]]
-    for s in order[1:]:
-        if seqs > 2 and 2 * s == seqs:
-            low, high = pair_blocks[order.index(s - 1)][0], pair_blocks[order.index(s + 1)][0]
-            middle = low.shape[1] // 2
-            pair_blocks.append([from_seq(low[:, :middle], 1), from_seq(high[:, middle:], -1)])
+    order = sorted(
+        ((a, b) for a in range(halves) for b in range(near)), key=lambda s: (s != (0, 0), s[0] > 0 and s[1] > 0)
+    )
+    blocks = {(0, 0): [own_pairs]}
+    for a, b in order[1:]:
+        if a and b:
+            across, along = blocks[a, 0][0], blocks[0, b][0]
+            middle = across.shape[1] // 2
+            blocks[a, b] = [from_near(along[:, :middle], a, 0), from_near(across[:, middle:], 0, b)]
         else:
-            pair_blocks.append([from_seq(own_pairs, s)])
+            blocks[a, b] = [from_near(own_pairs, a, b)]
+    pair_blocks = [blocks[s] for s in order]
+    count = len(order)
     q_rows = turn(q_blocks, heads)
     c_rows = turn(c_blocks, heads)
 
     expos, tops, before = [], [], None
     for i, pairs in enumerate(pair_blocks):
-        expo, top, stats, acc = forward(dims, q_rows, c_rows if i == seqs - 1 else None, pairs, before)
+        expo, top, stats, acc = forward(dims, q_rows, c_rows if i == count - 1 else None, pairs, before)
         expos.append(expo)
         tops.append(top)
         before = (stats, acc)
-    peers = [from_half(stats, r) for r in range(1, halves)]
+    peers = [from_far(stats, r) for r in range(1, fars)]
 
     dq, sends, context_parts = None, [], None
-    for i in reversed(range(seqs)):
+    for i in reversed(range(count)):
         parts, dq, dkv = backward(
             dims, q_rows, c_rows, pair_blocks[i], expos[i], tops[i], stats, peers, acc, dq, i == 0, tokens
         )
         if parts is not None:
             context_parts = parts
-        sends.append(dkv if i == 0 else from_seq(dkv, -order[i]))
+        sends.append(dkv if i == 0 else from_near(dkv, -order[i][0], -order[i][1]))
 
     def home(parts):
-        arrived = [parts[0]] + [from_half(parts[s], -s) for s in range(1, halves)]
+        arrived = [parts[0]] + [from_far(parts[s], -s) for s in range(1, fars)]
         return sum(x.astype(f32) for x in arrived).astype(bf16)
 
     context = home(context_parts)

time: 139 us -> 120 us (0.86)
  waiting for transfers between devices: 43.6 us -> 26.9 us
  starting transfers between devices: 19.9 us -> 17.9 us
    ppermute x12, waiting for transfers between devices: 43.6 us -> 26.9 us  [the longest x5 17.2 us: from_far(): lax.ppermute(x, 'seq', [(i, (i + shift * near) % seqs) for i in range(seq...]
    ppermute x12, starting transfers between devices: 19.9 us -> 17.9 us  [the longest x5 9.06 us: from_far(): lax.ppermute(x, 'seq', [(i, (i + shift * near) % seqs) for i in range(seq...]
  transfers between devices with their start and end apart: 12 -> 12, of which waited for: 7 -> 5; matrix products, arithmetic and copies ran while one was open for 1% -> 1% of each run, Pallas kernels for 39% -> 46%
where the time goes in v4:
time: 120 us
  Pallas kernels  70.6 us (59%)
  waiting for transfers between devices  26.9 us (22%)
  starting transfers between devices  17.9 us (15%)
  other arithmetic  2.58 us (2%)
    pallas_call x4, Pallas kernels, backward(): pl.pallas_call(functools.partial(backward_kernel, dims, len(pairs), len(p...  38.8 us
    pallas_call x4, Pallas kernels, forward(): pl.pallas_call(functools.partial(forward_kernel, dims, len(pairs), first,...  23.2 us
    ppermute x5, waiting for transfers between devices, from_far(): lax.ppermute(x, 'seq', [(i, (i + shift * near) % seqs) for i in range(seq...  17.2 us
    ppermute x7, waiting for transfers between devices, from_near(): return lax.ppermute(x, ('half', 'seq'), pairs)  9.76 us
    ppermute x5, starting transfers between devices, from_far(): lax.ppermute(x, 'seq', [(i, (i + shift * near) % seqs) for i in range(seq...  9.06 us
    ppermute x7, starting transfers between devices, from_near(): return lax.ppermute(x, ('half', 'seq'), pairs)  8.87 us
    pallas_call x1, Pallas kernels, project(): pl.pallas_call(project_kernel, grid=(rows // block,), in_specs=[pl.BlockS...  8.24 us
  transfers between devices with their start and end apart: 12, of which 5 were waited for; matrix products, arithmetic and copies ran while one was open for 1% of the time, Pallas kernels for 46%

profile of v4, /device:TPU:0, one launch (start us, length us, event | category | flops | bytes accessed | tf_op | source)
XLA Modules:
  0.0 120.0 jit_solution(15849530341468622973)
XLA Ops:
  0.7 4.1 %collective-permute-start = (bf16[128,1024]{1,0:T(8,128)(2,1)}, bf16[128,1024]{1,0:T(8,128)(2,1)S(1)}, u32[]{:S(2)}, u32[]{:S(2)}) collective-permute-start(bf16[128,1024]{1,0:T(8,128)(2,1)} %refs_0_.1), channel_id=1, source_target_pairs={{0,8},{4,12},{8,0},{12,4},{1,9},{5,13},{9,1},{13,5},{2,10},{6,14},... | collective-permute-start | bytes 786440 | tf_op jit(solution)/shard_map/ppermute | solution.py:408
  4.8 8.2 %project.1.refs_1_.refs_2_ = bf16[2,1024,128]{2,1,0:T(8,128)(2,1)} custom-call(bf16[1024,4096]{1,0:T(8,128)(2,1)} %x_ref.1, f32[1,4096]{1,0:T(1,128)} %bitcast.1, bf16[4096,256]{1,0:T(8,128)(2,1)} %w_ref.1), custom_call_target="tpu_custom_call" | custom-call | flops 2147483648 | bytes 8388608 | tf_op jit(solution)/shard_map/project/pallas_call | solution.py:40
  13.0 1.5 %collective-permute-start.4 = (bf16[2,1024,128]{2,1,0:T(8,128)(2,1)}, bf16[2,1024,128]{2,1,0:T(8,128)(2,1)S(1)}, u32[]{:S(2)}, u32[]{:S(2)}) collective-permute-start(bf16[2,1024,128]{2,1,0:T(8,128)(2,1)} %project.1.refs_1_.refs_2_), channel_id=1, source_target_pairs={{0,16},{4,20},{8,24},{12,28},{16,0},{20,4},{24,8},{28,12},{1,17},{... | collective-permute-start | bytes 1572872 | tf_op jit(solution)/shard_map/ppermute | solution.py:416
  14.5 1.6 %collective-permute-start.2 = (bf16[2,1024,128]{2,1,0:T(8,128)(2,1)}, bf16[2,1024,128]{2,1,0:T(8,128)(2,1)S(1)}, u32[]{:S(2)}, u32[]{:S(2)}) collective-permute-start(bf16[2,1024,128]{2,1,0:T(8,128)(2,1)} %project.1.refs_1_.refs_2_), channel_id=1, source_target_pairs={{0,4},{4,0},{8,12},{12,8},{16,20},{20,16},{24,28},{28,24},{1,5},{5... | collective-permute-start | bytes 1572872 | tf_op jit(solution)/shard_map/ppermute | solution.py:416
  17.2 1.0 copy-done
  18.2 5.5 %forward.4 = (bf16[8,1024,512]{2,1,0:T(8,128)(2,1)S(1)}, f32[8,512]{1,0:T(8,128)S(1)}, f32[2,8,512]{2,1,0:T(8,128)S(1)}, f32[8,64,512]{2,1,0:T(8,128)S(1)}) custom-call(bf16[8,64,512]{2,1,0:T(8,128)(2,1)S(1)} %turn.2.refs_0_, bf16[2,1024,128]{2,1,0:T(8,128)(2,1)S(1)} %copy-done), custom_call_target="tpu_custom_call" | custom-call | flops 4294967296 | bytes 8388608 | tf_op jit(solution)/shard_map/forward/pallas_call | solution.py:187
  23.7 2.9 %collective-permute-done.4.refs_1_.refs_2_ = bf16[2,1024,128]{2,1,0:T(8,128)(2,1)S(1)} collective-permute-done((bf16[2,1024,128]{2,1,0:T(8,128)(2,1)}, bf16[2,1024,128]{2,1,0:T(8,128)(2,1)S(1)}, u32[]{:S(2)}, u32[]{:S(2)}) %collective-permute-start.4) | collective-permute-done | bytes 524320 | tf_op jit(solution)/shard_map/ppermute | solution.py:416
  26.7 1.6 %collective-permute-start.5 = (bf16[2,512,128]{2,1,0:T(8,128)(2,1)S(1)}, bf16[2,512,128]{2,1,0:T(8,128)(2,1)S(1)}, u32[]{:S(2)}, u32[]{:S(2)}) collective-permute-start(bf16[2,512,128]{2,1,0:T(8,128)(2,1)S(1)} %slice.9), channel_id=1, source_target_pairs={{0,4},{4,0},{8,12},{12,8},{16,20},{20,16},{24,28},{28,24},{1,5},{5... | collective-permute-start | bytes 786440 | tf_op jit(solution)/shard_map/ppermute | solution.py:416
  28.3 6.9 %collective-permute-done.2.refs_1_.refs_2_ = bf16[2,1024,128]{2,1,0:T(8,128)(2,1)S(1)} collective-permute-done((bf16[2,1024,128]{2,1,0:T(8,128)(2,1)}, bf16[2,1024,128]{2,1,0:T(8,128)(2,1)S(1)}, u32[]{:S(2)}, u32[]{:S(2)}) %collective-permute-start.2) | collective-permute-done | bytes 524320 | tf_op jit(solution)/shard_map/ppermute | solution.py:416
  35.9 5.8 %forward.5 = (bf16[8,1024,512]{2,1,0:T(8,128)(2,1)S(1)}, f32[8,512]{1,0:T(8,128)S(1)}, f32[2,8,512]{2,1,0:T(8,128)S(1)}, f32[8,64,512]{2,1,0:T(8,128)S(1)}) custom-call(bf16[8,64,512]{2,1,0:T(8,128)(2,1)S(1)} %turn.2.refs_0_, bf16[2,1024,128]{2,1,0:T(8,128)(2,1)S(1)} %collective-permute-done.2.refs_1_.refs_2_, f32[2,8,512]{2,1,0:T(8,128)S(1)} %get-tuple-element.32.refs_2_, ...), custom_call_target="tpu_custom_call" | custom-call | flops 4294967296 | bytes 8388608 | tf_op jit(solution)/shard_map/forward/pallas_call | solution.py:187
  41.7 6.0 %forward.6 = (bf16[8,1024,512]{2,1,0:T(8,128)(2,1)S(1)}, f32[8,512]{1,0:T(8,128)S(1)}, f32[2,8,512]{2,1,0:T(8,128)S(1)}, f32[8,64,512]{2,1,0:T(8,128)S(1)}) custom-call(bf16[8,64,512]{2,1,0:T(8,128)(2,1)S(1)} %turn.2.refs_0_, bf16[2,1024,128]{2,1,0:T(8,128)(2,1)S(1)} %collective-permute-done.4.refs_1_.refs_2_, f32[2,8,512]{2,1,0:T(8,128)S(1)} %get-tuple-element.34.refs_2_, ...), custom_call_target="tpu_custom_call" | custom-call | flops 4294967296 | bytes 8388608 | tf_op jit(solution)/shard_map/forward/pallas_call | solution.py:187
  47.7 5.9 %forward.7 = (bf16[8,1024,512]{2,1,0:T(8,128)(2,1)S(1)}, f32[8,512]{1,0:T(8,128)S(1)}, f32[3,8,512]{2,1,0:T(8,128)S(1)}, f32[8,64,512]{2,1,0:T(8,128)S(1)}) custom-call(bf16[8,64,512]{2,1,0:T(8,128)(2,1)S(1)} %turn.2.refs_0_, bf16[8,64,512]{2,1,0:T(8,128)(2,1)S(1)} %turn.3.refs_1_, bf16[2,512,128]{2,1,0:T(8,128)(2,1)S(1)} %collective-permute-done.3.refs_2_, ...), custom_call_target="tpu_custom_call" | custom-call | flops 4294967296 | bytes 8388608 | tf_op jit(solution)/shard_map/forward/pallas_call | solution.py:187
  53.7 1.9 %collective-permute-start.6 = (f32[3,8,512]{2,1,0:T(8,128)S(1)}, f32[3,8,512]{2,1,0:T(8,128)S(1)}, u32[]{:S(2)}, u32[]{:S(2)}) collective-permute-start(f32[3,8,512]{2,1,0:T(8,128)S(1)} %get-tuple-element.40.refs_6_.refs_5_), channel_id=1, source_target_pairs={{0,8},{4,12},{8,0},{12,4},{1,9},{5,13},{9,1},{13,5},{2,10},{6,14},... | collective-permute-start | bytes 147464 | tf_op jit(solution)/shard_map/ppermute | solution.py:408
  55.6 3.7 %collective-permute-done.6.refs_7_.refs_6_ = f32[3,8,512]{2,1,0:T(8,128)S(1)} collective-permute-done((f32[3,8,512]{2,1,0:T(8,128)S(1)}, f32[3,8,512]{2,1,0:T(8,128)S(1)}, u32[]{:S(2)}, u32[]{:S(2)}) %collective-permute-start.6) | collective-permute-done | bytes 49184 | tf_op jit(solution)/shard_map/ppermute | solution.py:408
  59.2 10.0 %backward.4 = (bf16[128,1024]{1,0:T(8,128)(2,1)S(1)}, bf16[128,1024]{1,0:T(8,128)(2,1)S(1)}, f32[8,64,512]{2,1,0:T(8,128)S(1)}, bf16[1024,256]{1,0:T(8,128)(2,1)S(1)}) custom-call(bf16[8,64,512]{2,1,0:T(8,128)(2,1)S(1)} %turn.2.refs_0_, bf16[8,64,512]{2,1,0:T(8,128)(2,1)S(1)} %turn.3.refs_1_, bf16[2,512,128]{2,1,0:T(8,128)(2,1)S(1)} %collective-permute-done.3.refs_2_, ...), custom_call_target="tpu_custom_call" | custom-call | flops 6442450944 | bytes 8388608 | tf_op jit(solution)/shard_map/backward/pallas_call | solution.py:367
  69.3 1.4 %collective-permute-start.7 = (bf16[128,1024]{1,0:T(8,128)(2,1)S(1)}, bf16[128,1024]{1,0:T(8,128)(2,1)S(1)}, u32[]{:S(2)}, u32[]{:S(2)}) collective-permute-start(bf16[128,1024]{1,0:T(8,128)(2,1)S(1)} %get-tuple-element.43), channel_id=1, source_target_pairs={{0,8},{4,12},{8,0},{12,4},{1,9},{5,13},{9,1},{13,5},{2,10},{6,14},... | collective-permute-start | bytes 786440 | tf_op jit(solution)/shard_map/ppermute | solution.py:408
  70.7 9.4 %backward.5 = (f32[8,64,512]{2,1,0:T(8,128)S(1)}, bf16[1024,256]{1,0:T(8,128)(2,1)S(1)}) custom-call(bf16[8,64,512]{2,1,0:T(8,128)(2,1)S(1)} %turn.2.refs_0_, bf16[8,64,512]{2,1,0:T(8,128)(2,1)S(1)} %turn.3.refs_1_, bf16[2,1024,128]{2,1,0:T(8,128)(2,1)S(1)} %collective-permute-done.4.refs_1_.refs_2_, bf16[8,1024,512]{2,1,0:T(8,128)(2,1)S(1)} %get-tuple-element.48.refs_3_, ...), custom_call_target="tpu_custom_call" | custom-call | flops 6442450944 | bytes 8388608 | tf_op jit(solution)/shard_map/backward/pallas_call | solution.py:367
  80.1 9.6 %backward.6 = (f32[8,64,512]{2,1,0:T(8,128)S(1)}, bf16[1024,256]{1,0:T(8,128)(2,1)S(1)}) custom-call(bf16[8,64,512]{2,1,0:T(8,128)(2,1)S(1)} %turn.2.refs_0_, bf16[8,64,512]{2,1,0:T(8,128)(2,1)S(1)} %turn.3.refs_1_, bf16[2,1024,128]{2,1,0:T(8,128)(2,1)S(1)} %collective-permute-done.2.refs_1_.refs_2_, bf16[8,1024,512]{2,1,0:T(8,128)(2,1)S(1)} %get-tuple-element.46.refs_3_, ...), custom_call_target="tpu_custom_call" | custom-call | flops 6442450944 | bytes 8388608 | tf_op jit(solution)/shard_map/backward/pallas_call | solution.py:367
  89.7 2.0 %collective-permute-start.11 = (bf16[1024,256]{1,0:T(8,128)(2,1)S(1)}, bf16[1024,256]{1,0:T(8,128)(2,1)S(1)}, u32[]{:S(2)}, u32[]{:S(2)}) collective-permute-start(bf16[1024,256]{1,0:T(8,128)(2,1)S(1)} %get-tuple-element.57), channel_id=1, source_target_pairs={{0,4},{4,0},{8,12},{12,8},{16,20},{20,16},{24,28},{28,24},{1,5},{5... | collective-permute-start | bytes 1572872 | tf_op jit(solution)/shard_map/ppermute | solution.py:416
  92.3 1.0 collective-permute-start.9
  93.3 9.8 %backward.7 = (bf16[128,1024]{1,0:T(8,128)(2,1)S(1)}, bf16[128,1024]{1,0:T(8,128)(2,1)S(1)}, f32[1024,256]{1,0:T(8,128)S(1)}) custom-call(bf16[8,64,512]{2,1,0:T(8,128)(2,1)S(1)} %turn.2.refs_0_, bf16[8,64,512]{2,1,0:T(8,128)(2,1)S(1)} %turn.3.refs_1_, bf16[2,1024,128]{2,1,0:T(8,128)(2,1)S(1)} %copy-done.1, ...), custom_call_target="tpu_custom_call" | custom-call | flops 6442450944 | bytes 8388608 | tf_op jit(solution)/shard_map/backward/pallas_call | solution.py:367
  103.1 1.6 %collective-permute-start.8 = (bf16[128,1024]{1,0:T(8,128)(2,1)S(1)}, bf16[128,1024]{1,0:T(8,128)(2,1)S(1)}, u32[]{:S(2)}, u32[]{:S(2)}) collective-permute-start(bf16[128,1024]{1,0:T(8,128)(2,1)S(1)} %get-tuple-element.54), channel_id=1, source_target_pairs={{0,8},{4,12},{8,0},{12,4},{1,9},{5,13},{9,1},{13,5},{2,10},{6,14},... | collective-permute-start | bytes 786440 | tf_op jit(solution)/shard_map/ppermute | solution.py:408
  105.5 12.6 %collective-permute-done.8 = bf16[128,1024]{1,0:T(8,128)(2,1)S(1)} collective-permute-done((bf16[128,1024]{1,0:T(8,128)(2,1)S(1)}, bf16[128,1024]{1,0:T(8,128)(2,1)S(1)}, u32[]{:S(2)}, u32[]{:S(2)}) %collective-permute-start.8) | collective-permute-done | bytes 262176 | tf_op jit(solution)/shard_map/ppermute | solution.py:408
  118.9 1.0 add_convert_fusion
  (24 shorter events, 4.0 us)
Async XLA Ops:
  0.6 16.3 %copy-start.2 = (bf16[128,1024]{1,0:T(8,128)(2,1)S(1)}, bf16[128,1024]{1,0:T(8,128)(2,1)}, u32[]{:S(2)}) copy-start(bf16[128,1024]{1,0:T(8,128)(2,1)} %refs_0_.1) | copy-start | bytes 786436
  0.6 16.3 %copy-start.3 = (bf16[128,1024]{1,0:T(8,128)(2,1)S(1)}, bf16[128,1024]{1,0:T(8,128)(2,1)}, u32[]{:S(2)}) copy-start(bf16[128,1024]{1,0:T(8,128)(2,1)} %refs_0_.2) | copy-start | bytes 786436
  0.7 16.3 %collective-permute-start = (bf16[128,1024]{1,0:T(8,128)(2,1)}, bf16[128,1024]{1,0:T(8,128)(2,1)S(1)}, u32[]{:S(2)}, u32[]{:S(2)}) collective-permute-start(bf16[128,1024]{1,0:T(8,128)(2,1)} %refs_0_.1), channel_id=1, source_target_pairs={{0,8},{4,12},{8,0},{12,4},{1,9},{5,13},{9,1},{13,5},{2,10},{6,14},... | collective-permute-start | bytes 786440 | tf_op jit(solution)/shard_map/ppermute | solution.py:408
  13.0 13.6 %collective-permute-start.4 = (bf16[2,1024,128]{2,1,0:T(8,128)(2,1)}, bf16[2,1024,128]{2,1,0:T(8,128)(2,1)S(1)}, u32[]{:S(2)}, u32[]{:S(2)}) collective-permute-start(bf16[2,1024,128]{2,1,0:T(8,128)(2,1)} %project.1.refs_1_.refs_2_), channel_id=1, source_target_pairs={{0,16},{4,20},{8,24},{12,28},{16,0},{20,4},{24,8},{28,12},{1,17},{... | collective-permute-start | bytes 1572872 | tf_op jit(solution)/shard_map/ppermute | solution.py:416
  14.5 20.6 %collective-permute-start.2 = (bf16[2,1024,128]{2,1,0:T(8,128)(2,1)}, bf16[2,1024,128]{2,1,0:T(8,128)(2,1)S(1)}, u32[]{:S(2)}, u32[]{:S(2)}) collective-permute-start(bf16[2,1024,128]{2,1,0:T(8,128)(2,1)} %project.1.refs_1_.refs_2_), channel_id=1, source_target_pairs={{0,4},{4,0},{8,12},{12,8},{16,20},{20,16},{24,28},{28,24},{1,5},{5... | collective-permute-start | bytes 1572872 | tf_op jit(solution)/shard_map/ppermute | solution.py:416
  17.0 18.8 %collective-permute-start.1 = (bf16[128,1024]{1,0:T(8,128)(2,1)S(1)}, bf16[128,1024]{1,0:T(8,128)(2,1)S(1)}, u32[]{:S(2)}, u32[]{:S(2)}) collective-permute-start(bf16[128,1024]{1,0:T(8,128)(2,1)S(1)} %copy-done.3), channel_id=1, source_target_pairs={{0,8},{4,12},{8,0},{12,4},{1,9},{5,13},{9,1},{13,5},{2,10},{6,14},... | collective-permute-start | bytes 786440 | tf_op jit(solution)/shard_map/ppermute | solution.py:408
  17.1 1.0 copy-start
  26.7 21.1 %collective-permute-start.5 = (bf16[2,512,128]{2,1,0:T(8,128)(2,1)S(1)}, bf16[2,512,128]{2,1,0:T(8,128)(2,1)S(1)}, u32[]{:S(2)}, u32[]{:S(2)}) collective-permute-start(bf16[2,512,128]{2,1,0:T(8,128)(2,1)S(1)} %slice.9), channel_id=1, source_target_pairs={{0,4},{4,0},{8,12},{12,8},{16,20},{20,16},{24,28},{28,24},{1,5},{5... | collective-permute-start | bytes 786440 | tf_op jit(solution)/shard_map/ppermute | solution.py:416
  35.2 12.6 %collective-permute-start.3 = (bf16[2,512,128]{2,1,0:T(8,128)(2,1)S(1)}, bf16[2,512,128]{2,1,0:T(8,128)(2,1)S(1)}, u32[]{:S(2)}, u32[]{:S(2)}) collective-permute-start(bf16[2,512,128]{2,1,0:T(8,128)(2,1)S(1)} %slice.8), channel_id=1, source_target_pairs={{0,16},{4,20},{8,24},{12,28},{16,0},{20,4},{24,8},{28,12},{1,17},{... | collective-permute-start | bytes 786440 | tf_op jit(solution)/shard_map/ppermute | solution.py:416
  53.7 5.6 %collective-permute-start.6 = (f32[3,8,512]{2,1,0:T(8,128)S(1)}, f32[3,8,512]{2,1,0:T(8,128)S(1)}, u32[]{:S(2)}, u32[]{:S(2)}) collective-permute-start(f32[3,8,512]{2,1,0:T(8,128)S(1)} %get-tuple-element.40.refs_6_.refs_5_), channel_id=1, source_target_pairs={{0,8},{4,12},{8,0},{12,4},{1,9},{5,13},{9,1},{13,5},{2,10},{6,14},... | collective-permute-start | bytes 147464 | tf_op jit(solution)/shard_map/ppermute | solution.py:408
  69.3 35.5 %collective-permute-start.7 = (bf16[128,1024]{1,0:T(8,128)(2,1)S(1)}, bf16[128,1024]{1,0:T(8,128)(2,1)S(1)}, u32[]{:S(2)}, u32[]{:S(2)}) collective-permute-start(bf16[128,1024]{1,0:T(8,128)(2,1)S(1)} %get-tuple-element.43), channel_id=1, source_target_pairs={{0,8},{4,12},{8,0},{12,4},{1,9},{5,13},{9,1},{13,5},{2,10},{6,14},... | collective-permute-start | bytes 786440 | tf_op jit(solution)/shard_map/ppermute | solution.py:408
  80.1 13.2 %copy-start.1 = (bf16[2,1024,128]{2,1,0:T(8,128)(2,1)S(1)}, bf16[2,1024,128]{2,1,0:T(8,128)(2,1)}, u32[]{:S(2)}) copy-start(bf16[2,1024,128]{2,1,0:T(8,128)(2,1)} %project.1.refs_1_.refs_2_) | copy-start | bytes 1572868
  89.7 29.2 %collective-permute-start.11 = (bf16[1024,256]{1,0:T(8,128)(2,1)S(1)}, bf16[1024,256]{1,0:T(8,128)(2,1)S(1)}, u32[]{:S(2)}, u32[]{:S(2)}) collective-permute-start(bf16[1024,256]{1,0:T(8,128)(2,1)S(1)} %get-tuple-element.57), channel_id=1, source_target_pairs={{0,4},{4,0},{8,12},{12,8},{16,20},{20,16},{24,28},{28,24},{1,5},{5... | collective-permute-start | bytes 1572872 | tf_op jit(solution)/shard_map/ppermute | solution.py:416
  91.8 27.1 %collective-permute-start.10 = (bf16[1024,256]{1,0:T(8,128)(2,1)S(1)}, bf16[1024,256]{1,0:T(8,128)(2,1)S(1)}, u32[]{:S(2)}, u32[]{:S(2)}) collective-permute-start(bf16[1024,256]{1,0:T(8,128)(2,1)S(1)} %get-tuple-element.56), channel_id=1, source_target_pairs={{0,16},{4,20},{8,24},{12,28},{16,0},{20,4},{24,8},{28,12},{1,17},{... | collective-permute-start | bytes 1572872 | tf_op jit(solution)/shard_map/ppermute | solution.py:416
  92.3 26.6 %collective-permute-start.9 = (bf16[1024,256]{1,0:T(8,128)(2,1)S(1)}, bf16[1024,256]{1,0:T(8,128)(2,1)S(1)}, u32[]{:S(2)}, u32[]{:S(2)}) collective-permute-start(bf16[1024,256]{1,0:T(8,128)(2,1)S(1)} %get-tuple-element.55), channel_id=1, source_target_pairs={{0,20},{4,16},{8,28},{12,24},{16,4},{20,0},{24,12},{28,8},{1,21},{... | collective-permute-start | bytes 1572872 | tf_op jit(solution)/shard_map/ppermute | solution.py:416
  103.1 15.1 %collective-permute-start.8 = (bf16[128,1024]{1,0:T(8,128)(2,1)S(1)}, bf16[128,1024]{1,0:T(8,128)(2,1)S(1)}, u32[]{:S(2)}, u32[]{:S(2)}) collective-permute-start(bf16[128,1024]{1,0:T(8,128)(2,1)S(1)} %get-tuple-element.54), channel_id=1, source_target_pairs={{0,8},{4,12},{8,0},{12,4},{1,9},{5,13},{9,1},{13,5},{2,10},{6,14},... | collective-permute-start | bytes 786440 | tf_op jit(solution)/shard_map/ppermute | solution.py:408

commit v5 on v4

--- a/solution.py
+++ b/solution.py
@@ -101,7 +101,7 @@
     c_ref = refs.pop(0) if last else None
     piece_refs = [refs.pop(0) for _ in range(pieces)]
     past, past_acc = (None, None) if first else (refs.pop(0), refs.pop(0))
-    e_hbm, top_ref, st_ref, acc_ref, whole_ref, value_t, scores, expo, sem = refs
+    e_ref, top_ref, st_ref, acc_ref, whole_ref, value_t, scores, expo = refs
     kv_ref = gathered(piece_refs, whole_ref)
     length = kv_ref.shape[1]
     lanes = q_ref.shape[2]
@@ -114,24 +114,21 @@
     def group_of(c):
         return (c // per_group) % groups
 
-    def store(slot, c):
-        return pltpu.make_async_copy(expo.at[slot], e_hbm.at[c], sem.at[slot])
-
-    def emit(ca, cb, cc, slot, top, wait):
+    def emit(ca, cb, cc, slot, top):
         largest, total = None, None
         if ca is not None:
             weights = jnp.concatenate([q_ref[ca] * jnp.asarray(SCALE, bf16), pad], axis=0)
             ga = group_of(ca)
         if cb is not None:
             low_top = top * LOG2E
-            if wait:
-                store(slot, cb).wait()
         if cc is not None:
             gc = group_of(cc)
         for k in range(steps):
             ks = slice(k * KEY_ROWS, (k + 1) * KEY_ROWS)
             if cb is not None:
-                expo[slot, ks] = jnp.exp2(scores[ks] * LOG2E - low_top).astype(bf16)
+                weight = jnp.exp2(scores[ks] * LOG2E - low_top).astype(bf16)
+                expo[slot, ks] = weight
+                e_ref[cb, ks] = weight
             if ca is not None:
                 s = jnp.dot(kv_ref[ga, ks], weights, preferred_element_type=f32)
                 scores[ks] = s
@@ -142,7 +139,6 @@
                 total = part if total is None else total + part
         if cb is not None:
             top_ref[pl.ds(cb, 1)] = top
-            store(slot, cb).start()
         if cc is not None:
             m = top_ref[pl.ds(cc, 1)]
             l = total[HD : HD + 1]
@@ -162,19 +158,16 @@
         return None if largest is None else jnp.max(largest, axis=0, keepdims=True)
 
     n = chunks
-    top = emit(0, None, None, None, None, False)
-    top = emit(1, 0, None, 0, top, False)
-
-    def body(j, top, wait=True):
-        top = emit(2 * j + 2, 2 * j + 1, 2 * j, 1, top, wait)
-        return emit(2 * j + 3, 2 * j + 2, 2 * j + 1, 0, top, True)
-
-    top = body(0, top, wait=False)
-    top = lax.fori_loop(1, n // 2 - 1, body, top)
-    emit(None, n - 1, n - 2, 1, top, True)
-    emit(None, None, n - 1, 0, None, False)
-    store(0, n - 2).wait()
-    store(1, n - 1).wait()
+    top = emit(0, None, None, None, None)
+    top = emit(1, 0, None, 0, top)
+
+    def body(j, top):
+        top = emit(2 * j + 2, 2 * j + 1, 2 * j, 1, top)
+        return emit(2 * j + 3, 2 * j + 2, 2 * j + 1, 0, top)
+
+    top = lax.fori_loop(0, n // 2 - 1, body, top)
+    emit(None, n - 1, n - 2, 1, top)
+    emit(None, None, n - 1, 0, None)
 
 
 def forward(dims, q_rows, c_rows, pairs, before):
@@ -187,7 +180,7 @@
     return pl.pallas_call(
         functools.partial(forward_kernel, dims, len(pairs), first, last),
         in_specs=[IN_VMEM] * len(args),
-        out_specs=[IN_PLACE, IN_VMEM, IN_VMEM, IN_VMEM],
+        out_specs=[IN_VMEM] * 4,
         out_shape=[
             jax.ShapeDtypeStruct((chunks, length, lanes), bf16),
             jax.ShapeDtypeStruct((chunks, lanes), f32),
@@ -199,7 +192,6 @@
             pltpu.VMEM((groups, HD + 16, length), bf16),
             pltpu.VMEM((length, lanes), f32),
             pltpu.VMEM((2, length, lanes), bf16),
-            pltpu.SemaphoreType.DMA((2,)),
         ],
         compiler_params=pltpu.CompilerParams(vmem_limit_bytes=VMEM_BYTES),
         cost_estimate=pl.CostEstimate(flops=16 * size * HD, bytes_accessed=2 * size, transcendentals=size),
@@ -213,40 +205,40 @@
     return rows if shift == 0 else jnp.concatenate([rows[count - shift :], rows[: count - shift]], axis=0)
 
 
-def backward_kernel(dims, pieces, peers, first, last, *refs):
+def backward_kernel(dims, pieces, peers, span, first, last, *refs):
     chunks, groups, per_group = dims
+    begin, end = span
+    blocks = peers + 1
+    per_block = chunks // blocks
+    whole_span = span == (0, chunks)
     refs = list(refs)
     q_ref, c_ref = refs.pop(0), refs.pop(0)
     piece_refs = [refs.pop(0) for _ in range(pieces)]
-    e_hbm, top_ref, own_ref = [refs.pop(0) for _ in range(3)]
+    e_ref, top_ref, own_ref = [refs.pop(0) for _ in range(3)]
     peer_refs = [refs.pop(0) for _ in range(peers)]
     acc_ref = refs.pop(0) if first else None
     past_dq = None if first else refs.pop(0)
-    blocks = peers + 1
+    past_sums = [refs.pop(0), refs.pop(0)] if begin == 0 and not whole_span else None
     ctx_outs = [refs.pop(0) for _ in range(blocks)] if first else None
-    dq_outs = [refs.pop(0) for _ in range(blocks)] if last else [refs.pop(0)]
-    dkv_ref = refs.pop(0)
-    whole_ref, key_t, expo, score_grad, key_sum, value_sum, factor, delta, rows, sem, row_sem = refs
+    sent = list(range(begin // per_block, end // per_block))
+    dq_outs = [refs.pop(0) for _ in sent] if last else [refs.pop(0)]
+    outs = [refs.pop(0)] if begin == 0 else [refs.pop(0), refs.pop(0)]
+    whole_ref, key_t, score_grad, key_sum, value_sum, factor, delta, rows, row_sem = refs
     kv_ref = gathered(piece_refs, whole_ref)
     length = kv_ref.shape[1]
     lanes = q_ref.shape[2]
     steps = length // KEY_ROWS
-    heads = lanes // rows.shape[1]
-    per_block = chunks // blocks
+    tokens = rows.shape[1]
+    heads = lanes // tokens
     pad = jnp.zeros((HD, lanes), bf16)
 
     def group_of(c):
         return (c // per_group) % groups
 
-    def fetch(slot, c):
-        return pltpu.make_async_copy(e_hbm.at[c], expo.at[slot], sem.at[slot])
-
-    fetch(0, 0).start()
-    fetch(1, 1).start()
     for g in range(groups):
         key_t[g] = kv_ref[g].T[:HD]
-    key_sum[...] = jnp.zeros_like(key_sum)
-    value_sum[...] = jnp.zeros_like(value_sum)
+    key_sum[...] = jnp.zeros_like(key_sum) if past_sums is None else past_sums[0][...]
+    value_sum[...] = jnp.zeros_like(value_sum) if past_sums is None else past_sums[1][...]
 
     stats = [[own_ref[i] for i in range(3)]]
     for r in range(1, blocks):
@@ -260,12 +252,12 @@
         factor[1] = shares[0] / total
 
     def put_rows(c, value):
-        flat = jnp.concatenate([value[:, h * rows.shape[1] : (h + 1) * rows.shape[1]] for h in range(heads)], axis=0)
+        flat = jnp.concatenate([value[:, h * tokens : (h + 1) * tokens] for h in range(heads)], axis=0)
         offset = pl.multiple_of((c % per_block) * heads * HD, heads * HD)
         rows[c // per_block, :, pl.ds(offset, heads * HD)] = flat.astype(bf16).T
 
-    def send_rows(outs):
-        copies = [pltpu.make_async_copy(rows.at[s], outs[s], row_sem.at[s]) for s in range(blocks)]
+    def send_rows(which, refs):
+        copies = [pltpu.make_async_copy(rows.at[s], ref, row_sem.at[s]) for s, ref in zip(which, refs)]
         for copy in copies:
             copy.start()
         for copy in copies:
@@ -278,15 +270,14 @@
             return 0
 
         lax.fori_loop(0, chunks, put_context, 0)
-        send_rows(ctx_outs)
-
-    def emit(ca, cb, slot):
+        send_rows(range(blocks), ctx_outs)
+
+    def emit(ca, cb):
         if ca is not None:
             ga = group_of(ca)
             weights = jnp.concatenate([pad, c_ref[ca]], axis=0)
             fa, da = factor[0, pl.ds(ca, 1)], delta[pl.ds(ca, 1)]
             scaled_c = (c_ref[ca].astype(f32) * fa).astype(bf16)
-            fetch(slot, ca).wait()
         if cb is not None:
             gb = group_of(cb)
             fb = factor[0, pl.ds(cb, 1)] * SCALE
@@ -300,7 +291,7 @@
                 dq = part if dq is None else dq + part
                 key_sum[gb, :, ks] += lax.dot_general(scaled_q, ds, NT, preferred_element_type=f32)
             if ca is not None:
-                e = expo[slot, ks]
+                e = e_ref[ca, ks]
                 prob_grad = jnp.dot(kv_ref[ga, ks], weights, preferred_element_type=f32)
                 score_grad[ks] = (e.astype(f32) * (prob_grad - da)).astype(bf16)
                 value_sum[ga, :, ks] += lax.dot_general(scaled_c, e, NT, preferred_element_type=f32)
@@ -313,73 +304,73 @@
             else:
                 dq_outs[0][cb] = dq
 
-    n = chunks
-    emit(0, None, 0)
+    emit(begin, None)
 
     def body(j, _):
-        @pl.when(2 * j + 2 < n)
-        def _():
-            fetch(0, 2 * j + 2).start()
-
-        emit(2 * j + 1, 2 * j, 1)
-
-        @pl.when(2 * j + 2 < n)
-        def _():
-            fetch(1, 2 * j + 3).start()
-            emit(2 * j + 2, 2 * j + 1, 0)
-
+        c = begin + 2 * j
+        emit(c + 1, c)
+        emit(c + 2, c + 1)
         return 0
 
-    lax.fori_loop(0, n // 2, body, 0)
-    emit(None, n - 1, None)
+    lax.fori_loop(0, (end - begin) // 2 - 1, body, 0)
+    emit(end - 1, end - 2)
+    emit(None, end - 1)
     if last:
-        send_rows(dq_outs)
-    for g in range(groups):
-        both = jnp.concatenate([key_sum[g], value_sum[g]], axis=0)
-        dkv_ref[:, g * 2 * HD : (g + 1) * 2 * HD] = both.T.astype(dkv_ref.dtype)
-
-
-def backward(dims, q_rows, c_rows, pairs, expo, top, own, peers, acc, past_dq, last, tokens):
+        send_rows(sent, dq_outs)
+    if begin > 0:
+        outs[0][...] = key_sum[...]
+        outs[1][...] = value_sum[...]
+    else:
+        for g in range(groups):
+            both = jnp.concatenate([key_sum[g].astype(bf16), value_sum[g].astype(bf16)], axis=0)
+            outs[0][:, g * 2 * HD : (g + 1) * 2 * HD] = both.T
+
+
+def backward(dims, q_rows, c_rows, pairs, expo, top, own, peers, acc, past_dq, past_sums, span, last, tokens):
     chunks, groups, _ = dims
+    begin, end = span
     lanes = q_rows.shape[2]
     length = sum(p.shape[1] for p in pairs)
     first = past_dq is None
     blocks = len(peers) + 1
-    width = chunks // blocks * (lanes // tokens) * HD
-    args = [q_rows, c_rows, *pairs, expo, top, own, *peers] + [acc if first else past_dq]
-    specs = [IN_VMEM] * len(args)
-    specs[2 + len(pairs)] = IN_PLACE
+    per_block = chunks // blocks
+    width = per_block * (lanes // tokens) * HD
+    args = [q_rows, c_rows, *pairs, expo, top, own, *peers] + [acc if first else past_dq] + list(past_sums or [])
     row_block = jax.ShapeDtypeStruct((tokens, width), bf16)
+    sums = jax.ShapeDtypeStruct((groups, HD, length), f32)
     outs, out_specs = [], []
     if first:
         outs += [row_block] * blocks
         out_specs += [IN_PLACE] * blocks
+    sent = (end - begin) // per_block
     if last:
-        outs += [row_block] * blocks
-        out_specs += [IN_PLACE] * blocks
+        outs += [row_block] * sent
+        out_specs += [IN_PLACE] * sent
     else:
         outs.append(jax.ShapeDtypeStruct((chunks, HD, lanes), f32))
         out_specs.append(IN_VMEM)
-    outs.append(jax.ShapeDtypeStruct((length, groups * 2 * HD), f32 if last else bf16))
-    out_specs.append(IN_VMEM)
-    size = chunks * lanes * length
+    if begin > 0:
+        outs += [sums] * 2
+        out_specs += [IN_VMEM] * 2
+    else:
+        outs.append(jax.ShapeDtypeStruct((length, groups * 2 * HD), bf16))
+        out_specs.append(IN_VMEM)
+    size = (end - begin) * lanes * length
     results = list(
         pl.pallas_call(
-            functools.partial(backward_kernel, dims, len(pairs), len(peers), first, last),
-            in_specs=specs,
+            functools.partial(backward_kernel, dims, len(pairs), len(peers), span, first, last),
+            in_specs=[IN_VMEM] * len(args),
             out_specs=out_specs,
             out_shape=outs,
             scratch_shapes=[
                 pltpu.VMEM((groups, length, 2 * HD), bf16),
                 pltpu.VMEM((groups, HD, length), bf16),
-                pltpu.VMEM((2, length, lanes), bf16),
                 pltpu.VMEM((length, lanes), bf16),
                 pltpu.VMEM((groups, HD, length), f32),
                 pltpu.VMEM((groups, HD, length), f32),
                 pltpu.VMEM((2, chunks, lanes), f32),
                 pltpu.VMEM((chunks, lanes), f32),
                 pltpu.VMEM((blocks, tokens, width), bf16),
-                pltpu.SemaphoreType.DMA((2,)),
                 pltpu.SemaphoreType.DMA((blocks,)),
             ],
             compiler_params=pltpu.CompilerParams(vmem_limit_bytes=VMEM_BYTES),
@@ -388,8 +379,8 @@
         )(*args)
     )
     context = [results.pop(0) for _ in range(blocks)] if first else None
-    dq = [results.pop(0) for _ in range(blocks)] if last else results.pop(0)
-    return context, dq, results.pop(0)
+    dq = [results.pop(0) for _ in range(sent)] if last else results.pop(0)
+    return context, dq, results if begin > 0 else results[0]
 
 
 def on_device(halves, seqs, enc_states, norm_gain, kv_weight, queries, cotangent):
@@ -416,20 +407,21 @@
         return lax.ppermute(x, ("half", "seq"), pairs)
 
     q_blocks = [queries] + [from_far(queries, s) for s in range(1, fars)]
-    late, *_ = lax.optimization_barrier((cotangent, *q_blocks[1:]))
-    c_blocks = [late] + [from_far(late, s) for s in range(1, fars)]
     own_pairs = project(enc_states, norm_gain, kv_weight)
     order = sorted(
-        ((a, b) for a in range(halves) for b in range(near)), key=lambda s: (s != (0, 0), s[0] > 0 and s[1] > 0)
+        ((a, b) for a in range(halves) for b in range(near)), key=lambda s: (s[0] > 0 and s[1] > 0, s[1])
     )
     blocks = {(0, 0): [own_pairs]}
     for a, b in order[1:]:
         if a and b:
             across, along = blocks[a, 0][0], blocks[0, b][0]
             middle = across.shape[1] // 2
-            blocks[a, b] = [from_near(along[:, :middle], a, 0), from_near(across[:, middle:], 0, b)]
+            upper = from_near(across[:, middle:], 0, b)
+            blocks[a, b] = [from_near(along[:, :middle], a, 0), upper]
         else:
             blocks[a, b] = [from_near(own_pairs, a, b)]
+    c_own, *_ = lax.optimization_barrier((cotangent, *[blocks[s][0] for s in order[1:3]]))
+    c_blocks = [cotangent] + [from_far(c_own, s) for s in range(1, fars)]
     pair_blocks = [blocks[s] for s in order]
     count = len(order)
     q_rows = turn(q_blocks, heads)
@@ -443,22 +435,29 @@
         before = (stats, acc)
     peers = [from_far(stats, r) for r in range(1, fars)]
 
+    def back(i, span, dq, sums, last):
+        return backward(
+            dims, q_rows, c_rows, pair_blocks[i], expos[i], tops[i], stats, peers, acc, dq, sums, span, last, tokens
+        )
+
     dq, sends, context_parts = None, [], None
-    for i in reversed(range(count)):
-        parts, dq, dkv = backward(
-            dims, q_rows, c_rows, pair_blocks[i], expos[i], tops[i], stats, peers, acc, dq, i == 0, tokens
-        )
+    for i in reversed(range(1, count)):
+        parts, dq, dkv = back(i, (0, chunks), dq, None, False)
         if parts is not None:
             context_parts = parts
-        sends.append(dkv if i == 0 else from_near(dkv, -order[i][0], -order[i][1]))
-
-    def home(parts):
-        arrived = [parts[0]] + [from_far(parts[s], -s) for s in range(1, fars)]
-        return sum(x.astype(f32) for x in arrived).astype(bf16)
-
-    context = home(context_parts)
-    d_queries = home(dq)
-    d_pairs = sum(x.astype(f32) for x in sends).astype(bf16)
+        sends.append(from_near(dkv, -order[i][0], -order[i][1]))
+    split = chunks // fars
+    _, away, sums = back(0, (split, chunks), dq, None, True)
+    away = [from_far(x, -s) for s, x in enumerate(away, 1)]
+    _, (stay,), dkv = back(0, (0, split), dq, sums, True)
+    sends.append(dkv)
+
+    def total(arrays):
+        return sum(x.astype(f32) for x in arrays).astype(bf16)
+
+    context = total([context_parts[0]] + [from_far(context_parts[s], -s) for s in range(1, fars)])
+    d_queries = total([stay, *away])
+    d_pairs = total(sends)
     return (context, d_queries, d_pairs)
 
 

time: 120 us -> 115 us (0.958)
  Pallas kernels: 70.6 us -> 65.6 us
  waiting for transfers between devices: 26.9 us -> 24.9 us
  starting transfers between devices: 17.9 us -> 19.6 us
    pallas_call x4 -> x5, Pallas kernels: 38.8 us -> 33.8 us  [backward(): pl.pallas_call(functools.partial(backward_kernel, dims, len(pairs), len(p...]
    ppermute x7, waiting for transfers between devices: 9.76 us -> 5.21 us  [from_near(): return lax.ppermute(x, ('half', 'seq'), pairs)]
    ppermute x5, waiting for transfers between devices: 17.2 us -> 19.7 us  [from_far(): lax.ppermute(x, 'seq', [(i, (i + shift * near) % seqs) for i in range(seq...]
    ppermute x5, starting transfers between devices: 9.06 us -> 10.6 us  [from_far(): lax.ppermute(x, 'seq', [(i, (i + shift * near) % seqs) for i in range(seq...]
  transfers between devices with their start and end apart: 12 -> 12, of which waited for: 5 -> 6; matrix products, arithmetic and copies ran while one was open for 1% -> 1% of each run, Pallas kernels for 46% -> 44%
where the time goes in v5:
time: 115 us; the launch traced here: 114 us
  Pallas kernels  65.6 us (57%)
  waiting for transfers between devices  24.9 us (22%)
  starting transfers between devices  19.6 us (17%)
  other arithmetic  2.59 us (2%)
    pallas_call x5, Pallas kernels, backward(): pl.pallas_call(functools.partial(backward_kernel, dims, len(pairs), len(p...  33.8 us
    pallas_call x4, Pallas kernels, forward(): pl.pallas_call(functools.partial(forward_kernel, dims, len(pairs), first,...  23.2 us
    ppermute x5, waiting for transfers between devices, from_far(): lax.ppermute(x, 'seq', [(i, (i + shift * near) % seqs) for i in range(seq...  19.7 us
    ppermute x5, starting transfers between devices, from_far(): lax.ppermute(x, 'seq', [(i, (i + shift * near) % seqs) for i in range(seq...  10.6 us
    ppermute x7, starting transfers between devices, from_near(): return lax.ppermute(x, ('half', 'seq'), pairs)  8.96 us
    pallas_call x1, Pallas kernels, project(): pl.pallas_call(project_kernel, grid=(rows // block,), in_specs=[pl.BlockS...  8.25 us
    ppermute x7, waiting for transfers between devices, from_near(): return lax.ppermute(x, ('half', 'seq'), pairs)  5.21 us
    convert_element_type x3, other arithmetic, total(): return sum((x.astype(f32) for x in arrays)).astype(bf16)  2.59 us
  transfers between devices with their start and end apart: 12, of which 6 were waited for; matrix products, arithmetic and copies ran while one was open for 1% of the time, Pallas kernels for 44%

profile of v5, /device:TPU:0, one launch (start us, length us, event | category | flops | bytes accessed | tf_op | source)
XLA Modules:
  0.0 114.5 jit_solution(10515538524938408729)
XLA Ops:
  0.6 4.1 %collective-permute-start = (bf16[128,1024]{1,0:T(8,128)(2,1)}, bf16[128,1024]{1,0:T(8,128)(2,1)S(1)}, u32[]{:S(2)}, u32[]{:S(2)}) collective-permute-start(bf16[128,1024]{1,0:T(8,128)(2,1)} %refs_0_.2), channel_id=1, source_target_pairs={{0,8},{4,12},{8,0},{12,4},{1,9},{5,13},{9,1},{13,5},{2,10},{6,14},... | collective-permute-start | bytes 786440 | tf_op jit(solution)/shard_map/ppermute | solution.py:399
  4.8 8.2 %project.1.refs_1_.refs_2_ = bf16[2,1024,128]{2,1,0:T(8,128)(2,1)} custom-call(bf16[1024,4096]{1,0:T(8,128)(2,1)} %x_ref.1, f32[1,4096]{1,0:T(1,128)} %bitcast.1, bf16[4096,256]{1,0:T(8,128)(2,1)} %w_ref.1), custom_call_target="tpu_custom_call" | custom-call | flops 2147483648 | bytes 8388608 | tf_op jit(solution)/shard_map/project/pallas_call | solution.py:40
  13.0 1.6 %collective-permute-start.2 = (bf16[2,1024,128]{2,1,0:T(8,128)(2,1)}, bf16[2,1024,128]{2,1,0:T(8,128)(2,1)S(1)}, u32[]{:S(2)}, u32[]{:S(2)}) collective-permute-start(bf16[2,1024,128]{2,1,0:T(8,128)(2,1)} %project.1.refs_1_.refs_2_), channel_id=1, source_target_pairs={{0,4},{4,0},{8,12},{12,8},{16,20},{20,16},{24,28},{28,24},{1,5},{5... | collective-permute-start | bytes 1572872 | tf_op jit(solution)/shard_map/ppermute | solution.py:407
  14.6 1.5 %collective-permute-start.1 = (bf16[2,1024,128]{2,1,0:T(8,128)(2,1)}, bf16[2,1024,128]{2,1,0:T(8,128)(2,1)S(1)}, u32[]{:S(2)}, u32[]{:S(2)}) collective-permute-start(bf16[2,1024,128]{2,1,0:T(8,128)(2,1)} %project.1.refs_1_.refs_2_), channel_id=1, source_target_pairs={{0,16},{4,20},{8,24},{12,28},{16,0},{20,4},{24,8},{28,12},{1,17},{... | collective-permute-start | bytes 1572872 | tf_op jit(solution)/shard_map/ppermute | solution.py:407
  17.2 1.0 copy-done
  18.2 5.6 %forward.4 = (bf16[8,1024,512]{2,1,0:T(8,128)(2,1)S(1)}, f32[8,512]{1,0:T(8,128)S(1)}, f32[2,8,512]{2,1,0:T(8,128)S(1)}, f32[8,64,512]{2,1,0:T(8,128)S(1)}) custom-call(bf16[8,64,512]{2,1,0:T(8,128)(2,1)S(1)} %turn.2.refs_0_, bf16[2,1024,128]{2,1,0:T(8,128)(2,1)S(1)} %copy-done), custom_call_target="tpu_custom_call" | custom-call | flops 4294967296 | bytes 8388608 | tf_op jit(solution)/shard_map/forward/pallas_call | solution.py:180
  23.9 4.3 %collective-permute-done.2.refs_1_.refs_2_ = bf16[2,1024,128]{2,1,0:T(8,128)(2,1)S(1)} collective-permute-done((bf16[2,1024,128]{2,1,0:T(8,128)(2,1)}, bf16[2,1024,128]{2,1,0:T(8,128)(2,1)S(1)}, u32[]{:S(2)}, u32[]{:S(2)}) %collective-permute-start.2) | collective-permute-done | bytes 524320 | tf_op jit(solution)/shard_map/ppermute | solution.py:407
  28.2 1.6 %collective-permute-start.4 = (bf16[2,512,128]{2,1,0:T(8,128)(2,1)S(1)}, bf16[2,512,128]{2,1,0:T(8,128)(2,1)S(1)}, u32[]{:S(2)}, u32[]{:S(2)}) collective-permute-start(bf16[2,512,128]{2,1,0:T(8,128)(2,1)S(1)} %slice.8), channel_id=1, source_target_pairs={{0,16},{4,20},{8,24},{12,28},{16,0},{20,4},{24,8},{28,12},{1,17},{... | collective-permute-start | bytes 786440 | tf_op jit(solution)/shard_map/ppermute | solution.py:407
  29.9 4.0 %collective-permute-start.3 = (bf16[128,1024]{1,0:T(8,128)(2,1)S(1)}, bf16[128,1024]{1,0:T(8,128)(2,1)S(1)}, u32[]{:S(2)}, u32[]{:S(2)}) collective-permute-start(bf16[128,1024]{1,0:T(8,128)(2,1)S(1)} %copy-done.3), channel_id=1, source_target_pairs={{0,8},{4,12},{8,0},{12,4},{1,9},{5,13},{9,1},{13,5},{2,10},{6,14},... | collective-permute-start | bytes 786440 | tf_op jit(solution)/shard_map/ppermute | solution.py:399
  33.9 5.7 %forward.5 = (bf16[8,1024,512]{2,1,0:T(8,128)(2,1)S(1)}, f32[8,512]{1,0:T(8,128)S(1)}, f32[2,8,512]{2,1,0:T(8,128)S(1)}, f32[8,64,512]{2,1,0:T(8,128)S(1)}) custom-call(bf16[8,64,512]{2,1,0:T(8,128)(2,1)S(1)} %turn.2.refs_0_, bf16[2,1024,128]{2,1,0:T(8,128)(2,1)S(1)} %collective-permute-done.1.refs_1_.refs_2_, f32[2,8,512]{2,1,0:T(8,128)S(1)} %get-tuple-element.34.refs_2_, ...), custom_call_target="tpu_custom_call" | custom-call | flops 4294967296 | bytes 8388608 | tf_op jit(solution)/shard_map/forward/pallas_call | solution.py:180
  39.7 5.7 %forward.6 = (bf16[8,1024,512]{2,1,0:T(8,128)(2,1)S(1)}, f32[8,512]{1,0:T(8,128)S(1)}, f32[2,8,512]{2,1,0:T(8,128)S(1)}, f32[8,64,512]{2,1,0:T(8,128)S(1)}) custom-call(bf16[8,64,512]{2,1,0:T(8,128)(2,1)S(1)} %turn.2.refs_0_, bf16[2,1024,128]{2,1,0:T(8,128)(2,1)S(1)} %collective-permute-done.2.refs_1_.refs_2_, f32[2,8,512]{2,1,0:T(8,128)S(1)} %get-tuple-element.36.refs_2_, ...), custom_call_target="tpu_custom_call" | custom-call | flops 4294967296 | bytes 8388608 | tf_op jit(solution)/shard_map/forward/pallas_call | solution.py:180
  45.7 6.1 %forward.7 = (bf16[8,1024,512]{2,1,0:T(8,128)(2,1)S(1)}, f32[8,512]{1,0:T(8,128)S(1)}, f32[3,8,512]{2,1,0:T(8,128)S(1)}, f32[8,64,512]{2,1,0:T(8,128)S(1)}) custom-call(bf16[8,64,512]{2,1,0:T(8,128)(2,1)S(1)} %turn.2.refs_0_, bf16[8,64,512]{2,1,0:T(8,128)(2,1)S(1)} %turn.3.refs_1_, bf16[2,512,128]{2,1,0:T(8,128)(2,1)S(1)} %collective-permute-done.4.refs_2_, ...), custom_call_target="tpu_custom_call" | custom-call | flops 4294967296 | bytes 8388608 | tf_op jit(solution)/shard_map/forward/pallas_call | solution.py:180
  51.9 5.3 %collective-permute-done.6.refs_7_.refs_6_ = f32[3,8,512]{2,1,0:T(8,128)S(1)} collective-permute-done((f32[3,8,512]{2,1,0:T(8,128)S(1)}, f32[3,8,512]{2,1,0:T(8,128)S(1)}, u32[]{:S(2)}, u32[]{:S(2)}) %collective-permute-start.6) | collective-permute-done | bytes 49184 | tf_op jit(solution)/shard_map/ppermute | solution.py:399
  57.1 9.1 %backward.5 = (bf16[128,1024]{1,0:T(8,128)(2,1)S(1)}, bf16[128,1024]{1,0:T(8,128)(2,1)S(1)}, f32[8,64,512]{2,1,0:T(8,128)S(1)}, bf16[1024,256]{1,0:T(8,128)(2,1)S(1)}) custom-call(bf16[8,64,512]{2,1,0:T(8,128)(2,1)S(1)} %turn.2.refs_0_, bf16[8,64,512]{2,1,0:T(8,128)(2,1)S(1)} %turn.3.refs_1_, bf16[2,512,128]{2,1,0:T(8,128)(2,1)S(1)} %collective-permute-done.4.refs_2_, ...), custom_call_target="tpu_custom_call" | custom-call | flops 6442450944 | bytes 8388608 | tf_op jit(solution)/shard_map/backward/pallas_call | solution.py:360
  66.3 8.3 %backward.6 = (f32[8,64,512]{2,1,0:T(8,128)S(1)}, bf16[1024,256]{1,0:T(8,128)(2,1)S(1)}) custom-call(bf16[8,64,512]{2,1,0:T(8,128)(2,1)S(1)} %turn.2.refs_0_, bf16[8,64,512]{2,1,0:T(8,128)(2,1)S(1)} %turn.3.refs_1_, bf16[2,1024,128]{2,1,0:T(8,128)(2,1)S(1)} %collective-permute-done.2.refs_1_.refs_2_, bf16[8,1024,512]{2,1,0:T(8,128)(2,1)S(1)} %get-tuple-element.50.refs_3_, ...), custom_call_target="tpu_custom_call" | custom-call | flops 6442450944 | bytes 8388608 | tf_op jit(solution)/shard_map/backward/pallas_call | solution.py:360
  74.6 8.5 %backward.7 = (f32[8,64,512]{2,1,0:T(8,128)S(1)}, bf16[1024,256]{1,0:T(8,128)(2,1)S(1)}) custom-call(bf16[8,64,512]{2,1,0:T(8,128)(2,1)S(1)} %turn.2.refs_0_, bf16[8,64,512]{2,1,0:T(8,128)(2,1)S(1)} %turn.3.refs_1_, bf16[2,1024,128]{2,1,0:T(8,128)(2,1)S(1)} %collective-permute-done.1.refs_1_.refs_2_, bf16[8,1024,512]{2,1,0:T(8,128)(2,1)S(1)} %get-tuple-element.48.refs_3_, ...), custom_call_target="tpu_custom_call" | custom-call | flops 6442450944 | bytes 8388608 | tf_op jit(solution)/shard_map/backward/pallas_call | solution.py:360
  83.6 2.7 %collective-permute-start.10 = (bf16[1024,256]{1,0:T(8,128)(2,1)S(1)}, bf16[1024,256]{1,0:T(8,128)(2,1)S(1)}, u32[]{:S(2)}, u32[]{:S(2)}) collective-permute-start(bf16[1024,256]{1,0:T(8,128)(2,1)S(1)} %get-tuple-element.60), channel_id=1, source_target_pairs={{0,4},{4,0},{8,12},{12,8},{16,20},{20,16},{24,28},{28,24},{1,5},{5... | collective-permute-start | bytes 1572872 | tf_op jit(solution)/shard_map/ppermute | solution.py:407
  86.3 0.9 collective-permute-start.9
  87.3 3.9 %backward.8 = (bf16[128,1024]{1,0:T(8,128)(2,1)S(1)}, f32[2,64,1024]{2,1,0:T(8,128)S(1)}, f32[2,64,1024]{2,1,0:T(8,128)S(1)}) custom-call(bf16[8,64,512]{2,1,0:T(8,128)(2,1)S(1)} %turn.2.refs_0_, bf16[8,64,512]{2,1,0:T(8,128)(2,1)S(1)} %turn.3.refs_1_, bf16[2,1024,128]{2,1,0:T(8,128)(2,1)S(1)} %copy-done.1, ...), custom_call_target="tpu_custom_call" | custom-call | flops 3221225472 | bytes 4194304 | tf_op jit(solution)/shard_map/backward/pallas_call | solution.py:360
  91.2 2.3 %collective-permute-start.8 = (bf16[128,1024]{1,0:T(8,128)(2,1)S(1)}, bf16[128,1024]{1,0:T(8,128)(2,1)S(1)}, u32[]{:S(2)}, u32[]{:S(2)}) collective-permute-start(bf16[128,1024]{1,0:T(8,128)(2,1)S(1)} %get-tuple-element.58), channel_id=1, source_target_pairs={{0,8},{4,12},{8,0},{12,4},{1,9},{5,13},{9,1},{13,5},{2,10},{6,14},... | collective-permute-start | bytes 786440 | tf_op jit(solution)/shard_map/ppermute | solution.py:399
  93.5 4.1 %backward.9 = (bf16[128,1024]{1,0:T(8,128)(2,1)S(1)}, bf16[1024,256]{1,0:T(8,128)(2,1)S(1)}) custom-call(bf16[8,64,512]{2,1,0:T(8,128)(2,1)S(1)} %turn.2.refs_0_, bf16[8,64,512]{2,1,0:T(8,128)(2,1)S(1)} %turn.3.refs_1_, bf16[2,1024,128]{2,1,0:T(8,128)(2,1)S(1)} %copy-done.1, bf16[8,1024,512]{2,1,0:T(8,128)(2,1)S(1)} %get-tuple-element.46.refs_3_, ...), custom_call_target="tpu_custom_call" | custom-call | flops 3221225472 | bytes 4194304 | tf_op jit(solution)/shard_map/backward/pallas_call | solution.py:360
  98.4 13.4 %collective-permute-done.8 = bf16[128,1024]{1,0:T(8,128)(2,1)S(1)} collective-permute-done((bf16[128,1024]{1,0:T(8,128)(2,1)S(1)}, bf16[128,1024]{1,0:T(8,128)(2,1)S(1)}, u32[]{:S(2)}, u32[]{:S(2)}) %collective-permute-start.8) | collective-permute-done | bytes 262176 | tf_op jit(solution)/shard_map/ppermute | solution.py:399
  112.5 0.9 collective-permute-done.9
  113.4 1.1 add_convert_fusion
  (25 shorter events, 3.8 us)
Async XLA Ops:
  0.6 16.4 %copy-start.2 = (bf16[128,1024]{1,0:T(8,128)(2,1)S(1)}, bf16[128,1024]{1,0:T(8,128)(2,1)}, u32[]{:S(2)}) copy-start(bf16[128,1024]{1,0:T(8,128)(2,1)} %refs_0_.2) | copy-start | bytes 786436
  0.6 16.4 %collective-permute-start = (bf16[128,1024]{1,0:T(8,128)(2,1)}, bf16[128,1024]{1,0:T(8,128)(2,1)S(1)}, u32[]{:S(2)}, u32[]{:S(2)}) collective-permute-start(bf16[128,1024]{1,0:T(8,128)(2,1)} %refs_0_.2), channel_id=1, source_target_pairs={{0,8},{4,12},{8,0},{12,4},{1,9},{5,13},{9,1},{13,5},{2,10},{6,14},... | collective-permute-start | bytes 786440 | tf_op jit(solution)/shard_map/ppermute | solution.py:399
  13.0 15.1 %collective-permute-start.2 = (bf16[2,1024,128]{2,1,0:T(8,128)(2,1)}, bf16[2,1024,128]{2,1,0:T(8,128)(2,1)S(1)}, u32[]{:S(2)}, u32[]{:S(2)}) collective-permute-start(bf16[2,1024,128]{2,1,0:T(8,128)(2,1)} %project.1.refs_1_.refs_2_), channel_id=1, source_target_pairs={{0,4},{4,0},{8,12},{12,8},{16,20},{20,16},{24,28},{28,24},{1,5},{5... | collective-permute-start | bytes 1572872 | tf_op jit(solution)/shard_map/ppermute | solution.py:407
  14.6 15.2 %collective-permute-start.1 = (bf16[2,1024,128]{2,1,0:T(8,128)(2,1)}, bf16[2,1024,128]{2,1,0:T(8,128)(2,1)S(1)}, u32[]{:S(2)}, u32[]{:S(2)}) collective-permute-start(bf16[2,1024,128]{2,1,0:T(8,128)(2,1)} %project.1.refs_1_.refs_2_), channel_id=1, source_target_pairs={{0,16},{4,20},{8,24},{12,28},{16,0},{20,4},{24,8},{28,12},{1,17},{... | collective-permute-start | bytes 1572872 | tf_op jit(solution)/shard_map/ppermute | solution.py:407
  17.2 1.0 copy-start
  18.2 11.6 %copy-start.3 = (bf16[128,1024]{1,0:T(8,128)(2,1)S(1)}, bf16[128,1024]{1,0:T(8,128)(2,1)}, u32[]{:S(2)}) copy-start(bf16[128,1024]{1,0:T(8,128)(2,1)} %refs_0_.3) | copy-start | bytes 786436
  28.2 17.5 %collective-permute-start.4 = (bf16[2,512,128]{2,1,0:T(8,128)(2,1)S(1)}, bf16[2,512,128]{2,1,0:T(8,128)(2,1)S(1)}, u32[]{:S(2)}, u32[]{:S(2)}) collective-permute-start(bf16[2,512,128]{2,1,0:T(8,128)(2,1)S(1)} %slice.8), channel_id=1, source_target_pairs={{0,16},{4,20},{8,24},{12,28},{16,0},{20,4},{24,8},{28,12},{1,17},{... | collective-permute-start | bytes 786440 | tf_op jit(solution)/shard_map/ppermute | solution.py:407
  29.8 15.9 %collective-permute-start.5 = (bf16[2,512,128]{2,1,0:T(8,128)(2,1)S(1)}, bf16[2,512,128]{2,1,0:T(8,128)(2,1)S(1)}, u32[]{:S(2)}, u32[]{:S(2)}) collective-permute-start(bf16[2,512,128]{2,1,0:T(8,128)(2,1)S(1)} %slice.9), channel_id=1, source_target_pairs={{0,4},{4,0},{8,12},{12,8},{16,20},{20,16},{24,28},{28,24},{1,5},{5... | collective-permute-start | bytes 786440 | tf_op jit(solution)/shard_map/ppermute | solution.py:407
  29.9 15.6 %collective-permute-start.3 = (bf16[128,1024]{1,0:T(8,128)(2,1)S(1)}, bf16[128,1024]{1,0:T(8,128)(2,1)S(1)}, u32[]{:S(2)}, u32[]{:S(2)}) collective-permute-start(bf16[128,1024]{1,0:T(8,128)(2,1)S(1)} %copy-done.3), channel_id=1, source_target_pairs={{0,8},{4,12},{8,0},{12,4},{1,9},{5,13},{9,1},{13,5},{2,10},{6,14},... | collective-permute-start | bytes 786440 | tf_op jit(solution)/shard_map/ppermute | solution.py:399
  51.8 5.4 %collective-permute-start.6 = (f32[3,8,512]{2,1,0:T(8,128)S(1)}, f32[3,8,512]{2,1,0:T(8,128)S(1)}, u32[]{:S(2)}, u32[]{:S(2)}) collective-permute-start(f32[3,8,512]{2,1,0:T(8,128)S(1)} %get-tuple-element.42.refs_6_.refs_5_), channel_id=1, source_target_pairs={{0,8},{4,12},{8,0},{12,4},{1,9},{5,13},{9,1},{13,5},{2,10},{6,14},... | collective-permute-start | bytes 147464 | tf_op jit(solution)/shard_map/ppermute | solution.py:399
  66.2 31.4 %collective-permute-start.7 = (bf16[128,1024]{1,0:T(8,128)(2,1)S(1)}, bf16[128,1024]{1,0:T(8,128)(2,1)S(1)}, u32[]{:S(2)}, u32[]{:S(2)}) collective-permute-start(bf16[128,1024]{1,0:T(8,128)(2,1)S(1)} %get-tuple-element.45), channel_id=1, source_target_pairs={{0,8},{4,12},{8,0},{12,4},{1,9},{5,13},{9,1},{13,5},{2,10},{6,14},... | collective-permute-start | bytes 786440 | tf_op jit(solution)/shard_map/ppermute | solution.py:399
  74.6 12.7 %copy-start.1 = (bf16[2,1024,128]{2,1,0:T(8,128)(2,1)S(1)}, bf16[2,1024,128]{2,1,0:T(8,128)(2,1)}, u32[]{:S(2)}) copy-start(bf16[2,1024,128]{2,1,0:T(8,128)(2,1)} %project.1.refs_1_.refs_2_) | copy-start | bytes 1572868
  83.0 29.5 %collective-permute-start.11 = (bf16[1024,256]{1,0:T(8,128)(2,1)S(1)}, bf16[1024,256]{1,0:T(8,128)(2,1)S(1)}, u32[]{:S(2)}, u32[]{:S(2)}) collective-permute-start(bf16[1024,256]{1,0:T(8,128)(2,1)S(1)} %get-tuple-element.61), channel_id=1, source_target_pairs={{0,16},{4,20},{8,24},{12,28},{16,0},{20,4},{24,8},{28,12},{1,17},{... | collective-permute-start | bytes 1572872 | tf_op jit(solution)/shard_map/ppermute | solution.py:407
  83.6 28.9 %collective-permute-start.10 = (bf16[1024,256]{1,0:T(8,128)(2,1)S(1)}, bf16[1024,256]{1,0:T(8,128)(2,1)S(1)}, u32[]{:S(2)}, u32[]{:S(2)}) collective-permute-start(bf16[1024,256]{1,0:T(8,128)(2,1)S(1)} %get-tuple-element.60), channel_id=1, source_target_pairs={{0,4},{4,0},{8,12},{12,8},{16,20},{20,16},{24,28},{28,24},{1,5},{5... | collective-permute-start | bytes 1572872 | tf_op jit(solution)/shard_map/ppermute | solution.py:407
  86.3 27.1 %collective-permute-start.9 = (bf16[1024,256]{1,0:T(8,128)(2,1)S(1)}, bf16[1024,256]{1,0:T(8,128)(2,1)S(1)}, u32[]{:S(2)}, u32[]{:S(2)}) collective-permute-start(bf16[1024,256]{1,0:T(8,128)(2,1)S(1)} %get-tuple-element.59), channel_id=1, source_target_pairs={{0,20},{4,16},{8,28},{12,24},{16,4},{20,0},{24,12},{28,8},{1,21},{... | collective-permute-start | bytes 1572872 | tf_op jit(solution)/shard_map/ppermute | solution.py:407
  91.2 20.5 %collective-permute-start.8 = (bf16[128,1024]{1,0:T(8,128)(2,1)S(1)}, bf16[128,1024]{1,0:T(8,128)(2,1)S(1)}, u32[]{:S(2)}, u32[]{:S(2)}) collective-permute-start(bf16[128,1024]{1,0:T(8,128)(2,1)S(1)} %get-tuple-element.58), channel_id=1, source_target_pairs={{0,8},{4,12},{8,0},{12,4},{1,9},{5,13},{9,1},{13,5},{2,10},{6,14},... | collective-permute-start | bytes 786440 | tf_op jit(solution)/shard_map/ppermute | solution.py:399

commit v6 on v5

--- a/solution.py
+++ b/solution.py
@@ -36,7 +36,7 @@
 def project(states, gain, weight):
     rows, width = states.shape
     groups = weight.shape[1] // (2 * HD)
-    block = min(rows, 256)
+    block = min(rows, 512)
     return pl.pallas_call(
         project_kernel,
         grid=(rows // block,),
@@ -47,7 +47,7 @@
         ],
         out_specs=pl.BlockSpec((groups, block, 2 * HD), lambda i: (0, i, 0)),
         out_shape=jax.ShapeDtypeStruct((groups, rows, 2 * HD), bf16),
-        compiler_params=pltpu.CompilerParams(vmem_limit_bytes=60 << 20),
+        compiler_params=pltpu.CompilerParams(vmem_limit_bytes=57 << 20),
         cost_estimate=pl.CostEstimate(
             flops=2 * rows * width * weight.shape[1], bytes_accessed=2 * rows * width, transcendentals=0
         ),
@@ -420,7 +420,7 @@
             blocks[a, b] = [from_near(along[:, :middle], a, 0), upper]
         else:
             blocks[a, b] = [from_near(own_pairs, a, b)]
-    c_own, *_ = lax.optimization_barrier((cotangent, *[blocks[s][0] for s in order[1:3]]))
+    c_own, *_ = lax.optimization_barrier((cotangent, *[blocks[s][0] for s in order[1:2]]))
     c_blocks = [cotangent] + [from_far(c_own, s) for s in range(1, fars)]
     pair_blocks = [blocks[s] for s in order]
     count = len(order)
@@ -456,8 +456,8 @@
         return sum(x.astype(f32) for x in arrays).astype(bf16)
 
     context = total([context_parts[0]] + [from_far(context_parts[s], -s) for s in range(1, fars)])
+    d_pairs = total(sends)
     d_queries = total([stay, *away])
-    d_pairs = total(sends)
     return (context, d_queries, d_pairs)
 
 

time: 115 us -> 115 us (level)
  no operation moved by 1% of the time
where the time goes in v6:
time: 115 us; the launch traced here: 114 us
  Pallas kernels  65.2 us (57%)
  waiting for transfers between devices  25.3 us (22%)
  starting transfers between devices  19.6 us (17%)
  other arithmetic  2.59 us (2%)
    pallas_call x5, Pallas kernels, backward(): pl.pallas_call(functools.partial(backward_kernel, dims, len(pairs), len(p...  33.8 us
    pallas_call x4, Pallas kernels, forward(): pl.pallas_call(functools.partial(forward_kernel, dims, len(pairs), first,...  23.1 us
    ppermute x5, waiting for transfers between devices, from_far(): lax.ppermute(x, 'seq', [(i, (i + shift * near) % seqs) for i in range(seq...  20.1 us
    ppermute x5, starting transfers between devices, from_far(): lax.ppermute(x, 'seq', [(i, (i + shift * near) % seqs) for i in range(seq...  10.6 us
    ppermute x7, starting transfers between devices, from_near(): return lax.ppermute(x, ('half', 'seq'), pairs)  8.96 us
    pallas_call x1, Pallas kernels, project(): pl.pallas_call(project_kernel, grid=(rows // block,), in_specs=[pl.BlockS...  7.85 us
    ppermute x7, waiting for transfers between devices, from_near(): return lax.ppermute(x, ('half', 'seq'), pairs)  5.2 us
    convert_element_type x3, other arithmetic, total(): return sum((x.astype(f32) for x in arrays)).astype(bf16)  2.59 us
  transfers between devices with their start and end apart: 12, of which 6 were waited for; matrix products, arithmetic and copies ran while one was open for 1% of the time, Pallas kernels for 44%

profile of v6, /device:TPU:0, one launch (start us, length us, event | category | flops | bytes accessed | tf_op | source)
XLA Modules:
  0.0 114.5 jit_solution(7706262396396690393)
XLA Ops:
  0.6 4.1 %collective-permute-start = (bf16[128,1024]{1,0:T(8,128)(2,1)}, bf16[128,1024]{1,0:T(8,128)(2,1)S(1)}, u32[]{:S(2)}, u32[]{:S(2)}) collective-permute-start(bf16[128,1024]{1,0:T(8,128)(2,1)} %refs_0_.2), channel_id=1, source_target_pairs={{0,8},{4,12},{8,0},{12,4},{1,9},{5,13},{9,1},{13,5},{2,10},{6,14},... | collective-permute-start | bytes 786440 | tf_op jit(solution)/shard_map/ppermute | solution.py:399
  4.8 7.9 %project.1.refs_1_.refs_2_ = bf16[2,1024,128]{2,1,0:T(8,128)(2,1)} custom-call(bf16[1024,4096]{1,0:T(8,128)(2,1)} %x_ref.1, f32[1,4096]{1,0:T(1,128)} %bitcast.1, bf16[4096,256]{1,0:T(8,128)(2,1)} %w_ref.1), custom_call_target="tpu_custom_call" | custom-call | flops 2147483648 | bytes 8388608 | tf_op jit(solution)/shard_map/project/pallas_call | solution.py:40
  12.6 1.6 %collective-permute-start.3 = (bf16[2,1024,128]{2,1,0:T(8,128)(2,1)}, bf16[2,1024,128]{2,1,0:T(8,128)(2,1)S(1)}, u32[]{:S(2)}, u32[]{:S(2)}) collective-permute-start(bf16[2,1024,128]{2,1,0:T(8,128)(2,1)} %project.1.refs_1_.refs_2_), channel_id=1, source_target_pairs={{0,4},{4,0},{8,12},{12,8},{16,20},{20,16},{24,28},{28,24},{1,5},{5... | collective-permute-start | bytes 1572872 | tf_op jit(solution)/shard_map/ppermute | solution.py:407
  14.2 1.5 %collective-permute-start.1 = (bf16[2,1024,128]{2,1,0:T(8,128)(2,1)}, bf16[2,1024,128]{2,1,0:T(8,128)(2,1)S(1)}, u32[]{:S(2)}, u32[]{:S(2)}) collective-permute-start(bf16[2,1024,128]{2,1,0:T(8,128)(2,1)} %project.1.refs_1_.refs_2_), channel_id=1, source_target_pairs={{0,16},{4,20},{8,24},{12,28},{16,0},{20,4},{24,8},{28,12},{1,17},{... | collective-permute-start | bytes 1572872 | tf_op jit(solution)/shard_map/ppermute | solution.py:407
  15.7 1.3 %collective-permute-done.refs_1_ = bf16[128,1024]{1,0:T(8,128)(2,1)S(1)} collective-permute-done((bf16[128,1024]{1,0:T(8,128)(2,1)}, bf16[128,1024]{1,0:T(8,128)(2,1)S(1)}, u32[]{:S(2)}, u32[]{:S(2)}) %collective-permute-start) | collective-permute-done | bytes 262176 | tf_op jit(solution)/shard_map/ppermute | solution.py:399
  17.2 1.0 copy-done
  18.2 5.6 %forward.4 = (bf16[8,1024,512]{2,1,0:T(8,128)(2,1)S(1)}, f32[8,512]{1,0:T(8,128)S(1)}, f32[2,8,512]{2,1,0:T(8,128)S(1)}, f32[8,64,512]{2,1,0:T(8,128)S(1)}) custom-call(bf16[8,64,512]{2,1,0:T(8,128)(2,1)S(1)} %turn.2.refs_0_, bf16[2,1024,128]{2,1,0:T(8,128)(2,1)S(1)} %copy-done), custom_call_target="tpu_custom_call" | custom-call | flops 4294967296 | bytes 8388608 | tf_op jit(solution)/shard_map/forward/pallas_call | solution.py:180
  23.9 4.3 %collective-permute-done.3.refs_1_.refs_2_ = bf16[2,1024,128]{2,1,0:T(8,128)(2,1)S(1)} collective-permute-done((bf16[2,1024,128]{2,1,0:T(8,128)(2,1)}, bf16[2,1024,128]{2,1,0:T(8,128)(2,1)S(1)}, u32[]{:S(2)}, u32[]{:S(2)}) %collective-permute-start.3) | collective-permute-done | bytes 524320 | tf_op jit(solution)/shard_map/ppermute | solution.py:407
  28.2 1.6 %collective-permute-start.4 = (bf16[2,512,128]{2,1,0:T(8,128)(2,1)S(1)}, bf16[2,512,128]{2,1,0:T(8,128)(2,1)S(1)}, u32[]{:S(2)}, u32[]{:S(2)}) collective-permute-start(bf16[2,512,128]{2,1,0:T(8,128)(2,1)S(1)} %slice.8), channel_id=1, source_target_pairs={{0,16},{4,20},{8,24},{12,28},{16,0},{20,4},{24,8},{28,12},{1,17},{... | collective-permute-start | bytes 786440 | tf_op jit(solution)/shard_map/ppermute | solution.py:407
  29.9 4.0 %collective-permute-start.2 = (bf16[128,1024]{1,0:T(8,128)(2,1)S(1)}, bf16[128,1024]{1,0:T(8,128)(2,1)S(1)}, u32[]{:S(2)}, u32[]{:S(2)}) collective-permute-start(bf16[128,1024]{1,0:T(8,128)(2,1)S(1)} %copy-done.3), channel_id=1, source_target_pairs={{0,8},{4,12},{8,0},{12,4},{1,9},{5,13},{9,1},{13,5},{2,10},{6,14},... | collective-permute-start | bytes 786440 | tf_op jit(solution)/shard_map/ppermute | solution.py:399
  33.9 5.7 %forward.5 = (bf16[8,1024,512]{2,1,0:T(8,128)(2,1)S(1)}, f32[8,512]{1,0:T(8,128)S(1)}, f32[2,8,512]{2,1,0:T(8,128)S(1)}, f32[8,64,512]{2,1,0:T(8,128)S(1)}) custom-call(bf16[8,64,512]{2,1,0:T(8,128)(2,1)S(1)} %turn.2.refs_0_, bf16[2,1024,128]{2,1,0:T(8,128)(2,1)S(1)} %collective-permute-done.1.refs_1_.refs_2_, f32[2,8,512]{2,1,0:T(8,128)S(1)} %get-tuple-element.34.refs_2_, ...), custom_call_target="tpu_custom_call" | custom-call | flops 4294967296 | bytes 8388608 | tf_op jit(solution)/shard_map/forward/pallas_call | solution.py:180
  39.7 5.7 %forward.6 = (bf16[8,1024,512]{2,1,0:T(8,128)(2,1)S(1)}, f32[8,512]{1,0:T(8,128)S(1)}, f32[2,8,512]{2,1,0:T(8,128)S(1)}, f32[8,64,512]{2,1,0:T(8,128)S(1)}) custom-call(bf16[8,64,512]{2,1,0:T(8,128)(2,1)S(1)} %turn.2.refs_0_, bf16[2,1024,128]{2,1,0:T(8,128)(2,1)S(1)} %collective-permute-done.3.refs_1_.refs_2_, f32[2,8,512]{2,1,0:T(8,128)S(1)} %get-tuple-element.36.refs_2_, ...), custom_call_target="tpu_custom_call" | custom-call | flops 4294967296 | bytes 8388608 | tf_op jit(solution)/shard_map/forward/pallas_call | solution.py:180
  45.7 6.1 %forward.7 = (bf16[8,1024,512]{2,1,0:T(8,128)(2,1)S(1)}, f32[8,512]{1,0:T(8,128)S(1)}, f32[3,8,512]{2,1,0:T(8,128)S(1)}, f32[8,64,512]{2,1,0:T(8,128)S(1)}) custom-call(bf16[8,64,512]{2,1,0:T(8,128)(2,1)S(1)} %turn.2.refs_0_, bf16[8,64,512]{2,1,0:T(8,128)(2,1)S(1)} %turn.3.refs_1_, bf16[2,512,128]{2,1,0:T(8,128)(2,1)S(1)} %collective-permute-done.4.refs_2_, ...), custom_call_target="tpu_custom_call" | custom-call | flops 4294967296 | bytes 8388608 | tf_op jit(solution)/shard_map/forward/pallas_call | solution.py:180
  51.9 5.3 %collective-permute-done.6.refs_7_.refs_6_ = f32[3,8,512]{2,1,0:T(8,128)S(1)} collective-permute-done((f32[3,8,512]{2,1,0:T(8,128)S(1)}, f32[3,8,512]{2,1,0:T(8,128)S(1)}, u32[]{:S(2)}, u32[]{:S(2)}) %collective-permute-start.6) | collective-permute-done | bytes 49184 | tf_op jit(solution)/shard_map/ppermute | solution.py:399
  57.1 9.1 %backward.5 = (bf16[128,1024]{1,0:T(8,128)(2,1)S(1)}, bf16[128,1024]{1,0:T(8,128)(2,1)S(1)}, f32[8,64,512]{2,1,0:T(8,128)S(1)}, bf16[1024,256]{1,0:T(8,128)(2,1)S(1)}) custom-call(bf16[8,64,512]{2,1,0:T(8,128)(2,1)S(1)} %turn.2.refs_0_, bf16[8,64,512]{2,1,0:T(8,128)(2,1)S(1)} %turn.3.refs_1_, bf16[2,512,128]{2,1,0:T(8,128)(2,1)S(1)} %collective-permute-done.4.refs_2_, ...), custom_call_target="tpu_custom_call" | custom-call | flops 6442450944 | bytes 8388608 | tf_op jit(solution)/shard_map/backward/pallas_call | solution.py:360
  66.3 8.3 %backward.6 = (f32[8,64,512]{2,1,0:T(8,128)S(1)}, bf16[1024,256]{1,0:T(8,128)(2,1)S(1)}) custom-call(bf16[8,64,512]{2,1,0:T(8,128)(2,1)S(1)} %turn.2.refs_0_, bf16[8,64,512]{2,1,0:T(8,128)(2,1)S(1)} %turn.3.refs_1_, bf16[2,1024,128]{2,1,0:T(8,128)(2,1)S(1)} %collective-permute-done.3.refs_1_.refs_2_, bf16[8,1024,512]{2,1,0:T(8,128)(2,1)S(1)} %get-tuple-element.50.refs_3_, ...), custom_call_target="tpu_custom_call" | custom-call | flops 6442450944 | bytes 8388608 | tf_op jit(solution)/shard_map/backward/pallas_call | solution.py:360
  74.6 8.5 %backward.7 = (f32[8,64,512]{2,1,0:T(8,128)S(1)}, bf16[1024,256]{1,0:T(8,128)(2,1)S(1)}) custom-call(bf16[8,64,512]{2,1,0:T(8,128)(2,1)S(1)} %turn.2.refs_0_, bf16[8,64,512]{2,1,0:T(8,128)(2,1)S(1)} %turn.3.refs_1_, bf16[2,1024,128]{2,1,0:T(8,128)(2,1)S(1)} %collective-permute-done.1.refs_1_.refs_2_, bf16[8,1024,512]{2,1,0:T(8,128)(2,1)S(1)} %get-tuple-element.48.refs_3_, ...), custom_call_target="tpu_custom_call" | custom-call | flops 6442450944 | bytes 8388608 | tf_op jit(solution)/shard_map/backward/pallas_call | solution.py:360
  83.6 2.7 %collective-permute-start.10 = (bf16[1024,256]{1,0:T(8,128)(2,1)S(1)}, bf16[1024,256]{1,0:T(8,128)(2,1)S(1)}, u32[]{:S(2)}, u32[]{:S(2)}) collective-permute-start(bf16[1024,256]{1,0:T(8,128)(2,1)S(1)} %get-tuple-element.60), channel_id=1, source_target_pairs={{0,4},{4,0},{8,12},{12,8},{16,20},{20,16},{24,28},{28,24},{1,5},{5... | collective-permute-start | bytes 1572872 | tf_op jit(solution)/shard_map/ppermute | solution.py:407
  86.3 0.9 collective-permute-start.9
  87.3 3.9 %backward.8 = (bf16[128,1024]{1,0:T(8,128)(2,1)S(1)}, f32[2,64,1024]{2,1,0:T(8,128)S(1)}, f32[2,64,1024]{2,1,0:T(8,128)S(1)}) custom-call(bf16[8,64,512]{2,1,0:T(8,128)(2,1)S(1)} %turn.2.refs_0_, bf16[8,64,512]{2,1,0:T(8,128)(2,1)S(1)} %turn.3.refs_1_, bf16[2,1024,128]{2,1,0:T(8,128)(2,1)S(1)} %copy-done.1, ...), custom_call_target="tpu_custom_call" | custom-call | flops 3221225472 | bytes 4194304 | tf_op jit(solution)/shard_map/backward/pallas_call | solution.py:360
  91.2 2.3 %collective-permute-start.8 = (bf16[128,1024]{1,0:T(8,128)(2,1)S(1)}, bf16[128,1024]{1,0:T(8,128)(2,1)S(1)}, u32[]{:S(2)}, u32[]{:S(2)}) collective-permute-start(bf16[128,1024]{1,0:T(8,128)(2,1)S(1)} %get-tuple-element.58), channel_id=1, source_target_pairs={{0,8},{4,12},{8,0},{12,4},{1,9},{5,13},{9,1},{13,5},{2,10},{6,14},... | collective-permute-start | bytes 786440 | tf_op jit(solution)/shard_map/ppermute | solution.py:399
  93.5 4.1 %backward.9 = (bf16[128,1024]{1,0:T(8,128)(2,1)S(1)}, bf16[1024,256]{1,0:T(8,128)(2,1)S(1)}) custom-call(bf16[8,64,512]{2,1,0:T(8,128)(2,1)S(1)} %turn.2.refs_0_, bf16[8,64,512]{2,1,0:T(8,128)(2,1)S(1)} %turn.3.refs_1_, bf16[2,1024,128]{2,1,0:T(8,128)(2,1)S(1)} %copy-done.1, bf16[8,1024,512]{2,1,0:T(8,128)(2,1)S(1)} %get-tuple-element.46.refs_3_, ...), custom_call_target="tpu_custom_call" | custom-call | flops 3221225472 | bytes 4194304 | tf_op jit(solution)/shard_map/backward/pallas_call | solution.py:360
  98.4 13.4 %collective-permute-done.8 = bf16[128,1024]{1,0:T(8,128)(2,1)S(1)} collective-permute-done((bf16[128,1024]{1,0:T(8,128)(2,1)S(1)}, bf16[128,1024]{1,0:T(8,128)(2,1)S(1)}, u32[]{:S(2)}, u32[]{:S(2)}) %collective-permute-start.8) | collective-permute-done | bytes 262176 | tf_op jit(solution)/shard_map/ppermute | solution.py:399
  113.4 1.1 add_convert_fusion
  (25 shorter events, 3.8 us)
Async XLA Ops:
  0.6 16.4 %copy-start.2 = (bf16[128,1024]{1,0:T(8,128)(2,1)S(1)}, bf16[128,1024]{1,0:T(8,128)(2,1)}, u32[]{:S(2)}) copy-start(bf16[128,1024]{1,0:T(8,128)(2,1)} %refs_0_.2) | copy-start | bytes 786436
  0.6 16.4 %collective-permute-start = (bf16[128,1024]{1,0:T(8,128)(2,1)}, bf16[128,1024]{1,0:T(8,128)(2,1)S(1)}, u32[]{:S(2)}, u32[]{:S(2)}) collective-permute-start(bf16[128,1024]{1,0:T(8,128)(2,1)} %refs_0_.2), channel_id=1, source_target_pairs={{0,8},{4,12},{8,0},{12,4},{1,9},{5,13},{9,1},{13,5},{2,10},{6,14},... | collective-permute-start | bytes 786440 | tf_op jit(solution)/shard_map/ppermute | solution.py:399
  12.6 15.5 %collective-permute-start.3 = (bf16[2,1024,128]{2,1,0:T(8,128)(2,1)}, bf16[2,1024,128]{2,1,0:T(8,128)(2,1)S(1)}, u32[]{:S(2)}, u32[]{:S(2)}) collective-permute-start(bf16[2,1024,128]{2,1,0:T(8,128)(2,1)} %project.1.refs_1_.refs_2_), channel_id=1, source_target_pairs={{0,4},{4,0},{8,12},{12,8},{16,20},{20,16},{24,28},{28,24},{1,5},{5... | collective-permute-start | bytes 1572872 | tf_op jit(solution)/shard_map/ppermute | solution.py:407
  14.2 15.6 %collective-permute-start.1 = (bf16[2,1024,128]{2,1,0:T(8,128)(2,1)}, bf16[2,1024,128]{2,1,0:T(8,128)(2,1)S(1)}, u32[]{:S(2)}, u32[]{:S(2)}) collective-permute-start(bf16[2,1024,128]{2,1,0:T(8,128)(2,1)} %project.1.refs_1_.refs_2_), channel_id=1, source_target_pairs={{0,16},{4,20},{8,24},{12,28},{16,0},{20,4},{24,8},{28,12},{1,17},{... | collective-permute-start | bytes 1572872 | tf_op jit(solution)/shard_map/ppermute | solution.py:407
  17.2 1.0 copy-start
  18.2 11.6 %copy-start.3 = (bf16[128,1024]{1,0:T(8,128)(2,1)S(1)}, bf16[128,1024]{1,0:T(8,128)(2,1)}, u32[]{:S(2)}) copy-start(bf16[128,1024]{1,0:T(8,128)(2,1)} %refs_0_.3) | copy-start | bytes 786436
  28.2 17.5 %collective-permute-start.4 = (bf16[2,512,128]{2,1,0:T(8,128)(2,1)S(1)}, bf16[2,512,128]{2,1,0:T(8,128)(2,1)S(1)}, u32[]{:S(2)}, u32[]{:S(2)}) collective-permute-start(bf16[2,512,128]{2,1,0:T(8,128)(2,1)S(1)} %slice.8), channel_id=1, source_target_pairs={{0,16},{4,20},{8,24},{12,28},{16,0},{20,4},{24,8},{28,12},{1,17},{... | collective-permute-start | bytes 786440 | tf_op jit(solution)/shard_map/ppermute | solution.py:407
  29.8 15.9 %collective-permute-start.5 = (bf16[2,512,128]{2,1,0:T(8,128)(2,1)S(1)}, bf16[2,512,128]{2,1,0:T(8,128)(2,1)S(1)}, u32[]{:S(2)}, u32[]{:S(2)}) collective-permute-start(bf16[2,512,128]{2,1,0:T(8,128)(2,1)S(1)} %slice.9), channel_id=1, source_target_pairs={{0,4},{4,0},{8,12},{12,8},{16,20},{20,16},{24,28},{28,24},{1,5},{5... | collective-permute-start | bytes 786440 | tf_op jit(solution)/shard_map/ppermute | solution.py:407
  29.9 15.6 %collective-permute-start.2 = (bf16[128,1024]{1,0:T(8,128)(2,1)S(1)}, bf16[128,1024]{1,0:T(8,128)(2,1)S(1)}, u32[]{:S(2)}, u32[]{:S(2)}) collective-permute-start(bf16[128,1024]{1,0:T(8,128)(2,1)S(1)} %copy-done.3), channel_id=1, source_target_pairs={{0,8},{4,12},{8,0},{12,4},{1,9},{5,13},{9,1},{13,5},{2,10},{6,14},... | collective-permute-start | bytes 786440 | tf_op jit(solution)/shard_map/ppermute | solution.py:399
  51.8 5.4 %collective-permute-start.6 = (f32[3,8,512]{2,1,0:T(8,128)S(1)}, f32[3,8,512]{2,1,0:T(8,128)S(1)}, u32[]{:S(2)}, u32[]{:S(2)}) collective-permute-start(f32[3,8,512]{2,1,0:T(8,128)S(1)} %get-tuple-element.42.refs_6_.refs_5_), channel_id=1, source_target_pairs={{0,8},{4,12},{8,0},{12,4},{1,9},{5,13},{9,1},{13,5},{2,10},{6,14},... | collective-permute-start | bytes 147464 | tf_op jit(solution)/shard_map/ppermute | solution.py:399
  66.2 31.4 %collective-permute-start.7 = (bf16[128,1024]{1,0:T(8,128)(2,1)S(1)}, bf16[128,1024]{1,0:T(8,128)(2,1)S(1)}, u32[]{:S(2)}, u32[]{:S(2)}) collective-permute-start(bf16[128,1024]{1,0:T(8,128)(2,1)S(1)} %get-tuple-element.45), channel_id=1, source_target_pairs={{0,8},{4,12},{8,0},{12,4},{1,9},{5,13},{9,1},{13,5},{2,10},{6,14},... | collective-permute-start | bytes 786440 | tf_op jit(solution)/shard_map/ppermute | solution.py:399
  74.5 12.7 %copy-start.1 = (bf16[2,1024,128]{2,1,0:T(8,128)(2,1)S(1)}, bf16[2,1024,128]{2,1,0:T(8,128)(2,1)}, u32[]{:S(2)}) copy-start(bf16[2,1024,128]{2,1,0:T(8,128)(2,1)} %project.1.refs_1_.refs_2_) | copy-start | bytes 1572868
  83.0 29.5 %collective-permute-start.11 = (bf16[1024,256]{1,0:T(8,128)(2,1)S(1)}, bf16[1024,256]{1,0:T(8,128)(2,1)S(1)}, u32[]{:S(2)}, u32[]{:S(2)}) collective-permute-start(bf16[1024,256]{1,0:T(8,128)(2,1)S(1)} %get-tuple-element.61), channel_id=1, source_target_pairs={{0,16},{4,20},{8,24},{12,28},{16,0},{20,4},{24,8},{28,12},{1,17},{... | collective-permute-start | bytes 1572872 | tf_op jit(solution)/shard_map/ppermute | solution.py:407
  83.6 28.9 %collective-permute-start.10 = (bf16[1024,256]{1,0:T(8,128)(2,1)S(1)}, bf16[1024,256]{1,0:T(8,128)(2,1)S(1)}, u32[]{:S(2)}, u32[]{:S(2)}) collective-permute-start(bf16[1024,256]{1,0:T(8,128)(2,1)S(1)} %get-tuple-element.60), channel_id=1, source_target_pairs={{0,4},{4,0},{8,12},{12,8},{16,20},{20,16},{24,28},{28,24},{1,5},{5... | collective-permute-start | bytes 1572872 | tf_op jit(solution)/shard_map/ppermute | solution.py:407
  86.3 27.1 %collective-permute-start.9 = (bf16[1024,256]{1,0:T(8,128)(2,1)S(1)}, bf16[1024,256]{1,0:T(8,128)(2,1)S(1)}, u32[]{:S(2)}, u32[]{:S(2)}) collective-permute-start(bf16[1024,256]{1,0:T(8,128)(2,1)S(1)} %get-tuple-element.59), channel_id=1, source_target_pairs={{0,20},{4,16},{8,28},{12,24},{16,4},{20,0},{24,12},{28,8},{1,21},{... | collective-permute-start | bytes 1572872 | tf_op jit(solution)/shard_map/ppermute | solution.py:407
  91.2 20.6 %collective-permute-start.8 = (bf16[128,1024]{1,0:T(8,128)(2,1)S(1)}, bf16[128,1024]{1,0:T(8,128)(2,1)S(1)}, u32[]{:S(2)}, u32[]{:S(2)}) collective-permute-start(bf16[128,1024]{1,0:T(8,128)(2,1)S(1)} %get-tuple-element.58), channel_id=1, source_target_pairs={{0,8},{4,12},{8,0},{12,4},{1,9},{5,13},{9,1},{13,5},{2,10},{6,14},... | collective-permute-start | bytes 786440 | tf_op jit(solution)/shard_map/ppermute | solution.py:399

commit v7 on v6

--- a/solution.py
+++ b/solution.py
@@ -14,6 +14,7 @@
 LOG2E = math.log2(math.e)
 SCALE = HD ** (-0.5)
 KEY_ROWS = 256
+GRAD_ROWS = 256
 VMEM_BYTES = 14 << 20
 NT = (((1,), (1,)), ((), ()))
 
@@ -227,7 +228,7 @@
     kv_ref = gathered(piece_refs, whole_ref)
     length = kv_ref.shape[1]
     lanes = q_ref.shape[2]
-    steps = length // KEY_ROWS
+    steps = length // GRAD_ROWS
     tokens = rows.shape[1]
     heads = lanes // tokens
     pad = jnp.zeros((HD, lanes), bf16)
@@ -284,7 +285,7 @@
             scaled_q = (q_ref[cb].astype(f32) * fb).astype(bf16)
             dq = None
         for k in range(steps):
-            ks = slice(k * KEY_ROWS, (k + 1) * KEY_ROWS)
+            ks = slice(k * GRAD_ROWS, (k + 1) * GRAD_ROWS)
             if cb is not None:
                 ds = score_grad[ks]
                 part = jnp.dot(key_t[gb, :, ks], ds, preferred_element_type=f32)

time: 115 us -> 115 us (level)
  no operation moved by 1% of the time
where the time goes in v7:
time: 115 us; the launch traced here: 114 us
  Pallas kernels  65.2 us (57%)
  waiting for transfers between devices  25.3 us (22%)
  starting transfers between devices  19.6 us (17%)
  other arithmetic  2.59 us (2%)
    pallas_call x5, Pallas kernels, backward(): pl.pallas_call(functools.partial(backward_kernel, dims, len(pairs), len(p...  33.8 us
    pallas_call x4, Pallas kernels, forward(): pl.pallas_call(functools.partial(forward_kernel, dims, len(pairs), first,...  23.1 us
    ppermute x5, waiting for transfers between devices, from_far(): lax.ppermute(x, 'seq', [(i, (i + shift * near) % seqs) for i in range(seq...  20.1 us
    ppermute x5, starting transfers between devices, from_far(): lax.ppermute(x, 'seq', [(i, (i + shift * near) % seqs) for i in range(seq...  10.6 us
    ppermute x7, starting transfers between devices, from_near(): return lax.ppermute(x, ('half', 'seq'), pairs)  8.96 us
    pallas_call x1, Pallas kernels, project(): pl.pallas_call(project_kernel, grid=(rows // block,), in_specs=[pl.BlockS...  7.85 us
    ppermute x7, waiting for transfers between devices, from_near(): return lax.ppermute(x, ('half', 'seq'), pairs)  5.2 us
    convert_element_type x3, other arithmetic, total(): return sum((x.astype(f32) for x in arrays)).astype(bf16)  2.59 us
  transfers between devices with their start and end apart: 12, of which 6 were waited for; matrix products, arithmetic and copies ran while one was open for 1% of the time, Pallas kernels for 44%

profile of v7, /device:TPU:0, one launch (start us, length us, event | category | flops | bytes accessed | tf_op | source)
XLA Modules:
  0.0 114.5 jit_solution(7706262396396690393)
XLA Ops:
  0.6 4.1 %collective-permute-start = (bf16[128,1024]{1,0:T(8,128)(2,1)}, bf16[128,1024]{1,0:T(8,128)(2,1)S(1)}, u32[]{:S(2)}, u32[]{:S(2)}) collective-permute-start(bf16[128,1024]{1,0:T(8,128)(2,1)} %refs_0_.2), channel_id=1, source_target_pairs={{0,8},{4,12},{8,0},{12,4},{1,9},{5,13},{9,1},{13,5},{2,10},{6,14},... | collective-permute-start | bytes 786440 | tf_op jit(solution)/shard_map/ppermute | solution.py:400
  4.8 7.9 %project.1.refs_1_.refs_2_ = bf16[2,1024,128]{2,1,0:T(8,128)(2,1)} custom-call(bf16[1024,4096]{1,0:T(8,128)(2,1)} %x_ref.1, f32[1,4096]{1,0:T(1,128)} %bitcast.1, bf16[4096,256]{1,0:T(8,128)(2,1)} %w_ref.1), custom_call_target="tpu_custom_call" | custom-call | flops 2147483648 | bytes 8388608 | tf_op jit(solution)/shard_map/project/pallas_call | solution.py:41
  12.6 1.6 %collective-permute-start.3 = (bf16[2,1024,128]{2,1,0:T(8,128)(2,1)}, bf16[2,1024,128]{2,1,0:T(8,128)(2,1)S(1)}, u32[]{:S(2)}, u32[]{:S(2)}) collective-permute-start(bf16[2,1024,128]{2,1,0:T(8,128)(2,1)} %project.1.refs_1_.refs_2_), channel_id=1, source_target_pairs={{0,4},{4,0},{8,12},{12,8},{16,20},{20,16},{24,28},{28,24},{1,5},{5... | collective-permute-start | bytes 1572872 | tf_op jit(solution)/shard_map/ppermute | solution.py:408
  14.2 1.5 %collective-permute-start.1 = (bf16[2,1024,128]{2,1,0:T(8,128)(2,1)}, bf16[2,1024,128]{2,1,0:T(8,128)(2,1)S(1)}, u32[]{:S(2)}, u32[]{:S(2)}) collective-permute-start(bf16[2,1024,128]{2,1,0:T(8,128)(2,1)} %project.1.refs_1_.refs_2_), channel_id=1, source_target_pairs={{0,16},{4,20},{8,24},{12,28},{16,0},{20,4},{24,8},{28,12},{1,17},{... | collective-permute-start | bytes 1572872 | tf_op jit(solution)/shard_map/ppermute | solution.py:408
  15.7 1.3 %collective-permute-done.refs_1_ = bf16[128,1024]{1,0:T(8,128)(2,1)S(1)} collective-permute-done((bf16[128,1024]{1,0:T(8,128)(2,1)}, bf16[128,1024]{1,0:T(8,128)(2,1)S(1)}, u32[]{:S(2)}, u32[]{:S(2)}) %collective-permute-start) | collective-permute-done | bytes 262176 | tf_op jit(solution)/shard_map/ppermute | solution.py:400
  17.2 1.0 copy-done
  18.2 5.6 %forward.4 = (bf16[8,1024,512]{2,1,0:T(8,128)(2,1)S(1)}, f32[8,512]{1,0:T(8,128)S(1)}, f32[2,8,512]{2,1,0:T(8,128)S(1)}, f32[8,64,512]{2,1,0:T(8,128)S(1)}) custom-call(bf16[8,64,512]{2,1,0:T(8,128)(2,1)S(1)} %turn.2.refs_0_, bf16[2,1024,128]{2,1,0:T(8,128)(2,1)S(1)} %copy-done), custom_call_target="tpu_custom_call" | custom-call | flops 4294967296 | bytes 8388608 | tf_op jit(solution)/shard_map/forward/pallas_call | solution.py:181
  23.9 4.3 %collective-permute-done.3.refs_1_.refs_2_ = bf16[2,1024,128]{2,1,0:T(8,128)(2,1)S(1)} collective-permute-done((bf16[2,1024,128]{2,1,0:T(8,128)(2,1)}, bf16[2,1024,128]{2,1,0:T(8,128)(2,1)S(1)}, u32[]{:S(2)}, u32[]{:S(2)}) %collective-permute-start.3) | collective-permute-done | bytes 524320 | tf_op jit(solution)/shard_map/ppermute | solution.py:408
  28.2 1.6 %collective-permute-start.4 = (bf16[2,512,128]{2,1,0:T(8,128)(2,1)S(1)}, bf16[2,512,128]{2,1,0:T(8,128)(2,1)S(1)}, u32[]{:S(2)}, u32[]{:S(2)}) collective-permute-start(bf16[2,512,128]{2,1,0:T(8,128)(2,1)S(1)} %slice.8), channel_id=1, source_target_pairs={{0,16},{4,20},{8,24},{12,28},{16,0},{20,4},{24,8},{28,12},{1,17},{... | collective-permute-start | bytes 786440 | tf_op jit(solution)/shard_map/ppermute | solution.py:408
  29.9 4.0 %collective-permute-start.2 = (bf16[128,1024]{1,0:T(8,128)(2,1)S(1)}, bf16[128,1024]{1,0:T(8,128)(2,1)S(1)}, u32[]{:S(2)}, u32[]{:S(2)}) collective-permute-start(bf16[128,1024]{1,0:T(8,128)(2,1)S(1)} %copy-done.3), channel_id=1, source_target_pairs={{0,8},{4,12},{8,0},{12,4},{1,9},{5,13},{9,1},{13,5},{2,10},{6,14},... | collective-permute-start | bytes 786440 | tf_op jit(solution)/shard_map/ppermute | solution.py:400
  33.9 5.7 %forward.5 = (bf16[8,1024,512]{2,1,0:T(8,128)(2,1)S(1)}, f32[8,512]{1,0:T(8,128)S(1)}, f32[2,8,512]{2,1,0:T(8,128)S(1)}, f32[8,64,512]{2,1,0:T(8,128)S(1)}) custom-call(bf16[8,64,512]{2,1,0:T(8,128)(2,1)S(1)} %turn.2.refs_0_, bf16[2,1024,128]{2,1,0:T(8,128)(2,1)S(1)} %collective-permute-done.1.refs_1_.refs_2_, f32[2,8,512]{2,1,0:T(8,128)S(1)} %get-tuple-element.34.refs_2_, ...), custom_call_target="tpu_custom_call" | custom-call | flops 4294967296 | bytes 8388608 | tf_op jit(solution)/shard_map/forward/pallas_call | solution.py:181
  39.7 5.7 %forward.6 = (bf16[8,1024,512]{2,1,0:T(8,128)(2,1)S(1)}, f32[8,512]{1,0:T(8,128)S(1)}, f32[2,8,512]{2,1,0:T(8,128)S(1)}, f32[8,64,512]{2,1,0:T(8,128)S(1)}) custom-call(bf16[8,64,512]{2,1,0:T(8,128)(2,1)S(1)} %turn.2.refs_0_, bf16[2,1024,128]{2,1,0:T(8,128)(2,1)S(1)} %collective-permute-done.3.refs_1_.refs_2_, f32[2,8,512]{2,1,0:T(8,128)S(1)} %get-tuple-element.36.refs_2_, ...), custom_call_target="tpu_custom_call" | custom-call | flops 4294967296 | bytes 8388608 | tf_op jit(solution)/shard_map/forward/pallas_call | solution.py:181
  45.7 6.1 %forward.7 = (bf16[8,1024,512]{2,1,0:T(8,128)(2,1)S(1)}, f32[8,512]{1,0:T(8,128)S(1)}, f32[3,8,512]{2,1,0:T(8,128)S(1)}, f32[8,64,512]{2,1,0:T(8,128)S(1)}) custom-call(bf16[8,64,512]{2,1,0:T(8,128)(2,1)S(1)} %turn.2.refs_0_, bf16[8,64,512]{2,1,0:T(8,128)(2,1)S(1)} %turn.3.refs_1_, bf16[2,512,128]{2,1,0:T(8,128)(2,1)S(1)} %collective-permute-done.4.refs_2_, ...), custom_call_target="tpu_custom_call" | custom-call | flops 4294967296 | bytes 8388608 | tf_op jit(solution)/shard_map/forward/pallas_call | solution.py:181
  51.9 5.3 %collective-permute-done.6.refs_7_.refs_6_ = f32[3,8,512]{2,1,0:T(8,128)S(1)} collective-permute-done((f32[3,8,512]{2,1,0:T(8,128)S(1)}, f32[3,8,512]{2,1,0:T(8,128)S(1)}, u32[]{:S(2)}, u32[]{:S(2)}) %collective-permute-start.6) | collective-permute-done | bytes 49184 | tf_op jit(solution)/shard_map/ppermute | solution.py:400
  57.1 9.1 %backward.5 = (bf16[128,1024]{1,0:T(8,128)(2,1)S(1)}, bf16[128,1024]{1,0:T(8,128)(2,1)S(1)}, f32[8,64,512]{2,1,0:T(8,128)S(1)}, bf16[1024,256]{1,0:T(8,128)(2,1)S(1)}) custom-call(bf16[8,64,512]{2,1,0:T(8,128)(2,1)S(1)} %turn.2.refs_0_, bf16[8,64,512]{2,1,0:T(8,128)(2,1)S(1)} %turn.3.refs_1_, bf16[2,512,128]{2,1,0:T(8,128)(2,1)S(1)} %collective-permute-done.4.refs_2_, ...), custom_call_target="tpu_custom_call" | custom-call | flops 6442450944 | bytes 8388608 | tf_op jit(solution)/shard_map/backward/pallas_call | solution.py:361
  66.3 8.3 %backward.6 = (f32[8,64,512]{2,1,0:T(8,128)S(1)}, bf16[1024,256]{1,0:T(8,128)(2,1)S(1)}) custom-call(bf16[8,64,512]{2,1,0:T(8,128)(2,1)S(1)} %turn.2.refs_0_, bf16[8,64,512]{2,1,0:T(8,128)(2,1)S(1)} %turn.3.refs_1_, bf16[2,1024,128]{2,1,0:T(8,128)(2,1)S(1)} %collective-permute-done.3.refs_1_.refs_2_, bf16[8,1024,512]{2,1,0:T(8,128)(2,1)S(1)} %get-tuple-element.50.refs_3_, ...), custom_call_target="tpu_custom_call" | custom-call | flops 6442450944 | bytes 8388608 | tf_op jit(solution)/shard_map/backward/pallas_call | solution.py:361
  74.6 8.5 %backward.7 = (f32[8,64,512]{2,1,0:T(8,128)S(1)}, bf16[1024,256]{1,0:T(8,128)(2,1)S(1)}) custom-call(bf16[8,64,512]{2,1,0:T(8,128)(2,1)S(1)} %turn.2.refs_0_, bf16[8,64,512]{2,1,0:T(8,128)(2,1)S(1)} %turn.3.refs_1_, bf16[2,1024,128]{2,1,0:T(8,128)(2,1)S(1)} %collective-permute-done.1.refs_1_.refs_2_, bf16[8,1024,512]{2,1,0:T(8,128)(2,1)S(1)} %get-tuple-element.48.refs_3_, ...), custom_call_target="tpu_custom_call" | custom-call | flops 6442450944 | bytes 8388608 | tf_op jit(solution)/shard_map/backward/pallas_call | solution.py:361
  83.6 2.7 %collective-permute-start.10 = (bf16[1024,256]{1,0:T(8,128)(2,1)S(1)}, bf16[1024,256]{1,0:T(8,128)(2,1)S(1)}, u32[]{:S(2)}, u32[]{:S(2)}) collective-permute-start(bf16[1024,256]{1,0:T(8,128)(2,1)S(1)} %get-tuple-element.60), channel_id=1, source_target_pairs={{0,4},{4,0},{8,12},{12,8},{16,20},{20,16},{24,28},{28,24},{1,5},{5... | collective-permute-start | bytes 1572872 | tf_op jit(solution)/shard_map/ppermute | solution.py:408
  86.3 0.9 collective-permute-start.9
  87.3 3.9 %backward.8 = (bf16[128,1024]{1,0:T(8,128)(2,1)S(1)}, f32[2,64,1024]{2,1,0:T(8,128)S(1)}, f32[2,64,1024]{2,1,0:T(8,128)S(1)}) custom-call(bf16[8,64,512]{2,1,0:T(8,128)(2,1)S(1)} %turn.2.refs_0_, bf16[8,64,512]{2,1,0:T(8,128)(2,1)S(1)} %turn.3.refs_1_, bf16[2,1024,128]{2,1,0:T(8,128)(2,1)S(1)} %copy-done.1, ...), custom_call_target="tpu_custom_call" | custom-call | flops 3221225472 | bytes 4194304 | tf_op jit(solution)/shard_map/backward/pallas_call | solution.py:361
  91.2 2.3 %collective-permute-start.8 = (bf16[128,1024]{1,0:T(8,128)(2,1)S(1)}, bf16[128,1024]{1,0:T(8,128)(2,1)S(1)}, u32[]{:S(2)}, u32[]{:S(2)}) collective-permute-start(bf16[128,1024]{1,0:T(8,128)(2,1)S(1)} %get-tuple-element.58), channel_id=1, source_target_pairs={{0,8},{4,12},{8,0},{12,4},{1,9},{5,13},{9,1},{13,5},{2,10},{6,14},... | collective-permute-start | bytes 786440 | tf_op jit(solution)/shard_map/ppermute | solution.py:400
  93.5 4.1 %backward.9 = (bf16[128,1024]{1,0:T(8,128)(2,1)S(1)}, bf16[1024,256]{1,0:T(8,128)(2,1)S(1)}) custom-call(bf16[8,64,512]{2,1,0:T(8,128)(2,1)S(1)} %turn.2.refs_0_, bf16[8,64,512]{2,1,0:T(8,128)(2,1)S(1)} %turn.3.refs_1_, bf16[2,1024,128]{2,1,0:T(8,128)(2,1)S(1)} %copy-done.1, bf16[8,1024,512]{2,1,0:T(8,128)(2,1)S(1)} %get-tuple-element.46.refs_3_, ...), custom_call_target="tpu_custom_call" | custom-call | flops 3221225472 | bytes 4194304 | tf_op jit(solution)/shard_map/backward/pallas_call | solution.py:361
  98.4 13.4 %collective-permute-done.8 = bf16[128,1024]{1,0:T(8,128)(2,1)S(1)} collective-permute-done((bf16[128,1024]{1,0:T(8,128)(2,1)S(1)}, bf16[128,1024]{1,0:T(8,128)(2,1)S(1)}, u32[]{:S(2)}, u32[]{:S(2)}) %collective-permute-start.8) | collective-permute-done | bytes 262176 | tf_op jit(solution)/shard_map/ppermute | solution.py:400
  113.4 1.1 add_convert_fusion
  (25 shorter events, 3.8 us)
Async XLA Ops:
  0.6 16.4 %copy-start.2 = (bf16[128,1024]{1,0:T(8,128)(2,1)S(1)}, bf16[128,1024]{1,0:T(8,128)(2,1)}, u32[]{:S(2)}) copy-start(bf16[128,1024]{1,0:T(8,128)(2,1)} %refs_0_.2) | copy-start | bytes 786436
  0.6 16.4 %collective-permute-start = (bf16[128,1024]{1,0:T(8,128)(2,1)}, bf16[128,1024]{1,0:T(8,128)(2,1)S(1)}, u32[]{:S(2)}, u32[]{:S(2)}) collective-permute-start(bf16[128,1024]{1,0:T(8,128)(2,1)} %refs_0_.2), channel_id=1, source_target_pairs={{0,8},{4,12},{8,0},{12,4},{1,9},{5,13},{9,1},{13,5},{2,10},{6,14},... | collective-permute-start | bytes 786440 | tf_op jit(solution)/shard_map/ppermute | solution.py:400
  12.6 15.5 %collective-permute-start.3 = (bf16[2,1024,128]{2,1,0:T(8,128)(2,1)}, bf16[2,1024,128]{2,1,0:T(8,128)(2,1)S(1)}, u32[]{:S(2)}, u32[]{:S(2)}) collective-permute-start(bf16[2,1024,128]{2,1,0:T(8,128)(2,1)} %project.1.refs_1_.refs_2_), channel_id=1, source_target_pairs={{0,4},{4,0},{8,12},{12,8},{16,20},{20,16},{24,28},{28,24},{1,5},{5... | collective-permute-start | bytes 1572872 | tf_op jit(solution)/shard_map/ppermute | solution.py:408
  14.2 15.6 %collective-permute-start.1 = (bf16[2,1024,128]{2,1,0:T(8,128)(2,1)}, bf16[2,1024,128]{2,1,0:T(8,128)(2,1)S(1)}, u32[]{:S(2)}, u32[]{:S(2)}) collective-permute-start(bf16[2,1024,128]{2,1,0:T(8,128)(2,1)} %project.1.refs_1_.refs_2_), channel_id=1, source_target_pairs={{0,16},{4,20},{8,24},{12,28},{16,0},{20,4},{24,8},{28,12},{1,17},{... | collective-permute-start | bytes 1572872 | tf_op jit(solution)/shard_map/ppermute | solution.py:408
  17.2 1.0 copy-start
  18.2 11.6 %copy-start.3 = (bf16[128,1024]{1,0:T(8,128)(2,1)S(1)}, bf16[128,1024]{1,0:T(8,128)(2,1)}, u32[]{:S(2)}) copy-start(bf16[128,1024]{1,0:T(8,128)(2,1)} %refs_0_.3) | copy-start | bytes 786436
  28.2 17.5 %collective-permute-start.4 = (bf16[2,512,128]{2,1,0:T(8,128)(2,1)S(1)}, bf16[2,512,128]{2,1,0:T(8,128)(2,1)S(1)}, u32[]{:S(2)}, u32[]{:S(2)}) collective-permute-start(bf16[2,512,128]{2,1,0:T(8,128)(2,1)S(1)} %slice.8), channel_id=1, source_target_pairs={{0,16},{4,20},{8,24},{12,28},{16,0},{20,4},{24,8},{28,12},{1,17},{... | collective-permute-start | bytes 786440 | tf_op jit(solution)/shard_map/ppermute | solution.py:408
  29.8 15.9 %collective-permute-start.5 = (bf16[2,512,128]{2,1,0:T(8,128)(2,1)S(1)}, bf16[2,512,128]{2,1,0:T(8,128)(2,1)S(1)}, u32[]{:S(2)}, u32[]{:S(2)}) collective-permute-start(bf16[2,512,128]{2,1,0:T(8,128)(2,1)S(1)} %slice.9), channel_id=1, source_target_pairs={{0,4},{4,0},{8,12},{12,8},{16,20},{20,16},{24,28},{28,24},{1,5},{5... | collective-permute-start | bytes 786440 | tf_op jit(solution)/shard_map/ppermute | solution.py:408
  29.9 15.6 %collective-permute-start.2 = (bf16[128,1024]{1,0:T(8,128)(2,1)S(1)}, bf16[128,1024]{1,0:T(8,128)(2,1)S(1)}, u32[]{:S(2)}, u32[]{:S(2)}) collective-permute-start(bf16[128,1024]{1,0:T(8,128)(2,1)S(1)} %copy-done.3), channel_id=1, source_target_pairs={{0,8},{4,12},{8,0},{12,4},{1,9},{5,13},{9,1},{13,5},{2,10},{6,14},... | collective-permute-start | bytes 786440 | tf_op jit(solution)/shard_map/ppermute | solution.py:400
  51.8 5.4 %collective-permute-start.6 = (f32[3,8,512]{2,1,0:T(8,128)S(1)}, f32[3,8,512]{2,1,0:T(8,128)S(1)}, u32[]{:S(2)}, u32[]{:S(2)}) collective-permute-start(f32[3,8,512]{2,1,0:T(8,128)S(1)} %get-tuple-element.42.refs_6_.refs_5_), channel_id=1, source_target_pairs={{0,8},{4,12},{8,0},{12,4},{1,9},{5,13},{9,1},{13,5},{2,10},{6,14},... | collective-permute-start | bytes 147464 | tf_op jit(solution)/shard_map/ppermute | solution.py:400
  66.2 31.4 %collective-permute-start.7 = (bf16[128,1024]{1,0:T(8,128)(2,1)S(1)}, bf16[128,1024]{1,0:T(8,128)(2,1)S(1)}, u32[]{:S(2)}, u32[]{:S(2)}) collective-permute-start(bf16[128,1024]{1,0:T(8,128)(2,1)S(1)} %get-tuple-element.45), channel_id=1, source_target_pairs={{0,8},{4,12},{8,0},{12,4},{1,9},{5,13},{9,1},{13,5},{2,10},{6,14},... | collective-permute-start | bytes 786440 | tf_op jit(solution)/shard_map/ppermute | solution.py:400
  74.5 12.7 %copy-start.1 = (bf16[2,1024,128]{2,1,0:T(8,128)(2,1)S(1)}, bf16[2,1024,128]{2,1,0:T(8,128)(2,1)}, u32[]{:S(2)}) copy-start(bf16[2,1024,128]{2,1,0:T(8,128)(2,1)} %project.1.refs_1_.refs_2_) | copy-start | bytes 1572868
  83.0 29.5 %collective-permute-start.11 = (bf16[1024,256]{1,0:T(8,128)(2,1)S(1)}, bf16[1024,256]{1,0:T(8,128)(2,1)S(1)}, u32[]{:S(2)}, u32[]{:S(2)}) collective-permute-start(bf16[1024,256]{1,0:T(8,128)(2,1)S(1)} %get-tuple-element.61), channel_id=1, source_target_pairs={{0,16},{4,20},{8,24},{12,28},{16,0},{20,4},{24,8},{28,12},{1,17},{... | collective-permute-start | bytes 1572872 | tf_op jit(solution)/shard_map/ppermute | solution.py:408
  83.6 28.9 %collective-permute-start.10 = (bf16[1024,256]{1,0:T(8,128)(2,1)S(1)}, bf16[1024,256]{1,0:T(8,128)(2,1)S(1)}, u32[]{:S(2)}, u32[]{:S(2)}) collective-permute-start(bf16[1024,256]{1,0:T(8,128)(2,1)S(1)} %get-tuple-element.60), channel_id=1, source_target_pairs={{0,4},{4,0},{8,12},{12,8},{16,20},{20,16},{24,28},{28,24},{1,5},{5... | collective-permute-start | bytes 1572872 | tf_op jit(solution)/shard_map/ppermute | solution.py:408
  86.3 27.1 %collective-permute-start.9 = (bf16[1024,256]{1,0:T(8,128)(2,1)S(1)}, bf16[1024,256]{1,0:T(8,128)(2,1)S(1)}, u32[]{:S(2)}, u32[]{:S(2)}) collective-permute-start(bf16[1024,256]{1,0:T(8,128)(2,1)S(1)} %get-tuple-element.59), channel_id=1, source_target_pairs={{0,20},{4,16},{8,28},{12,24},{16,4},{20,0},{24,12},{28,8},{1,21},{... | collective-permute-start | bytes 1572872 | tf_op jit(solution)/shard_map/ppermute | solution.py:408
  91.2 20.6 %collective-permute-start.8 = (bf16[128,1024]{1,0:T(8,128)(2,1)S(1)}, bf16[128,1024]{1,0:T(8,128)(2,1)S(1)}, u32[]{:S(2)}, u32[]{:S(2)}) collective-permute-start(bf16[128,1024]{1,0:T(8,128)(2,1)S(1)} %get-tuple-element.58), channel_id=1, source_target_pairs={{0,8},{4,12},{8,0},{12,4},{1,9},{5,13},{9,1},{13,5},{2,10},{6,14},... | collective-permute-start | bytes 786440 | tf_op jit(solution)/shard_map/ppermute | solution.py:400
